TPU v7x, 512 devices: a whole 4x8x8 slice. The times are simulated.
512 devices in a mesh: dp: 4 (over x), ctx: 16 (over y, core), tensor: 8 (over z).
Axes of the slice: x: 4, y: 8, z: 8, core: 2. Of those that a mesh axis runs over, the one named last changes fastest.
Arguments:
- tokens: bfloat16 [8192, 8192], P(('dp', 'tensor'), 'ctx'), parts along dimension 0, may hold values from -6 to 6
- queries: bfloat16 [8192, 8192], P(('dp', 'ctx'), 'tensor'), parts along dimension 0, may hold values from -100 to 100
- key_value_weight: bfloat16 [8192, 2048], P('ctx', 'tensor'), may hold values from -0.0625 to 0.0625
- out_weight: bfloat16 [8192, 8192], P('tensor', 'ctx'), may hold values from -0.0625 to 0.0625
- doc_lengths: int32 [32], P('dp'), parts along dimension 0, may hold values from 1 to 1024, 2048 in all
- block_order: int32 [128], P('dp'), parts along dimension 0, may hold values from 0 to 31, each once
Outputs:
- mixed: bfloat16 [8192, 8192], P(('dp', 'tensor'), 'ctx'), parts along dimension 0
There are 4 independent parts, one for each index of `dp`. A program takes and returns all parts, laid end to end along the dimension named above; an argument that names none is the same for every part. Nothing has to cross between parts.
Inputs may be any that keep to these rules, and one draw needn't show every extreme that they name: `doc_lengths`: the lengths add up to 2048. `block_order`: each of 0 to 31 once.
All inputs are finite; a program needn't handle non-finite values.
Results may differ from a plain program's by a relative error of at most 0.014.
Values may be sent and summed in bfloat16 or wider, within the bound.
No kernel may reach another device: no remote copies, remote signals or barrier semaphores. Data moves between devices by JAX's collectives and lax.ppermute only.
A program may use at most 64 MiB of HBM per device.

v0:
```python
import math

import jax
import jax.numpy as jnp
from jax import lax
from jax.sharding import PartitionSpec as P

HEAD_WIDTH = 128


def doc_index(positions, doc_ends):
    return jnp.sum((doc_ends[None, :] <= positions[:, None]).astype(jnp.int32), axis=1)


def make_attend(query_groups, query_pos, query_doc, doc_ends):
    scale = 1.0 / jnp.sqrt(jnp.float32(HEAD_WIDTH))

    def attend(running, kv_piece, first_row):
        key_count = kv_piece.shape[0]
        key_pos = first_row + jnp.arange(key_count, dtype=jnp.int32)
        key_doc = doc_index(key_pos, doc_ends)
        allowed = (query_doc[:, None] == key_doc[None, :]) & (
            key_pos[None, :] <= query_pos[:, None]
        )

        def update(state_in):
            top_score, total, weighted = state_in
            split_kv = kv_piece.reshape(key_count, query_groups.shape[1], 2, HEAD_WIDTH)
            keys_now = split_kv[:, :, 0, :]
            values_now = split_kv[:, :, 1, :]
            scores = (
                jnp.einsum(
                    "tkgd,nkd->tkgn", query_groups, keys_now, preferred_element_type=jnp.float32
                )
                * scale
            )
            visible = allowed[:, None, None, :]
            piece_top = jnp.max(jnp.where(visible, scores, jnp.float32(-1e30)), axis=-1)
            new_top = jnp.maximum(top_score, piece_top)
            probs = jnp.where(visible, jnp.exp(scores - new_top[..., None]), jnp.float32(0.0))
            rescale = jnp.exp(top_score - new_top)
            total = total * rescale + jnp.sum(probs, axis=-1)
            weighted = weighted * rescale[..., None] + jnp.einsum(
                "tkgn,nkd->tkgd",
                probs.astype(jnp.bfloat16),
                values_now,
                preferred_element_type=jnp.float32,
            )
            return (new_top, total, weighted)

        def unchanged(state_in):
            return state_in

        return lax.cond(jnp.any(allowed), update, unchanged, running)

    return attend


def local(tokens, queries, key_value_weight, out_weight, doc_lengths, block_order):
    ctx_count = lax.axis_size("ctx")
    ctx_rank = lax.axis_index("ctx")
    local_rows = queries.shape[0]
    seq_rows = local_rows * ctx_count
    half_rows = local_rows // 2
    doc_ends = jnp.cumsum(doc_lengths)
    own_blocks = lax.dynamic_slice_in_dim(block_order, 2 * ctx_rank, 2)
    query_pos = jnp.repeat(
        own_blocks, half_rows, total_repeat_length=local_rows
    ) * half_rows + jnp.tile(jnp.arange(half_rows, dtype=jnp.int32), 2)
    query_doc = doc_index(query_pos, doc_ends)
    heads_width = queries.shape[1]
    kv_heads = key_value_weight.shape[1] // (2 * HEAD_WIDTH)
    queries_per_group = heads_width // HEAD_WIDTH // kv_heads
    query_groups = queries.reshape(local_rows, kv_heads, queries_per_group, HEAD_WIDTH)
    attend = make_attend(query_groups, query_pos, query_doc, doc_ends)
    initial = (
        jnp.full((local_rows, kv_heads, queries_per_group), -1e30, jnp.float32),
        jnp.zeros((local_rows, kv_heads, queries_per_group), jnp.float32),
        jnp.zeros((local_rows, kv_heads, queries_per_group, HEAD_WIDTH), jnp.float32),
    )
    partial_kv = jnp.dot(
        lax.all_gather(tokens, "tensor", axis=0, tiled=True),
        key_value_weight,
        preferred_element_type=jnp.float32,
    )
    whole_kv = lax.psum(partial_kv, "ctx").astype(jnp.bfloat16)
    key_step = math.gcd(seq_rows, 512)

    def visit(key_block, running):
        kv_piece = lax.dynamic_slice_in_dim(whole_kv, key_block * key_step, key_step, 0)
        return attend(running, kv_piece, key_block * key_step)

    result = lax.fori_loop(0, seq_rows // key_step, visit, initial)
    top_score, total, weighted = result
    attn = (weighted / total[..., None]).astype(jnp.bfloat16).reshape(local_rows, heads_width)
    partial_out = jnp.dot(
        lax.all_gather(attn, "ctx", axis=0, tiled=True),
        out_weight,
        preferred_element_type=jnp.float32,
    )
    mixed = lax.psum_scatter(
        partial_out.astype(jnp.bfloat16), "tensor", scatter_dimension=0, tiled=True
    )
    return mixed


def solution(mesh):
    in_specs = (
        P(("dp", "tensor"), "ctx"),
        P(("dp", "ctx"), "tensor"),
        P("ctx", "tensor"),
        P("tensor", "ctx"),
        P("dp"),
        P("dp"),
    )
    out_specs = P(("dp", "tensor"), "ctx")
    return jax.shard_map(local, mesh=mesh, in_specs=in_specs, out_specs=out_specs, check_vma=False)
```

profile of v0, /device:TPU:14, one launch (start us, length us, event | category | flops | bytes accessed | tf_op | source)
XLA Modules:
  0.0 247.5 jit_solution(3208315371400769322)
XLA Ops:
  6.5 0.7 all-gather.3.cloned.1.call-update
  7.3 0.8 reduce-window.10
  8.2 1.1 copy.16
  9.6 0.7 dynamic_slice.14
  10.3 0.6 fusion.21
  10.9 1.9 fusion.19
  12.8 45.1 %all-gather.3.cloned.1.call-done = bf16[2048,512]{1,0:T(8,128)(2,1)} async-done(((bf16[256,512]{1,0:T(8,128)(2,1)}), bf16[2048,512]{1,0:T(8,128)(2,1)}) %all-gather.3.cloned.1.call-update) | async-done | bytes 2097168 | tf_op jit(solution)/shard_map/all_gather | solution.py:82
  57.9 2.3 fusion.22
  60.2 55.5 %all-reduce.1 = bf16[2048,256]{1,0:T(8,128)(2,1)} all-reduce(f32[2048,256]{1,0:T(8,128)S(1)} %fusion.22), channel_id=1, replica_groups=mesh['dp'=4,'ctx'=16,'tensor'=8] {'ctx'}, use_global_device_ids=true, to_apply=%region_0.0 | all-reduce | flops 524288 | bytes 3145728 | tf_op jit(solution)/shard_map/psum | solution.py:86
  115.7 1.5 copy.17
  117.3 16.8 %while.19 = (s32[]{:T(128)}, f32[128,1,8]{0,2,1:T(8,128)S(1)}, f32[128,1,8]{0,2,1:T(8,128)S(1)}, f32[128,1,8,128]{0,3,2,1:T(8,128)S(1)}, s32[128]{0:T(128)S(1)},...) while((s32[]{:T(128)}, f32[128,1,8]{0,2,1:T(8,128)S(1)}, ...), condition=%wide.region_10.11_spmd.clone, body=%wide.region_3.10_spmd.clone.sunk | while | flops 274742656 | bytes 8730577 | solution.py:93
  117.4 1.2 multiply_add_fusion.2
  118.7 0.9 fusion.28
  120.2 1.7 conditional.3
  120.3 0.5 fusion.2
  121.2 0.6 fusion.7
  122.0 1.2 multiply_add_fusion.2
  123.4 0.9 fusion.28
  124.9 1.7 conditional.3
  124.9 0.5 fusion.2
  125.9 0.6 fusion.7
  126.7 1.2 multiply_add_fusion.2
  128.0 0.9 fusion.28
  129.6 1.2 multiply_add_fusion.2
  131.0 0.9 fusion.28
  132.5 1.7 conditional.3
  132.5 0.5 fusion.2
  133.5 0.6 fusion.7
  134.2 0.8 divide_convert_fusion
  135.0 54.3 %all-gather.5.cloned.1.call-done = bf16[2048,1024]{0,1:T(8,128)(2,1)} async-done(((bf16[128,1024]{0,1:T(8,128)(2,1)}), bf16[2048,1024]{0,1:T(8,128)(2,1)}) %all-gather.5.cloned.1.call-update) | async-done | bytes 4194320 | tf_op jit(solution)/shard_map/all_gather | solution.py:97
  189.2 5.9 %convolution_convert_fusion = bf16[2048,512]{1,0:T(8,128)(2,1)} fusion(bf16[2048,1024]{0,1:T(8,128)(2,1)} %all-gather.5.cloned.1.call-done, bf16[1024,512]{1,0:T(8,128)(2,1)S(1)} %copy-done), kind=kOutput, calls=%fused_computation.30 | convolution fusion | flops 2148532224 | bytes 7340032 | tf_op jit(solution)/shard_map/dot_general | solution.py:96
  195.2 45.8 %reduce-scatter.2.cloned.1.call-done = bf16[256,512]{1,0:T(8,128)(2,1)} async-done(((bf16[2048,512]{1,0:T(8,128)(2,1)}), bf16[256,512]{1,0:T(8,128)(2,1)}) %reduce-scatter.2.cloned.1.call-update) | async-done | bytes 262160 | tf_op jit(solution)/shard_map/reduce_scatter | solution.py:101
  (48 shorter events, 2.7 us)
Async XLA Ops:
  6.5 182.7 %copy-start = (bf16[1024,512]{1,0:T(8,128)(2,1)S(1)}, bf16[1024,512]{1,0:T(8,128)(2,1)}, u32[]{:S(2)}) copy-start(bf16[1024,512]{1,0:T(8,128)(2,1)} %param.15) | copy-start | bytes 3145732
  6.5 51.4 %all-gather.3.cloned.1.call-start = ((), (), s32[]{:S(2)}) async-start(), calls=%async_computation.1 | async-start | bytes 2359296 | tf_op jit(solution)/shard_map/all_gather | solution.py:82
  7.3 182.0 %all-gather.5.cloned.1.call-start = ((), (), s32[]{:S(2)}) async-start(), calls=%async_computation.2 | async-start | bytes 4456448 | tf_op jit(solution)/shard_map/all_gather | solution.py:97
  115.7 1.6 copy-start.1
  134.9 106.1 %reduce-scatter.2.cloned.1.call-start = ((), (), s32[]{:S(2)}) async-start(), calls=%async_computation.3 | async-start | bytes 2359296 | tf_op jit(solution)/shard_map/reduce_scatter | solution.py:101
Sparse Core Ops, SparseCore 0:
  9.4 48.4 all-gather.2
  135.1 54.1 all-gather.4
  195.3 45.6 reduce-scatter.1
where the time goes:
time: 247 us; the launch traced here: 248 us
  waiting for transfers between devices  146 us (59%)
  blocking collectives  55.5 us (22%)
  other arithmetic  13.6 us (6%)
  between operations  13.2 us (5%)
  matrix products  11.6 us (5%)
  local copies, waits for them, and re-layouts  4.69 us (2%)
  loops' own time  2.97 us (1%)
    psum x1, blocking collectives, local(): whole_kv = lax.psum(partial_kv, 'ctx').astype(jnp.bfloat16)  55.5 us
    all_gather x1, waiting for transfers between devices, local(): lax.all_gather(attn, 'ctx', axis=0, tiled=True)  54.3 us
    reduce_scatter x1, waiting for transfers between devices, local(): lax.psum_scatter(partial_out.astype(jnp.bfloat16), 'tensor', scatter_dime...  45.8 us
    all_gather x1, waiting for transfers between devices, local(): lax.all_gather(tokens, 'tensor', axis=0, tiled=True)  45.1 us
    add x5, other arithmetic, local(): jnp.repeat(own_blocks, half_rows, total_repeat_length=local_rows)  6.79 us
    dot_general x1, matrix products, local(): jnp.dot(lax.all_gather(attn, 'ctx', axis=0, tiled=True), out_weight, pref...  5.9 us
  transfers between devices with their start and end apart: 3, of which 3 were waited for; matrix products, arithmetic and copies ran while one was open for 2% of the time, Pallas kernels for 0%

commit v1 on v0

v1 whole, which is shorter than its diff:
```python
import functools
import math

import jax
import jax.numpy as jnp
from jax import lax
from jax.experimental import pallas as pl
from jax.experimental.pallas import tpu as pltpu
from jax.sharding import Mesh, PartitionSpec as P

HEAD = 128
RING = 8
BLOCK = 64
KEYS = 256
NEG = -1e30
EXP_SCALE = math.log2(math.e) / math.sqrt(HEAD)


def attend_kernel(base, gap, ids, lengths, order, q_ref, kv_ref, out_ref, acc_ref, top_ref):
    step = pl.program_id(0)
    unit = step // 2
    z, core = ids[0], ids[2]
    owner = (z + base + unit + gap * (unit // 2)) % RING
    first = order[(owner * 2 + core) * 2 + step % 2] * BLOCK
    heads = q_ref.shape[1] // HEAD
    rows = BLOCK * heads

    row_pos = first + lax.broadcasted_iota(jnp.int32, (BLOCK, KEYS), 0)
    row_start = jnp.zeros((BLOCK, KEYS), jnp.int32)
    lowest = jnp.int32(0)
    end = jnp.int32(0)
    for j in range(lengths.shape[0]):
        end = end + lengths[j]
        row_start = jnp.where(row_pos >= end, end, row_start)
        lowest = jnp.where(first >= end, end, lowest)
    columns = lax.broadcasted_iota(jnp.int32, (BLOCK, KEYS), 1)

    query = jnp.concatenate(
        [q_ref[:, h * HEAD : (h + 1) * HEAD] for h in range(heads)], axis=0
    )
    ones = jnp.ones((KEYS, HEAD), jnp.bfloat16)
    acc_ref[...] = jnp.zeros_like(acc_ref)
    top_ref[...] = jnp.full_like(top_ref, NEG)
    last = first // KEYS

    @pl.loop(0, last - lowest // KEYS + 1)
    def _(i):
        block = last - i
        offset = pl.multiple_of(((block - z + RING) % RING) * KEYS, KEYS)
        keys = kv_ref[pl.ds(offset, KEYS), :HEAD]
        values = kv_ref[pl.ds(offset, KEYS), HEAD:]
        scores = lax.dot_general(
            query, keys, (((1,), (1,)), ((), ())), preferred_element_type=jnp.float32
        )
        key_pos = block * KEYS + columns
        allowed = (key_pos >= row_start) & (key_pos <= row_pos)
        scores = jnp.where(
            allowed[None], scores.reshape(heads, BLOCK, KEYS), jnp.float32(NEG)
        ).reshape(rows, KEYS)
        old = top_ref[...]
        new = jnp.maximum(old, jnp.max(scores, axis=1, keepdims=True))
        top_ref[...] = new
        keep = jnp.exp2((old - new) * EXP_SCALE)
        probs = jnp.exp2((scores - new[:, :1]) * EXP_SCALE).astype(jnp.bfloat16)
        both = jnp.concatenate([values, ones], axis=1)
        acc_ref[...] = acc_ref[...] * keep[:, :1] + jnp.dot(
            probs, both, preferred_element_type=jnp.float32
        )

    for h in range(heads):
        part = acc_ref[h * BLOCK : (h + 1) * BLOCK, :]
        out_ref[:, h * HEAD : (h + 1) * HEAD] = (part[:, :HEAD] / part[:, HEAD:]).astype(
            out_ref.dtype
        )


def attend(base, gap, units, ids, lengths, order, queries, kv):
    width = queries.shape[1]
    heads = width // HEAD

    def q_map(i, ids, lengths, order):
        unit = i // 2
        block = (ids[0] + base + unit + gap * (unit // 2) - ids[1] + RING) % RING
        return (block * 2 + i % 2, 0)

    return pl.pallas_call(
        functools.partial(attend_kernel, base, gap),
        out_shape=jax.ShapeDtypeStruct((units * 2 * BLOCK, width), jnp.bfloat16),
        grid_spec=pltpu.PrefetchScalarGridSpec(
            num_scalar_prefetch=3,
            grid=(units * 2,),
            in_specs=[
                pl.BlockSpec((BLOCK, width), q_map),
                pl.BlockSpec(kv.shape, lambda i, *_: (0, 0)),
            ],
            out_specs=pl.BlockSpec((BLOCK, width), lambda i, *_: (i, 0)),
            scratch_shapes=[
                pltpu.VMEM((BLOCK * heads, 2 * HEAD), jnp.float32),
                pltpu.VMEM((BLOCK * heads, HEAD), jnp.float32),
            ],
        ),
        cost_estimate=pl.CostEstimate(
            flops=units * 600_000_000, bytes_accessed=units * 1_000_000, transcendentals=units * 500_000
        ),
        name="attend",
    )(ids, lengths, order, queries, kv)


def shift(x, axis, by):
    return lax.ppermute(x, axis, [(i, (i + by) % RING) for i in range(RING)])


def swap(x):
    return lax.ppermute(x, "core", [(0, 1), (1, 0)])


def gather_rounds(x, axis):
    half = x.shape[0] // 2
    up, down = shift(x, axis, -1), shift(x, axis, 1)
    yield (up, down)
    up2 = shift(jnp.concatenate([x, up], axis=0), axis, -2)
    down2 = shift(jnp.concatenate([down, x], axis=0), axis, 2)
    yield (up2, down2)
    rows = x.shape[0]
    far_top = shift(down2[:half], axis, 1)
    far_bottom = shift(up2[rows + half :], axis, -1)
    yield (far_top, far_bottom)


def local(tokens, queries, key_value_weight, out_weight, doc_lengths, block_order):
    z, y, core = lax.axis_index("z"), lax.axis_index("y"), lax.axis_index("core")
    ids = jnp.stack([z, y, core]).astype(jnp.int32)
    other_weight = swap(out_weight)

    def project(block):
        return jnp.dot(block, key_value_weight, preferred_element_type=jnp.float32)

    token_rounds, query_rounds = gather_rounds(tokens, "z"), gather_rounds(queries, "y")
    (t_up, t_down), (q_up, q_down) = next(token_rounds), next(query_rounds)
    (t_up2, t_down2), (q_up2, q_down2) = next(token_rounds), next(query_rounds)
    t_far, q_far = next(token_rounds), next(query_rounds)
    partial_kv = jnp.concatenate(
        [project(b) for b in (tokens, t_up, t_up2, *t_far, t_down2, t_down)], axis=0
    )
    all_queries = jnp.concatenate([queries, q_up, q_up2, *q_far, q_down2, q_down], axis=0)
    partial_kv, all_queries, other_weight = lax.optimization_barrier(
        (partial_kv, all_queries, other_weight)
    )
    kv = lax.psum(partial_kv, ("y", "core")).astype(jnp.bfloat16)

    def products(base, gap, units):
        attn = attend(base, gap, units, ids, doc_lengths, block_order, all_queries, kv)
        return tuple(
            jnp.dot(attn, w, preferred_element_type=jnp.float32) for w in (out_weight, other_weight)
        )

    rows = queries.shape[0]
    f32, bf16 = jnp.float32, jnp.bfloat16

    def both(parts, unit):
        return jnp.concatenate([p[unit * rows : (unit + 1) * rows] for p in parts], axis=1)

    far = products(4, 0, 1)
    far_up, far_down = shift(far[0].astype(bf16), "z", 1), shift(far[1].astype(bf16), "z", -1)
    middle = products(2, 1, 4)
    width = far_up.shape[1]
    zero = jnp.zeros((rows, width), f32)
    third = both(middle, 1) + jnp.concatenate([far_up.astype(f32), zero], axis=1)
    minus_third = both(middle, 2) + jnp.concatenate([zero, far_down.astype(f32)], axis=1)
    up2 = shift(jnp.concatenate([both(middle, 0), third], axis=0).astype(bf16), "z", 2)
    down2 = shift(jnp.concatenate([both(middle, 3), minus_third], axis=0).astype(bf16), "z", -2)
    near = products(7, 0, 3)
    up1 = shift((both(near, 2) + up2[rows:].astype(f32)).astype(bf16), "z", 1)
    down1 = shift((both(near, 0) + down2[rows:].astype(f32)).astype(bf16), "z", -1)
    total = (
        both(near, 1)
        + up2[:rows].astype(f32)
        + down2[:rows].astype(f32)
        + up1.astype(f32)
        + down1.astype(f32)
    ).astype(bf16)
    mine, theirs = total[:, :width], swap(total[:, width:])
    return jnp.where(
        core == 0,
        jnp.concatenate([mine, theirs], axis=0),
        jnp.concatenate([theirs, mine], axis=0),
    )


def solution(mesh):
    fine = Mesh(mesh.devices.reshape(4, 8, 2, 8), ("dp", "y", "core", "z"))
    ctx = ("y", "core")
    in_specs = (
        P(("dp", "z"), ctx),
        P(("dp", "y", "core"), "z"),
        P(ctx, "z"),
        P("z", ctx),
        P("dp"),
        P("dp"),
    )
    return jax.shard_map(
        local, mesh=fine, in_specs=in_specs, out_specs=P(("dp", "z"), ctx), check_vma=False
    )
```

time: 247 us -> 240 us (0.972)
  the two profiles are of different devices: /device:TPU:14 before, /device:TPU:3 now
where the time goes in v1:
time: 240 us; the launch traced here: 237 us
  starting transfers between devices  75.2 us (31%)
  blocking collectives  57.8 us (24%)
  Pallas kernels  44.9 us (19%)
  waiting for transfers between devices  43.7 us (18%)
  matrix products  11.1 us (5%)
  other arithmetic  2.99 us (1%)
    ppermute x18, starting transfers between devices, shift(): return lax.ppermute(x, axis, [(i, (i + by) % RING) for i in range(RING)])  68 us
    psum x1, blocking collectives, local(): kv = lax.psum(partial_kv, ('y', 'core')).astype(jnp.bfloat16)  57.8 us
    pallas_call x3, Pallas kernels, attend(): pl.pallas_call(functools.partial(attend_kernel, base, gap), out_shape=jax...  44.9 us
    ppermute x18, waiting for transfers between devices, shift(): return lax.ppermute(x, axis, [(i, (i + by) % RING) for i in range(RING)])  42.7 us
    dot_general x7, matrix products, project(): return jnp.dot(block, key_value_weight, preferred_element_type=jnp.float32)  7.92 us
    ppermute x2, starting transfers between devices, swap(): return lax.ppermute(x, 'core', [(0, 1), (1, 0)])  7.14 us
  transfers between devices with their start and end apart: 20, of which 8 were waited for; matrix products, arithmetic and copies ran while one was open for 5% of the time, Pallas kernels for 0%

profile of v1, /device:TPU:3, one launch (start us, length us, event | category | flops | bytes accessed | tf_op | source)
XLA Modules:
  0.0 237.3 jit_solution(5750479644430919076)
XLA Ops:
  0.0 3.3 %collective-permute-start.8 = (bf16[128,1024]{1,0:T(8,128)(2,1)}, bf16[128,1024]{1,0:T(8,128)(2,1)S(1)}, u32[]{:S(2)}, u32[]{:S(2)}) collective-permute-start(bf16[128,1024]{1,0:T(8,128)(2,1)} %param.7), channel_id=1, source_target_pairs={{0,16},{16,32},{32,48},{48,64},{64,80},{80,96},{96,112},{112,0},{1... | collective-permute-start | bytes 786440 | tf_op jit(solution)/shard_map/ppermute | solution.py:110
  3.3 3.8 %collective-permute-start.6 = (bf16[128,1024]{1,0:T(8,128)(2,1)}, bf16[128,1024]{1,0:T(8,128)(2,1)S(1)}, u32[]{:S(2)}, u32[]{:S(2)}) collective-permute-start(bf16[128,1024]{1,0:T(8,128)(2,1)} %param.7), channel_id=1, source_target_pairs={{0,112},{16,0},{32,16},{48,32},{64,48},{80,64},{96,80},{112,96},{1... | collective-permute-start | bytes 786440 | tf_op jit(solution)/shard_map/ppermute | solution.py:110
  7.2 10.7 %collective-permute-start = (bf16[256,512]{1,0:T(8,128)(2,1)}, bf16[256,512]{1,0:T(8,128)(2,1)S(1)}, u32[]{:S(2)}, u32[]{:S(2)}) collective-permute-start(bf16[256,512]{1,0:T(8,128)(2,1)} %param.6), channel_id=1, source_target_pairs={{0,7},{1,0},{2,1},{3,2},{4,3},{5,4},{6,5},{7,6},{8,15},{9,8},{10,9... | collective-permute-start | bytes 786440 | tf_op jit(solution)/shard_map/ppermute | solution.py:110
  17.8 1.9 collective-permute-start.2
  19.8 3.1 %collective-permute-start.12 = (bf16[1024,512]{1,0:T(8,128)(2,1)}, bf16[1024,512]{1,0:T(8,128)(2,1)S(1)}, u32[]{:S(2)}, u32[]{:S(2)}) collective-permute-start(bf16[1024,512]{1,0:T(8,128)(2,1)} %param.9), channel_id=1, source_target_pairs={{0,8},{8,0},{1,9},{9,1},{2,10},{10,2},{3,11},{11,3},{4,12},{12,4},... | collective-permute-start | bytes 3145736 | tf_op jit(solution)/shard_map/ppermute | solution.py:114
  22.9 1.9 convolution_dynamic-update-slice_fusion.4
  26.0 2.8 %collective-permute-start.9 = (bf16[256,1024]{1,0:T(8,128)(2,1)S(1)}, bf16[256,1024]{1,0:T(8,128)(2,1)S(1)}, u32[]{:S(2)}, u32[]{:S(2)}) collective-permute-start(bf16[256,1024]{1,0:T(8,128)(2,1)S(1)} %get-tuple-element.27), channel_id=1, source_target_pairs={{0,32},{16,48},{32,64},{48,80},{64,96},{80,112},{96,0},{112,16},{1... | collective-permute-start | bytes 1572872 | tf_op jit(solution)/shard_map/ppermute | solution.py:110
  28.8 4.6 %collective-permute-start.7 = (bf16[256,1024]{1,0:T(8,128)(2,1)S(1)}, bf16[256,1024]{1,0:T(8,128)(2,1)S(1)}, u32[]{:S(2)}, u32[]{:S(2)}) collective-permute-start(bf16[256,1024]{1,0:T(8,128)(2,1)S(1)} %get-tuple-element.28), channel_id=1, source_target_pairs={{0,96},{16,112},{32,0},{48,16},{64,32},{80,48},{96,64},{112,80},{1... | collective-permute-start | bytes 1572872 | tf_op jit(solution)/shard_map/ppermute | solution.py:110
  33.5 1.9 collective-permute-start.3
  35.5 5.5 %collective-permute-start.1 = (bf16[512,512]{1,0:T(8,128)(2,1)S(1)}, bf16[512,512]{1,0:T(8,128)(2,1)S(1)}, u32[]{:S(2)}, u32[]{:S(2)}) collective-permute-start(bf16[512,512]{1,0:T(8,128)(2,1)S(1)} %get-tuple-element.30), channel_id=1, source_target_pairs={{0,6},{1,7},{2,0},{3,1},{4,2},{5,3},{6,4},{7,5},{8,14},{9,15},{10,... | collective-permute-start | bytes 1572872 | tf_op jit(solution)/shard_map/ppermute | solution.py:110
  42.5 12.4 %collective-permute-done.9 = bf16[256,1024]{1,0:T(8,128)(2,1)S(1)} collective-permute-done((bf16[256,1024]{1,0:T(8,128)(2,1)S(1)}, bf16[256,1024]{1,0:T(8,128)(2,1)S(1)}, u32[]{:S(2)}, u32[]{:S(2)}) %collective-permute-start.9) | collective-permute-done | bytes 524320 | tf_op jit(solution)/shard_map/ppermute | solution.py:110
  54.9 1.9 collective-permute-start.10
  56.8 1.7 collective-permute-done.7
  58.5 2.9 %collective-permute-start.11 = (bf16[64,1024]{1,0:T(8,128)(2,1)S(1)}, bf16[64,1024]{1,0:T(8,128)(2,1)S(1)}, u32[]{:S(2)}, u32[]{:S(2)}) collective-permute-start(bf16[64,1024]{1,0:T(8,128)(2,1)S(1)} %slice.103), channel_id=1, source_target_pairs={{0,112},{16,0},{32,16},{48,32},{64,48},{80,64},{96,80},{112,96},{1... | collective-permute-start | bytes 393224 | tf_op jit(solution)/shard_map/ppermute | solution.py:110
  61.5 3.0 %collective-permute-start.4 = (bf16[128,512]{1,0:T(8,128)(2,1)S(1)}, bf16[128,512]{1,0:T(8,128)(2,1)S(1)}, u32[]{:S(2)}, u32[]{:S(2)}) collective-permute-start(bf16[128,512]{1,0:T(8,128)(2,1)S(1)} %slice.100), channel_id=1, source_target_pairs={{0,1},{1,2},{2,3},{3,4},{4,5},{5,6},{6,7},{7,0},{8,9},{9,10},{10,1... | collective-permute-start | bytes 393224 | tf_op jit(solution)/shard_map/ppermute | solution.py:110
  64.5 3.8 %collective-permute-start.5 = (bf16[128,512]{1,0:T(8,128)(2,1)S(1)}, bf16[128,512]{1,0:T(8,128)(2,1)S(1)}, u32[]{:S(2)}, u32[]{:S(2)}) collective-permute-start(bf16[128,512]{1,0:T(8,128)(2,1)S(1)} %slice.101), channel_id=1, source_target_pairs={{0,7},{1,0},{2,1},{3,2},{4,3},{5,4},{6,5},{7,6},{8,15},{9,8},{10,9... | collective-permute-start | bytes 393224 | tf_op jit(solution)/shard_map/ppermute | solution.py:110
  71.5 1.1 convolution_dynamic-update-slice_fusion
  73.6 57.8 %all-reduce.3.kv_ref = bf16[2048,256]{1,0:T(8,128)(2,1)} all-reduce(f32[2048,256]{1,0:T(8,128)} %convolution_dynamic-update-slice_fusion.2), channel_id=1, replica_groups=mesh['dp'=4,'y'=8,'core'=2,'z'=8] {'y','core'}, use_global_device_ids=true, to_apply=%region_0.0 | all-reduce | flops 524288 | bytes 3145728 | tf_op jit(solution)/shard_map/psum | solution.py:149
  131.4 9.3 %attend.5 = bf16[128,1024]{1,0:T(8,128)(2,1)} custom-call(s32[3]{0:T(128)} %pad_add_fusion.ids, s32[8]{0:T(128)} %lengths.5, s32[32]{0:T(128)} %order.5, bf16[1024,1024]{1,0:T(8,128)(2,1)} %copy-done.4, bf16[2048,256]{1,0:T(8,128)(2,1)} %all-reduce.3.kv_ref), custom_call_target="tpu_custom_call" | custom-call | flops 600000000 | bytes 1000000 | tf_op jit(solution)/shard_map/attend/pallas_call | solution.py:86
  140.6 15.3 %attend.3 = bf16[384,1024]{1,0:T(8,128)(2,1)} custom-call(s32[3]{0:T(128)} %pad_add_fusion.ids, s32[8]{0:T(128)} %lengths.5, s32[32]{0:T(128)} %order.5, bf16[1024,1024]{1,0:T(8,128)(2,1)} %copy-done.4, bf16[2048,256]{1,0:T(8,128)(2,1)} %all-reduce.3.kv_ref), custom_call_target="tpu_custom_call" | custom-call | flops 1800000000 | bytes 3000000 | tf_op jit(solution)/shard_map/attend/pallas_call | solution.py:86
  155.9 20.3 %attend.4 = bf16[512,1024]{1,0:T(8,128)(2,1)} custom-call(s32[3]{0:T(128)} %pad_add_fusion.ids, s32[8]{0:T(128)} %lengths.5, s32[32]{0:T(128)} %order.5, bf16[1024,1024]{1,0:T(8,128)(2,1)} %copy-done.4, bf16[2048,256]{1,0:T(8,128)(2,1)} %all-reduce.3.kv_ref), custom_call_target="tpu_custom_call" | custom-call | flops 2400000000 | bytes 4000000 | tf_op jit(solution)/shard_map/attend/pallas_call | solution.py:86
  178.9 1.9 collective-permute-start.13
  180.8 4.9 %collective-permute-start.15 = (bf16[128,512]{1,0:T(8,128)(2,1)S(1)}, bf16[128,512]{1,0:T(8,128)(2,1)S(1)}, u32[]{:S(2)}, u32[]{:S(2)}) collective-permute-start(bf16[128,512]{1,0:T(8,128)(2,1)S(1)} %convolution_convert_fusion), channel_id=1, source_target_pairs={{0,7},{1,0},{2,1},{3,2},{4,3},{5,4},{6,5},{7,6},{8,15},{9,8},{10,9... | collective-permute-start | bytes 393224 | tf_op jit(solution)/shard_map/ppermute | solution.py:110
  186.4 1.5 collective-permute-done.15
  188.0 5.3 %collective-permute-start.16 = (bf16[256,1024]{1,0:T(8,128)(2,1)S(1)}, bf16[256,1024]{1,0:T(8,128)(2,1)S(1)}, u32[]{:S(2)}, u32[]{:S(2)}) collective-permute-start(bf16[256,1024]{1,0:T(8,128)(2,1)S(1)} %pad_maximum_fusion.5), channel_id=1, source_target_pairs={{0,6},{1,7},{2,0},{3,1},{4,2},{5,3},{6,4},{7,5},{8,14},{9,15},{10,... | collective-permute-start | bytes 1572872 | tf_op jit(solution)/shard_map/ppermute | solution.py:110
  193.4 1.9 collective-permute-start.14
  196.1 20.4 %collective-permute-done.16 = bf16[256,1024]{1,0:T(8,128)(2,1)S(1)} collective-permute-done((bf16[256,1024]{1,0:T(8,128)(2,1)S(1)}, bf16[256,1024]{1,0:T(8,128)(2,1)S(1)}, u32[]{:S(2)}, u32[]{:S(2)}) %collective-permute-start.16) | collective-permute-done | bytes 524320 | tf_op jit(solution)/shard_map/ppermute | solution.py:110
  216.6 4.9 %collective-permute-start.18 = (bf16[128,1024]{1,0:T(8,128)(2,1)S(1)}, bf16[128,1024]{1,0:T(8,128)(2,1)S(1)}, u32[]{:S(2)}, u32[]{:S(2)}) collective-permute-start(bf16[128,1024]{1,0:T(8,128)(2,1)S(1)} %fusion.7), channel_id=1, source_target_pairs={{0,7},{1,0},{2,1},{3,2},{4,3},{5,4},{6,5},{7,6},{8,15},{9,8},{10,9... | collective-permute-start | bytes 786440 | tf_op jit(solution)/shard_map/ppermute | solution.py:110
  221.6 3.0 %collective-permute-start.17 = (bf16[128,1024]{1,0:T(8,128)(2,1)S(1)}, bf16[128,1024]{1,0:T(8,128)(2,1)S(1)}, u32[]{:S(2)}, u32[]{:S(2)}) collective-permute-start(bf16[128,1024]{1,0:T(8,128)(2,1)S(1)} %fusion.6), channel_id=1, source_target_pairs={{0,1},{1,2},{2,3},{3,4},{4,5},{5,6},{6,7},{7,0},{8,9},{9,10},{10,1... | collective-permute-start | bytes 786440 | tf_op jit(solution)/shard_map/ppermute | solution.py:110
  224.6 2.0 collective-permute-done.18
  226.6 4.7 %collective-permute-done.17 = bf16[128,1024]{1,0:T(8,128)(2,1)S(1)} collective-permute-done((bf16[128,1024]{1,0:T(8,128)(2,1)S(1)}, bf16[128,1024]{1,0:T(8,128)(2,1)S(1)}, u32[]{:S(2)}, u32[]{:S(2)}) %collective-permute-start.17) | collective-permute-done | bytes 262176 | tf_op jit(solution)/shard_map/ppermute | solution.py:110
  231.6 4.0 %collective-permute-start.19 = (bf16[128,512]{1,0:T(8,128)(2,1)S(1)}, bf16[128,512]{1,0:T(8,128)(2,1)S(1)}, u32[]{:S(2)}, u32[]{:S(2)}) collective-permute-start(bf16[128,512]{1,0:T(8,128)(2,1)S(1)} %get-tuple-element.26), channel_id=1, source_target_pairs={{0,8},{8,0},{1,9},{9,1},{2,10},{10,2},{3,11},{11,3},{4,12},{12,4},... | collective-permute-start | bytes 393224 | tf_op jit(solution)/shard_map/ppermute | solution.py:114
  (67 shorter events, 13.2 us)
Async XLA Ops:
  0.0 22.9 %copy-start = (bf16[512,256]{1,0:T(8,128)(2,1)S(1)}, bf16[512,256]{1,0:T(8,128)(2,1)}, u32[]{:S(2)}) copy-start(bf16[512,256]{1,0:T(8,128)(2,1)} %param.8) | copy-start | bytes 786436
  0.0 33.4 %copy-start.6 = (bf16[256,512]{1,0:T(8,128)(2,1)S(1)}, bf16[256,512]{1,0:T(8,128)(2,1)}, u32[]{:S(2)}) copy-start(bf16[256,512]{1,0:T(8,128)(2,1)} %param.6) | copy-start | bytes 786436
  0.0 24.9 %collective-permute-start.8 = (bf16[128,1024]{1,0:T(8,128)(2,1)}, bf16[128,1024]{1,0:T(8,128)(2,1)S(1)}, u32[]{:S(2)}, u32[]{:S(2)}) collective-permute-start(bf16[128,1024]{1,0:T(8,128)(2,1)} %param.7), channel_id=1, source_target_pairs={{0,16},{16,32},{32,48},{48,64},{64,80},{80,96},{96,112},{112,0},{1... | collective-permute-start | bytes 786440 | tf_op jit(solution)/shard_map/ppermute | solution.py:110
  3.3 21.5 %collective-permute-start.6 = (bf16[128,1024]{1,0:T(8,128)(2,1)}, bf16[128,1024]{1,0:T(8,128)(2,1)S(1)}, u32[]{:S(2)}, u32[]{:S(2)}) collective-permute-start(bf16[128,1024]{1,0:T(8,128)(2,1)} %param.7), channel_id=1, source_target_pairs={{0,112},{16,0},{32,16},{48,32},{64,48},{80,64},{96,80},{112,96},{1... | collective-permute-start | bytes 786440 | tf_op jit(solution)/shard_map/ppermute | solution.py:110
  7.2 26.2 %collective-permute-start = (bf16[256,512]{1,0:T(8,128)(2,1)}, bf16[256,512]{1,0:T(8,128)(2,1)S(1)}, u32[]{:S(2)}, u32[]{:S(2)}) collective-permute-start(bf16[256,512]{1,0:T(8,128)(2,1)} %param.6), channel_id=1, source_target_pairs={{0,7},{1,0},{2,1},{3,2},{4,3},{5,4},{6,5},{7,6},{8,15},{9,8},{10,9... | collective-permute-start | bytes 786440 | tf_op jit(solution)/shard_map/ppermute | solution.py:110
  17.8 15.6 %collective-permute-start.2 = (bf16[256,512]{1,0:T(8,128)(2,1)}, bf16[256,512]{1,0:T(8,128)(2,1)S(1)}, u32[]{:S(2)}, u32[]{:S(2)}) collective-permute-start(bf16[256,512]{1,0:T(8,128)(2,1)} %param.6), channel_id=1, source_target_pairs={{0,1},{1,2},{2,3},{3,4},{4,5},{5,6},{6,7},{7,0},{8,9},{9,10},{10,1... | collective-permute-start | bytes 786440 | tf_op jit(solution)/shard_map/ppermute | solution.py:110
  19.8 53.8 %collective-permute-start.12 = (bf16[1024,512]{1,0:T(8,128)(2,1)}, bf16[1024,512]{1,0:T(8,128)(2,1)S(1)}, u32[]{:S(2)}, u32[]{:S(2)}) collective-permute-start(bf16[1024,512]{1,0:T(8,128)(2,1)} %param.9), channel_id=1, source_target_pairs={{0,8},{8,0},{1,9},{9,1},{2,10},{10,2},{3,11},{11,3},{4,12},{12,4},... | collective-permute-start | bytes 3145736 | tf_op jit(solution)/shard_map/ppermute | solution.py:114
  22.9 18.6 %copy-start.7 = (bf16[128,1024]{1,0:T(8,128)(2,1)S(1)}, bf16[128,1024]{1,0:T(8,128)(2,1)}, u32[]{:S(2)}) copy-start(bf16[128,1024]{1,0:T(8,128)(2,1)} %param.7) | copy-start | bytes 786436
  26.0 28.9 %collective-permute-start.9 = (bf16[256,1024]{1,0:T(8,128)(2,1)S(1)}, bf16[256,1024]{1,0:T(8,128)(2,1)S(1)}, u32[]{:S(2)}, u32[]{:S(2)}) collective-permute-start(bf16[256,1024]{1,0:T(8,128)(2,1)S(1)} %get-tuple-element.27), channel_id=1, source_target_pairs={{0,32},{16,48},{32,64},{48,80},{64,96},{80,112},{96,0},{112,16},{1... | collective-permute-start | bytes 1572872 | tf_op jit(solution)/shard_map/ppermute | solution.py:110
  28.8 29.7 %collective-permute-start.7 = (bf16[256,1024]{1,0:T(8,128)(2,1)S(1)}, bf16[256,1024]{1,0:T(8,128)(2,1)S(1)}, u32[]{:S(2)}, u32[]{:S(2)}) collective-permute-start(bf16[256,1024]{1,0:T(8,128)(2,1)S(1)} %get-tuple-element.28), channel_id=1, source_target_pairs={{0,96},{16,112},{32,0},{48,16},{64,32},{80,48},{96,64},{112,80},{1... | collective-permute-start | bytes 1572872 | tf_op jit(solution)/shard_map/ppermute | solution.py:110
  33.5 27.9 %collective-permute-start.3 = (bf16[512,512]{1,0:T(8,128)(2,1)S(1)}, bf16[512,512]{1,0:T(8,128)(2,1)S(1)}, u32[]{:S(2)}, u32[]{:S(2)}) collective-permute-start(bf16[512,512]{1,0:T(8,128)(2,1)S(1)} %get-tuple-element.29), channel_id=1, source_target_pairs={{0,2},{1,3},{2,4},{3,5},{4,6},{5,7},{6,0},{7,1},{8,10},{9,11},{10,... | collective-permute-start | bytes 1572872 | tf_op jit(solution)/shard_map/ppermute | solution.py:110
  35.5 29.0 %collective-permute-start.1 = (bf16[512,512]{1,0:T(8,128)(2,1)S(1)}, bf16[512,512]{1,0:T(8,128)(2,1)S(1)}, u32[]{:S(2)}, u32[]{:S(2)}) collective-permute-start(bf16[512,512]{1,0:T(8,128)(2,1)S(1)} %get-tuple-element.30), channel_id=1, source_target_pairs={{0,6},{1,7},{2,0},{3,1},{4,2},{5,3},{6,4},{7,5},{8,14},{9,15},{10,... | collective-permute-start | bytes 1572872 | tf_op jit(solution)/shard_map/ppermute | solution.py:110
  54.9 15.3 %collective-permute-start.10 = (bf16[64,1024]{1,0:T(8,128)(2,1)S(1)}, bf16[64,1024]{1,0:T(8,128)(2,1)S(1)}, u32[]{:S(2)}, u32[]{:S(2)}) collective-permute-start(bf16[64,1024]{1,0:T(8,128)(2,1)S(1)} %slice.102), channel_id=1, source_target_pairs={{0,16},{16,32},{32,48},{48,64},{64,80},{80,96},{96,112},{112,0},{1... | collective-permute-start | bytes 393224 | tf_op jit(solution)/shard_map/ppermute | solution.py:110
  58.5 11.8 %collective-permute-start.11 = (bf16[64,1024]{1,0:T(8,128)(2,1)S(1)}, bf16[64,1024]{1,0:T(8,128)(2,1)S(1)}, u32[]{:S(2)}, u32[]{:S(2)}) collective-permute-start(bf16[64,1024]{1,0:T(8,128)(2,1)S(1)} %slice.103), channel_id=1, source_target_pairs={{0,112},{16,0},{32,16},{48,32},{64,48},{80,64},{96,80},{112,96},{1... | collective-permute-start | bytes 393224 | tf_op jit(solution)/shard_map/ppermute | solution.py:110
  61.5 7.9 %collective-permute-start.4 = (bf16[128,512]{1,0:T(8,128)(2,1)S(1)}, bf16[128,512]{1,0:T(8,128)(2,1)S(1)}, u32[]{:S(2)}, u32[]{:S(2)}) collective-permute-start(bf16[128,512]{1,0:T(8,128)(2,1)S(1)} %slice.100), channel_id=1, source_target_pairs={{0,1},{1,2},{2,3},{3,4},{4,5},{5,6},{6,7},{7,0},{8,9},{9,10},{10,1... | collective-permute-start | bytes 393224 | tf_op jit(solution)/shard_map/ppermute | solution.py:110
  64.5 5.9 %collective-permute-start.5 = (bf16[128,512]{1,0:T(8,128)(2,1)S(1)}, bf16[128,512]{1,0:T(8,128)(2,1)S(1)}, u32[]{:S(2)}, u32[]{:S(2)}) collective-permute-start(bf16[128,512]{1,0:T(8,128)(2,1)S(1)} %slice.101), channel_id=1, source_target_pairs={{0,7},{1,0},{2,1},{3,2},{4,3},{5,4},{6,5},{7,6},{8,15},{9,8},{10,9... | collective-permute-start | bytes 393224 | tf_op jit(solution)/shard_map/ppermute | solution.py:110
  70.4 2.3 copy-start.4
  155.9 20.4 %copy-start.1 = (bf16[1024,512]{1,0:T(8,128)(2,1)S(1)}, bf16[1024,512]{1,0:T(8,128)(2,1)}, u32[]{:S(2)}) copy-start(bf16[1024,512]{1,0:T(8,128)(2,1)} %param.9) | copy-start | bytes 3145732
  155.9 20.4 %copy-start.5 = (bf16[128,1024]{1,0:T(8,128)(2,1)S(1)}, bf16[128,1024]{1,0:T(8,128)(2,1)}, u32[]{:S(2)}) copy-start(bf16[128,1024]{1,0:T(8,128)(2,1)} %attend.5) | copy-start | bytes 786436
  176.3 1.2 copy-start.2
  178.2 7.5 %copy-start.3 = (bf16[384,1024]{1,0:T(8,128)(2,1)S(1)}, bf16[384,1024]{1,0:T(8,128)(2,1)}, u32[]{:S(2)}) copy-start(bf16[384,1024]{1,0:T(8,128)(2,1)} %attend.3) | copy-start | bytes 2359300
  178.9 14.4 %collective-permute-start.13 = (bf16[128,512]{1,0:T(8,128)(2,1)S(1)}, bf16[128,512]{1,0:T(8,128)(2,1)S(1)}, u32[]{:S(2)}, u32[]{:S(2)}) collective-permute-start(bf16[128,512]{1,0:T(8,128)(2,1)S(1)} %convolution_convert_fusion.1), channel_id=1, source_target_pairs={{0,1},{1,2},{2,3},{3,4},{4,5},{5,6},{6,7},{7,0},{8,9},{9,10},{10,1... | collective-permute-start | bytes 393224 | tf_op jit(solution)/shard_map/ppermute | solution.py:110
  180.8 7.1 %collective-permute-start.15 = (bf16[128,512]{1,0:T(8,128)(2,1)S(1)}, bf16[128,512]{1,0:T(8,128)(2,1)S(1)}, u32[]{:S(2)}, u32[]{:S(2)}) collective-permute-start(bf16[128,512]{1,0:T(8,128)(2,1)S(1)} %convolution_convert_fusion), channel_id=1, source_target_pairs={{0,7},{1,0},{2,1},{3,2},{4,3},{5,4},{6,5},{7,6},{8,15},{9,8},{10,9... | collective-permute-start | bytes 393224 | tf_op jit(solution)/shard_map/ppermute | solution.py:110
  188.0 28.5 %collective-permute-start.16 = (bf16[256,1024]{1,0:T(8,128)(2,1)S(1)}, bf16[256,1024]{1,0:T(8,128)(2,1)S(1)}, u32[]{:S(2)}, u32[]{:S(2)}) collective-permute-start(bf16[256,1024]{1,0:T(8,128)(2,1)S(1)} %pad_maximum_fusion.5), channel_id=1, source_target_pairs={{0,6},{1,7},{2,0},{3,1},{4,2},{5,3},{6,4},{7,5},{8,14},{9,15},{10,... | collective-permute-start | bytes 1572872 | tf_op jit(solution)/shard_map/ppermute | solution.py:110
  193.4 28.1 %collective-permute-start.14 = (bf16[256,1024]{1,0:T(8,128)(2,1)S(1)}, bf16[256,1024]{1,0:T(8,128)(2,1)S(1)}, u32[]{:S(2)}, u32[]{:S(2)}) collective-permute-start(bf16[256,1024]{1,0:T(8,128)(2,1)S(1)} %pad_maximum_fusion.4), channel_id=1, source_target_pairs={{0,2},{1,3},{2,4},{3,5},{4,6},{5,7},{6,0},{7,1},{8,10},{9,11},{10,... | collective-permute-start | bytes 1572872 | tf_op jit(solution)/shard_map/ppermute | solution.py:110
  216.6 10.0 %collective-permute-start.18 = (bf16[128,1024]{1,0:T(8,128)(2,1)S(1)}, bf16[128,1024]{1,0:T(8,128)(2,1)S(1)}, u32[]{:S(2)}, u32[]{:S(2)}) collective-permute-start(bf16[128,1024]{1,0:T(8,128)(2,1)S(1)} %fusion.7), channel_id=1, source_target_pairs={{0,7},{1,0},{2,1},{3,2},{4,3},{5,4},{6,5},{7,6},{8,15},{9,8},{10,9... | collective-permute-start | bytes 786440 | tf_op jit(solution)/shard_map/ppermute | solution.py:110
  221.6 9.7 %collective-permute-start.17 = (bf16[128,1024]{1,0:T(8,128)(2,1)S(1)}, bf16[128,1024]{1,0:T(8,128)(2,1)S(1)}, u32[]{:S(2)}, u32[]{:S(2)}) collective-permute-start(bf16[128,1024]{1,0:T(8,128)(2,1)S(1)} %fusion.6), channel_id=1, source_target_pairs={{0,1},{1,2},{2,3},{3,4},{4,5},{5,6},{6,7},{7,0},{8,9},{9,10},{10,1... | collective-permute-start | bytes 786440 | tf_op jit(solution)/shard_map/ppermute | solution.py:110
  231.6 5.0 %collective-permute-start.19 = (bf16[128,512]{1,0:T(8,128)(2,1)S(1)}, bf16[128,512]{1,0:T(8,128)(2,1)S(1)}, u32[]{:S(2)}, u32[]{:S(2)}) collective-permute-start(bf16[128,512]{1,0:T(8,128)(2,1)S(1)} %get-tuple-element.26), channel_id=1, source_target_pairs={{0,8},{8,0},{1,9},{9,1},{2,10},{10,2},{3,11},{11,3},{4,12},{12,4},... | collective-permute-start | bytes 393224 | tf_op jit(solution)/shard_map/ppermute | solution.py:114

commit v2 on v1

--- a/solution.py
+++ b/solution.py
@@ -7,6 +7,7 @@
 from jax.experimental import pallas as pl
 from jax.experimental.pallas import tpu as pltpu
 from jax.sharding import Mesh, PartitionSpec as P
+
 
 HEAD = 128
 RING = 8
@@ -61,9 +62,10 @@
         new = jnp.maximum(old, jnp.max(scores, axis=1, keepdims=True))
         top_ref[...] = new
         keep = jnp.exp2((old - new) * EXP_SCALE)
-        probs = jnp.exp2((scores - new[:, :1]) * EXP_SCALE).astype(jnp.bfloat16)
+        wide = jnp.concatenate([new, new], axis=1)
+        probs = jnp.exp2((scores - wide) * EXP_SCALE).astype(jnp.bfloat16)
         both = jnp.concatenate([values, ones], axis=1)
-        acc_ref[...] = acc_ref[...] * keep[:, :1] + jnp.dot(
+        acc_ref[...] = acc_ref[...] * jnp.concatenate([keep, keep], axis=1) + jnp.dot(
             probs, both, preferred_element_type=jnp.float32
         )
 
@@ -114,19 +116,6 @@
     return lax.ppermute(x, "core", [(0, 1), (1, 0)])
 
 
-def gather_rounds(x, axis):
-    half = x.shape[0] // 2
-    up, down = shift(x, axis, -1), shift(x, axis, 1)
-    yield (up, down)
-    up2 = shift(jnp.concatenate([x, up], axis=0), axis, -2)
-    down2 = shift(jnp.concatenate([down, x], axis=0), axis, 2)
-    yield (up2, down2)
-    rows = x.shape[0]
-    far_top = shift(down2[:half], axis, 1)
-    far_bottom = shift(up2[rows + half :], axis, -1)
-    yield (far_top, far_bottom)
-
-
 def local(tokens, queries, key_value_weight, out_weight, doc_lengths, block_order):
     z, y, core = lax.axis_index("z"), lax.axis_index("y"), lax.axis_index("core")
     ids = jnp.stack([z, y, core]).astype(jnp.int32)
@@ -135,18 +124,24 @@
     def project(block):
         return jnp.dot(block, key_value_weight, preferred_element_type=jnp.float32)
 
-    token_rounds, query_rounds = gather_rounds(tokens, "z"), gather_rounds(queries, "y")
-    (t_up, t_down), (q_up, q_down) = next(token_rounds), next(query_rounds)
-    (t_up2, t_down2), (q_up2, q_down2) = next(token_rounds), next(query_rounds)
-    t_far, q_far = next(token_rounds), next(query_rounds)
+    size = tokens.shape[0]
+    t_up, t_down = shift(tokens, "z", -1), shift(tokens, "z", 1)
+    t_up2 = shift(jnp.concatenate([tokens, t_up], axis=0), "z", -2)
+    t_down2 = shift(jnp.concatenate([t_down, tokens], axis=0), "z", 2)
+    t_top = shift(t_down2[: size // 2], "z", 1)
+    t_bottom = shift(t_up2[size + size // 2 :], "z", -1)
+
+    q_far = shift(queries, "y", 4)
+    q_up, q_down = shift(queries, "y", -1), shift(queries, "y", 1)
+    q_up2 = shift(jnp.concatenate([queries, q_up], axis=0), "y", -2)
+    q_down2 = shift(jnp.concatenate([q_down, queries], axis=0), "y", 2)
+
     partial_kv = jnp.concatenate(
-        [project(b) for b in (tokens, t_up, t_up2, *t_far, t_down2, t_down)], axis=0
+        [project(b) for b in (tokens, t_up, t_up2, t_top, t_bottom, t_down2, t_down)], axis=0
     )
-    all_queries = jnp.concatenate([queries, q_up, q_up2, *q_far, q_down2, q_down], axis=0)
-    partial_kv, all_queries, other_weight = lax.optimization_barrier(
-        (partial_kv, all_queries, other_weight)
-    )
-    kv = lax.psum(partial_kv, ("y", "core")).astype(jnp.bfloat16)
+    kv = lax.psum(partial_kv, ("y", "core"))
+    kv = kv.astype(jnp.bfloat16)
+    all_queries = jnp.concatenate([queries, q_up, q_up2, q_far, q_down2, q_down], axis=0)
 
     def products(base, gap, units):
         attn = attend(base, gap, units, ids, doc_lengths, block_order, all_queries, kv)
@@ -161,7 +156,8 @@
         return jnp.concatenate([p[unit * rows : (unit + 1) * rows] for p in parts], axis=1)
 
     far = products(4, 0, 1)
-    far_up, far_down = shift(far[0].astype(bf16), "z", 1), shift(far[1].astype(bf16), "z", -1)
+    far_up = shift(far[0].astype(bf16), "z", 1)
+    far_down = shift(far[1].astype(bf16), "z", -1)
     middle = products(2, 1, 4)
     width = far_up.shape[1]
     zero = jnp.zeros((rows, width), f32)

time: 240 us -> 229 us (0.954)
  the two profiles are of different devices: /device:TPU:3 before, /device:TPU:31 now
where the time goes in v2:
time: 229 us; the launch traced here: 228 us
  starting transfers between devices  85.1 us (37%)
  blocking collectives  59.5 us (26%)
  Pallas kernels  33.5 us (15%)
  waiting for transfers between devices  26.5 us (12%)
  matrix products  13.1 us (6%)
  local copies, waits for them, and re-layouts  7.03 us (3%)
  other arithmetic  3.02 us (1%)
    ppermute x17, starting transfers between devices, shift(): return lax.ppermute(x, axis, [(i, (i + by) % RING) for i in range(RING)])  66.4 us
    psum x1, blocking collectives, local(): kv = lax.psum(partial_kv, ('y', 'core'))  59.5 us
    pallas_call x3, Pallas kernels, attend(): pl.pallas_call(functools.partial(attend_kernel, base, gap), out_shape=jax...  33.5 us
    ppermute x17, waiting for transfers between devices, shift(): return lax.ppermute(x, axis, [(i, (i + by) % RING) for i in range(RING)])  25.5 us
    ppermute x2, starting transfers between devices, swap(): return lax.ppermute(x, 'core', [(0, 1), (1, 0)])  18.7 us
    dot_general x7, matrix products, project(): return jnp.dot(block, key_value_weight, preferred_element_type=jnp.float32)  7.64 us
    dot_general x6, matrix products, products(): jnp.dot(attn, w, preferred_element_type=jnp.float32)  5.47 us
  transfers between devices with their start and end apart: 19, of which 5 were waited for; matrix products, arithmetic and copies ran while one was open for 10% of the time, Pallas kernels for 15%

profile of v2, /device:TPU:31, one launch (start us, length us, event | category | flops | bytes accessed | tf_op | source)
XLA Modules:
  0.0 228.3 jit_solution(627937031466516909)
XLA Ops:
  0.0 10.8 %collective-permute-start.5 = (bf16[256,512]{1,0:T(8,128)(2,1)}, bf16[256,512]{1,0:T(8,128)(2,1)S(1)}, u32[]{:S(2)}, u32[]{:S(2)}) collective-permute-start(bf16[256,512]{1,0:T(8,128)(2,1)} %param.6), channel_id=1, source_target_pairs={{0,7},{1,0},{2,1},{3,2},{4,3},{5,4},{6,5},{7,6},{8,15},{9,8},{10,9... | collective-permute-start | bytes 786440 | tf_op jit(solution)/shard_map/ppermute | solution.py:112
  10.8 1.9 collective-permute-start.7
  12.7 2.1 collective-permute-start
  14.8 4.4 %collective-permute-start.3 = (bf16[128,1024]{1,0:T(8,128)(2,1)}, bf16[128,1024]{1,0:T(8,128)(2,1)S(1)}, u32[]{:S(2)}, u32[]{:S(2)}) collective-permute-start(bf16[128,1024]{1,0:T(8,128)(2,1)} %param.7), channel_id=1, source_target_pairs={{0,16},{16,32},{32,48},{48,64},{64,80},{80,96},{96,112},{112,0},{1... | collective-permute-start | bytes 786440 | tf_op jit(solution)/shard_map/ppermute | solution.py:112
  19.2 4.8 %collective-permute-start.2 = (bf16[128,1024]{1,0:T(8,128)(2,1)}, bf16[128,1024]{1,0:T(8,128)(2,1)S(1)}, u32[]{:S(2)}, u32[]{:S(2)}) collective-permute-start(bf16[128,1024]{1,0:T(8,128)(2,1)} %param.7), channel_id=1, source_target_pairs={{0,64},{16,80},{32,96},{48,112},{64,0},{80,16},{96,32},{112,48},{1... | collective-permute-start | bytes 786440 | tf_op jit(solution)/shard_map/ppermute | solution.py:112
  24.0 1.9 convolution_dynamic-update-slice_fusion.4
  25.9 1.1 pad_maximum_fusion.3
  27.0 3.5 %collective-permute-start.6 = (bf16[512,512]{1,0:T(8,128)(2,1)S(1)}, bf16[512,512]{1,0:T(8,128)(2,1)S(1)}, u32[]{:S(2)}, u32[]{:S(2)}) collective-permute-start(bf16[512,512]{1,0:T(8,128)(2,1)S(1)} %get-tuple-element.22), channel_id=1, source_target_pairs={{0,6},{1,7},{2,0},{3,1},{4,2},{5,3},{6,4},{7,5},{8,14},{9,15},{10,... | collective-permute-start | bytes 1572872 | tf_op jit(solution)/shard_map/ppermute | solution.py:112
  30.5 2.8 %collective-permute-start.8 = (bf16[512,512]{1,0:T(8,128)(2,1)S(1)}, bf16[512,512]{1,0:T(8,128)(2,1)S(1)}, u32[]{:S(2)}, u32[]{:S(2)}) collective-permute-start(bf16[512,512]{1,0:T(8,128)(2,1)S(1)} %get-tuple-element.21), channel_id=1, source_target_pairs={{0,2},{1,3},{2,4},{3,5},{4,6},{5,7},{6,0},{7,1},{8,10},{9,11},{10,... | collective-permute-start | bytes 1572872 | tf_op jit(solution)/shard_map/ppermute | solution.py:112
  33.5 2.6 %collective-permute-start.1 = (bf16[256,1024]{1,0:T(8,128)(2,1)S(1)}, bf16[256,1024]{1,0:T(8,128)(2,1)S(1)}, u32[]{:S(2)}, u32[]{:S(2)}) collective-permute-start(bf16[256,1024]{1,0:T(8,128)(2,1)S(1)} %get-tuple-element.24), channel_id=1, source_target_pairs={{0,96},{16,112},{32,0},{48,16},{64,32},{80,48},{96,64},{112,80},{1... | collective-permute-start | bytes 1572872 | tf_op jit(solution)/shard_map/ppermute | solution.py:112
  37.4 4.8 %collective-permute-start.4 = (bf16[256,1024]{1,0:T(8,128)(2,1)S(1)}, bf16[256,1024]{1,0:T(8,128)(2,1)S(1)}, u32[]{:S(2)}, u32[]{:S(2)}) collective-permute-start(bf16[256,1024]{1,0:T(8,128)(2,1)S(1)} %get-tuple-element.23), channel_id=1, source_target_pairs={{0,32},{16,48},{32,64},{48,80},{64,96},{80,112},{96,0},{112,16},{1... | collective-permute-start | bytes 1572872 | tf_op jit(solution)/shard_map/ppermute | solution.py:112
  43.9 2.0 collective-permute-done.8
  45.9 16.1 %collective-permute-start.11 = (bf16[1024,512]{1,0:T(8,128)(2,1)S(1)}, bf16[1024,512]{1,0:T(8,128)(2,1)S(1)}, u32[]{:S(2)}, u32[]{:S(2)}) collective-permute-start(bf16[1024,512]{1,0:T(8,128)(2,1)S(1)} %copy-done.1), channel_id=1, source_target_pairs={{0,8},{8,0},{1,9},{9,1},{2,10},{10,2},{3,11},{11,3},{4,12},{12,4},... | collective-permute-start | bytes 3145736 | tf_op jit(solution)/shard_map/ppermute | solution.py:116
  62.1 1.9 collective-permute-start.9
  64.1 4.5 %collective-permute-start.10 = (bf16[128,512]{1,0:T(8,128)(2,1)S(1)}, bf16[128,512]{1,0:T(8,128)(2,1)S(1)}, u32[]{:S(2)}, u32[]{:S(2)}) collective-permute-start(bf16[128,512]{1,0:T(8,128)(2,1)S(1)} %slice.93), channel_id=1, source_target_pairs={{0,7},{1,0},{2,1},{3,2},{4,3},{5,4},{6,5},{7,6},{8,15},{9,8},{10,9... | collective-permute-start | bytes 393224 | tf_op jit(solution)/shard_map/ppermute | solution.py:112
  74.5 1.1 convolution_dynamic-update-slice_fusion
  76.6 59.5 %all-reduce.3.kv_ref = bf16[2048,256]{1,0:T(8,128)(2,1)} all-reduce(f32[2048,256]{1,0:T(8,128)} %convolution_dynamic-update-slice_fusion.2), channel_id=1, replica_groups=mesh['dp'=4,'y'=8,'core'=2,'z'=8] {'y','core'}, use_global_device_ids=true, to_apply=%region_0.0 | all-reduce | flops 524288 | bytes 3145728 | tf_op jit(solution)/shard_map/psum | solution.py:142
  136.1 15.0 %attend.4 = bf16[512,1024]{1,0:T(8,128)(2,1)} custom-call(s32[3]{0:T(128)} %pad_add_fusion.ids, s32[8]{0:T(128)} %lengths.5, s32[32]{0:T(128)} %order.5, bf16[1024,1024]{1,0:T(8,128)(2,1)} %constant_dynamic-update-slice_fusion.q_ref, bf16[2048,256]{1,0:T(8,128)(2,1)} %all-reduce.3.kv_ref), custom_call_target="tpu_custom_call" | custom-call | flops 2400000000 | bytes 4000000 | tf_op jit(solution)/shard_map/attend/pallas_call | solution.py:88
  151.2 5.6 %attend.5 = bf16[128,1024]{1,0:T(8,128)(2,1)} custom-call(s32[3]{0:T(128)} %pad_add_fusion.ids, s32[8]{0:T(128)} %lengths.5, s32[32]{0:T(128)} %order.5, bf16[1024,1024]{1,0:T(8,128)(2,1)} %constant_dynamic-update-slice_fusion.q_ref, bf16[2048,256]{1,0:T(8,128)(2,1)} %all-reduce.3.kv_ref), custom_call_target="tpu_custom_call" | custom-call | flops 600000000 | bytes 1000000 | tf_op jit(solution)/shard_map/attend/pallas_call | solution.py:88
  156.8 1.9 fusion.15
  159.0 12.9 %attend.3 = bf16[384,1024]{1,0:T(8,128)(2,1)} custom-call(s32[3]{0:T(128)} %pad_add_fusion.ids, s32[8]{0:T(128)} %lengths.5, s32[32]{0:T(128)} %order.5, bf16[1024,1024]{1,0:T(8,128)(2,1)} %constant_dynamic-update-slice_fusion.q_ref, bf16[2048,256]{1,0:T(8,128)(2,1)} %all-reduce.3.kv_ref), custom_call_target="tpu_custom_call" | custom-call | flops 1800000000 | bytes 3000000 | tf_op jit(solution)/shard_map/attend/pallas_call | solution.py:88
  171.9 1.9 collective-permute-start.12
  175.9 1.7 fusion.17
  178.9 4.6 %collective-permute-start.14 = (bf16[128,512]{1,0:T(8,128)(2,1)S(1)}, bf16[128,512]{1,0:T(8,128)(2,1)S(1)}, u32[]{:S(2)}, u32[]{:S(2)}) collective-permute-start(bf16[128,512]{1,0:T(8,128)(2,1)S(1)} %convolution_convert_fusion), channel_id=1, source_target_pairs={{0,7},{1,0},{2,1},{3,2},{4,3},{5,4},{6,5},{7,6},{8,15},{9,8},{10,9... | collective-permute-start | bytes 393224 | tf_op jit(solution)/shard_map/ppermute | solution.py:112
  183.6 2.1 collective-permute-start.13
  185.8 5.5 %collective-permute-start.15 = (bf16[256,1024]{1,0:T(8,128)(2,1)S(1)}, bf16[256,1024]{1,0:T(8,128)(2,1)S(1)}, u32[]{:S(2)}, u32[]{:S(2)}) collective-permute-start(bf16[256,1024]{1,0:T(8,128)(2,1)S(1)} %pad_maximum_fusion.5), channel_id=1, source_target_pairs={{0,6},{1,7},{2,0},{3,1},{4,2},{5,3},{6,4},{7,5},{8,14},{9,15},{10,... | collective-permute-start | bytes 1572872 | tf_op jit(solution)/shard_map/ppermute | solution.py:112
  191.9 17.6 %collective-permute-done.13 = bf16[256,1024]{1,0:T(8,128)(2,1)S(1)} collective-permute-done((bf16[256,1024]{1,0:T(8,128)(2,1)S(1)}, bf16[256,1024]{1,0:T(8,128)(2,1)S(1)}, u32[]{:S(2)}, u32[]{:S(2)}) %collective-permute-start.13) | collective-permute-done | bytes 524320 | tf_op jit(solution)/shard_map/ppermute | solution.py:112
  209.6 1.9 collective-permute-start.16
  211.6 6.3 %collective-permute-start.17 = (bf16[128,1024]{1,0:T(8,128)(2,1)S(1)}, bf16[128,1024]{1,0:T(8,128)(2,1)S(1)}, u32[]{:S(2)}, u32[]{:S(2)}) collective-permute-start(bf16[128,1024]{1,0:T(8,128)(2,1)S(1)} %fusion.7), channel_id=1, source_target_pairs={{0,7},{1,0},{2,1},{3,2},{4,3},{5,4},{6,5},{7,6},{8,15},{9,8},{10,9... | collective-permute-start | bytes 786440 | tf_op jit(solution)/shard_map/ppermute | solution.py:112
  217.9 2.2 collective-permute-done.16
  220.2 3.6 %collective-permute-done.17 = bf16[128,1024]{1,0:T(8,128)(2,1)S(1)} collective-permute-done((bf16[128,1024]{1,0:T(8,128)(2,1)S(1)}, bf16[128,1024]{1,0:T(8,128)(2,1)S(1)}, u32[]{:S(2)}, u32[]{:S(2)}) %collective-permute-start.17) | collective-permute-done | bytes 262176 | tf_op jit(solution)/shard_map/ppermute | solution.py:112
  223.9 2.6 %collective-permute-start.18 = (bf16[128,512]{1,0:T(8,128)(2,1)S(1)}, bf16[128,512]{1,0:T(8,128)(2,1)S(1)}, u32[]{:S(2)}, u32[]{:S(2)}) collective-permute-start(bf16[128,512]{1,0:T(8,128)(2,1)S(1)} %get-tuple-element.20), channel_id=1, source_target_pairs={{0,8},{8,0},{1,9},{9,1},{2,10},{10,2},{3,11},{11,3},{4,12},{12,4},... | collective-permute-start | bytes 393224 | tf_op jit(solution)/shard_map/ppermute | solution.py:116
  (63 shorter events, 16.5 us)
Async XLA Ops:
  0.0 24.0 %copy-start = (bf16[512,256]{1,0:T(8,128)(2,1)S(1)}, bf16[512,256]{1,0:T(8,128)(2,1)}, u32[]{:S(2)}) copy-start(bf16[512,256]{1,0:T(8,128)(2,1)} %param.8) | copy-start | bytes 786436
  0.0 33.4 %copy-start.6 = (bf16[128,1024]{1,0:T(8,128)(2,1)S(1)}, bf16[128,1024]{1,0:T(8,128)(2,1)}, u32[]{:S(2)}) copy-start(bf16[128,1024]{1,0:T(8,128)(2,1)} %param.7) | copy-start | bytes 786436
  0.0 25.9 %collective-permute-start.5 = (bf16[256,512]{1,0:T(8,128)(2,1)}, bf16[256,512]{1,0:T(8,128)(2,1)S(1)}, u32[]{:S(2)}, u32[]{:S(2)}) collective-permute-start(bf16[256,512]{1,0:T(8,128)(2,1)} %param.6), channel_id=1, source_target_pairs={{0,7},{1,0},{2,1},{3,2},{4,3},{5,4},{6,5},{7,6},{8,15},{9,8},{10,9... | collective-permute-start | bytes 786440 | tf_op jit(solution)/shard_map/ppermute | solution.py:112
  10.8 15.1 %collective-permute-start.7 = (bf16[256,512]{1,0:T(8,128)(2,1)}, bf16[256,512]{1,0:T(8,128)(2,1)S(1)}, u32[]{:S(2)}, u32[]{:S(2)}) collective-permute-start(bf16[256,512]{1,0:T(8,128)(2,1)} %param.6), channel_id=1, source_target_pairs={{0,1},{1,2},{2,3},{3,4},{4,5},{5,6},{6,7},{7,0},{8,9},{9,10},{10,1... | collective-permute-start | bytes 786440 | tf_op jit(solution)/shard_map/ppermute | solution.py:112
  12.7 20.6 %collective-permute-start = (bf16[128,1024]{1,0:T(8,128)(2,1)}, bf16[128,1024]{1,0:T(8,128)(2,1)S(1)}, u32[]{:S(2)}, u32[]{:S(2)}) collective-permute-start(bf16[128,1024]{1,0:T(8,128)(2,1)} %param.7), channel_id=1, source_target_pairs={{0,112},{16,0},{32,16},{48,32},{64,48},{80,64},{96,80},{112,96},{1... | collective-permute-start | bytes 786440 | tf_op jit(solution)/shard_map/ppermute | solution.py:112
  14.8 18.5 %collective-permute-start.3 = (bf16[128,1024]{1,0:T(8,128)(2,1)}, bf16[128,1024]{1,0:T(8,128)(2,1)S(1)}, u32[]{:S(2)}, u32[]{:S(2)}) collective-permute-start(bf16[128,1024]{1,0:T(8,128)(2,1)} %param.7), channel_id=1, source_target_pairs={{0,16},{16,32},{32,48},{48,64},{64,80},{80,96},{96,112},{112,0},{1... | collective-permute-start | bytes 786440 | tf_op jit(solution)/shard_map/ppermute | solution.py:112
  19.2 50.2 %collective-permute-start.2 = (bf16[128,1024]{1,0:T(8,128)(2,1)}, bf16[128,1024]{1,0:T(8,128)(2,1)S(1)}, u32[]{:S(2)}, u32[]{:S(2)}) collective-permute-start(bf16[128,1024]{1,0:T(8,128)(2,1)} %param.7), channel_id=1, source_target_pairs={{0,64},{16,80},{32,96},{48,112},{64,0},{80,16},{96,32},{112,48},{1... | collective-permute-start | bytes 786440 | tf_op jit(solution)/shard_map/ppermute | solution.py:112
  27.0 18.9 %copy-start.1 = (bf16[1024,512]{1,0:T(8,128)(2,1)S(1)}, bf16[1024,512]{1,0:T(8,128)(2,1)}, u32[]{:S(2)}) copy-start(bf16[1024,512]{1,0:T(8,128)(2,1)} %param.9) | copy-start | bytes 3145732
  27.0 35.1 %collective-permute-start.6 = (bf16[512,512]{1,0:T(8,128)(2,1)S(1)}, bf16[512,512]{1,0:T(8,128)(2,1)S(1)}, u32[]{:S(2)}, u32[]{:S(2)}) collective-permute-start(bf16[512,512]{1,0:T(8,128)(2,1)S(1)} %get-tuple-element.22), channel_id=1, source_target_pairs={{0,6},{1,7},{2,0},{3,1},{4,2},{5,3},{6,4},{7,5},{8,14},{9,15},{10,... | collective-permute-start | bytes 1572872 | tf_op jit(solution)/shard_map/ppermute | solution.py:112
  30.5 15.4 %collective-permute-start.8 = (bf16[512,512]{1,0:T(8,128)(2,1)S(1)}, bf16[512,512]{1,0:T(8,128)(2,1)S(1)}, u32[]{:S(2)}, u32[]{:S(2)}) collective-permute-start(bf16[512,512]{1,0:T(8,128)(2,1)S(1)} %get-tuple-element.21), channel_id=1, source_target_pairs={{0,2},{1,3},{2,4},{3,5},{4,6},{5,7},{6,0},{7,1},{8,10},{9,11},{10,... | collective-permute-start | bytes 1572872 | tf_op jit(solution)/shard_map/ppermute | solution.py:112
  33.5 30.6 %collective-permute-start.1 = (bf16[256,1024]{1,0:T(8,128)(2,1)S(1)}, bf16[256,1024]{1,0:T(8,128)(2,1)S(1)}, u32[]{:S(2)}, u32[]{:S(2)}) collective-permute-start(bf16[256,1024]{1,0:T(8,128)(2,1)S(1)} %get-tuple-element.24), channel_id=1, source_target_pairs={{0,96},{16,112},{32,0},{48,16},{64,32},{80,48},{96,64},{112,80},{1... | collective-permute-start | bytes 1572872 | tf_op jit(solution)/shard_map/ppermute | solution.py:112
  37.4 33.9 %collective-permute-start.4 = (bf16[256,1024]{1,0:T(8,128)(2,1)S(1)}, bf16[256,1024]{1,0:T(8,128)(2,1)S(1)}, u32[]{:S(2)}, u32[]{:S(2)}) collective-permute-start(bf16[256,1024]{1,0:T(8,128)(2,1)S(1)} %get-tuple-element.23), channel_id=1, source_target_pairs={{0,32},{16,48},{32,64},{48,80},{64,96},{80,112},{96,0},{112,16},{1... | collective-permute-start | bytes 1572872 | tf_op jit(solution)/shard_map/ppermute | solution.py:112
  45.9 131.7 %collective-permute-start.11 = (bf16[1024,512]{1,0:T(8,128)(2,1)S(1)}, bf16[1024,512]{1,0:T(8,128)(2,1)S(1)}, u32[]{:S(2)}, u32[]{:S(2)}) collective-permute-start(bf16[1024,512]{1,0:T(8,128)(2,1)S(1)} %copy-done.1), channel_id=1, source_target_pairs={{0,8},{8,0},{1,9},{9,1},{2,10},{10,2},{3,11},{11,3},{4,12},{12,4},... | collective-permute-start | bytes 3145736 | tf_op jit(solution)/shard_map/ppermute | solution.py:116
  62.1 10.7 %collective-permute-start.9 = (bf16[128,512]{1,0:T(8,128)(2,1)S(1)}, bf16[128,512]{1,0:T(8,128)(2,1)S(1)}, u32[]{:S(2)}, u32[]{:S(2)}) collective-permute-start(bf16[128,512]{1,0:T(8,128)(2,1)S(1)} %slice.92), channel_id=1, source_target_pairs={{0,1},{1,2},{2,3},{3,4},{4,5},{5,6},{6,7},{7,0},{8,9},{9,10},{10,1... | collective-permute-start | bytes 393224 | tf_op jit(solution)/shard_map/ppermute | solution.py:112
  64.1 9.6 %collective-permute-start.10 = (bf16[128,512]{1,0:T(8,128)(2,1)S(1)}, bf16[128,512]{1,0:T(8,128)(2,1)S(1)}, u32[]{:S(2)}, u32[]{:S(2)}) collective-permute-start(bf16[128,512]{1,0:T(8,128)(2,1)S(1)} %slice.93), channel_id=1, source_target_pairs={{0,7},{1,0},{2,1},{3,2},{4,3},{5,4},{6,5},{7,6},{8,15},{9,8},{10,9... | collective-permute-start | bytes 393224 | tf_op jit(solution)/shard_map/ppermute | solution.py:112
  151.2 5.6 %copy-start.2 = (bf16[512,1024]{1,0:T(8,128)(2,1)S(1)}, bf16[512,1024]{1,0:T(8,128)(2,1)}, u32[]{:S(2)}) copy-start(bf16[512,1024]{1,0:T(8,128)(2,1)} %attend.4) | copy-start | bytes 3145732
  156.8 1.9 copy-start.4
  171.9 11.6 %collective-permute-start.12 = (bf16[128,512]{1,0:T(8,128)(2,1)S(1)}, bf16[128,512]{1,0:T(8,128)(2,1)S(1)}, u32[]{:S(2)}, u32[]{:S(2)}) collective-permute-start(bf16[128,512]{1,0:T(8,128)(2,1)S(1)} %convolution_convert_fusion.1), channel_id=1, source_target_pairs={{0,1},{1,2},{2,3},{3,4},{4,5},{5,6},{6,7},{7,0},{8,9},{9,10},{10,1... | collective-permute-start | bytes 393224 | tf_op jit(solution)/shard_map/ppermute | solution.py:112
  177.6 1.0 copy-start.5
  178.9 6.8 %collective-permute-start.14 = (bf16[128,512]{1,0:T(8,128)(2,1)S(1)}, bf16[128,512]{1,0:T(8,128)(2,1)S(1)}, u32[]{:S(2)}, u32[]{:S(2)}) collective-permute-start(bf16[128,512]{1,0:T(8,128)(2,1)S(1)} %convolution_convert_fusion), channel_id=1, source_target_pairs={{0,7},{1,0},{2,1},{3,2},{4,3},{5,4},{6,5},{7,6},{8,15},{9,8},{10,9... | collective-permute-start | bytes 393224 | tf_op jit(solution)/shard_map/ppermute | solution.py:112
  183.5 7.8 %copy-start.3 = (bf16[384,1024]{1,0:T(8,128)(2,1)S(1)}, bf16[384,1024]{1,0:T(8,128)(2,1)}, u32[]{:S(2)}) copy-start(bf16[384,1024]{1,0:T(8,128)(2,1)} %attend.3) | copy-start | bytes 2359300
  183.6 25.9 %collective-permute-start.13 = (bf16[256,1024]{1,0:T(8,128)(2,1)S(1)}, bf16[256,1024]{1,0:T(8,128)(2,1)S(1)}, u32[]{:S(2)}, u32[]{:S(2)}) collective-permute-start(bf16[256,1024]{1,0:T(8,128)(2,1)S(1)} %pad_maximum_fusion.4), channel_id=1, source_target_pairs={{0,2},{1,3},{2,4},{3,5},{4,6},{5,7},{6,0},{7,1},{8,10},{9,11},{10,... | collective-permute-start | bytes 1572872 | tf_op jit(solution)/shard_map/ppermute | solution.py:112
  185.8 25.7 %collective-permute-start.15 = (bf16[256,1024]{1,0:T(8,128)(2,1)S(1)}, bf16[256,1024]{1,0:T(8,128)(2,1)S(1)}, u32[]{:S(2)}, u32[]{:S(2)}) collective-permute-start(bf16[256,1024]{1,0:T(8,128)(2,1)S(1)} %pad_maximum_fusion.5), channel_id=1, source_target_pairs={{0,6},{1,7},{2,0},{3,1},{4,2},{5,3},{6,4},{7,5},{8,14},{9,15},{10,... | collective-permute-start | bytes 1572872 | tf_op jit(solution)/shard_map/ppermute | solution.py:112
  209.6 10.6 %collective-permute-start.16 = (bf16[128,1024]{1,0:T(8,128)(2,1)S(1)}, bf16[128,1024]{1,0:T(8,128)(2,1)S(1)}, u32[]{:S(2)}, u32[]{:S(2)}) collective-permute-start(bf16[128,1024]{1,0:T(8,128)(2,1)S(1)} %fusion.6), channel_id=1, source_target_pairs={{0,1},{1,2},{2,3},{3,4},{4,5},{5,6},{6,7},{7,0},{8,9},{9,10},{10,1... | collective-permute-start | bytes 786440 | tf_op jit(solution)/shard_map/ppermute | solution.py:112
  211.6 12.1 %collective-permute-start.17 = (bf16[128,1024]{1,0:T(8,128)(2,1)S(1)}, bf16[128,1024]{1,0:T(8,128)(2,1)S(1)}, u32[]{:S(2)}, u32[]{:S(2)}) collective-permute-start(bf16[128,1024]{1,0:T(8,128)(2,1)S(1)} %fusion.7), channel_id=1, source_target_pairs={{0,7},{1,0},{2,1},{3,2},{4,3},{5,4},{6,5},{7,6},{8,15},{9,8},{10,9... | collective-permute-start | bytes 786440 | tf_op jit(solution)/shard_map/ppermute | solution.py:112
  223.9 3.6 %collective-permute-start.18 = (bf16[128,512]{1,0:T(8,128)(2,1)S(1)}, bf16[128,512]{1,0:T(8,128)(2,1)S(1)}, u32[]{:S(2)}, u32[]{:S(2)}) collective-permute-start(bf16[128,512]{1,0:T(8,128)(2,1)S(1)} %get-tuple-element.20), channel_id=1, source_target_pairs={{0,8},{8,0},{1,9},{9,1},{2,10},{10,2},{3,11},{11,3},{4,12},{12,4},... | collective-permute-start | bytes 393224 | tf_op jit(solution)/shard_map/ppermute | solution.py:116

commit v3 on v2

--- a/solution.py
+++ b/solution.py
@@ -20,7 +20,7 @@
 def attend_kernel(base, gap, ids, lengths, order, q_ref, kv_ref, out_ref, acc_ref, top_ref):
     step = pl.program_id(0)
     unit = step // 2
-    z, core = ids[0], ids[2]
+    z, core = ids[0], ids[1]
     owner = (z + base + unit + gap * (unit // 2)) % RING
     first = order[(owner * 2 + core) * 2 + step % 2] * BLOCK
     heads = q_ref.shape[1] // HEAD
@@ -82,7 +82,7 @@
 
     def q_map(i, ids, lengths, order):
         unit = i // 2
-        block = (ids[0] + base + unit + gap * (unit // 2) - ids[1] + RING) % RING
+        block = (ids[0] + base + unit + gap * (unit // 2)) % RING
         return (block * 2 + i % 2, 0)
 
     return pl.pallas_call(
@@ -117,8 +117,8 @@
 
 
 def local(tokens, queries, key_value_weight, out_weight, doc_lengths, block_order):
-    z, y, core = lax.axis_index("z"), lax.axis_index("y"), lax.axis_index("core")
-    ids = jnp.stack([z, y, core]).astype(jnp.int32)
+    z, core = lax.axis_index("z"), lax.axis_index("core")
+    ids = jnp.stack([z, core]).astype(jnp.int32)
     other_weight = swap(out_weight)
 
     def project(block):
@@ -131,17 +131,13 @@
     t_top = shift(t_down2[: size // 2], "z", 1)
     t_bottom = shift(t_up2[size + size // 2 :], "z", -1)
 
-    q_far = shift(queries, "y", 4)
-    q_up, q_down = shift(queries, "y", -1), shift(queries, "y", 1)
-    q_up2 = shift(jnp.concatenate([queries, q_up], axis=0), "y", -2)
-    q_down2 = shift(jnp.concatenate([q_down, queries], axis=0), "y", 2)
+    all_queries = lax.all_gather(queries, "y", axis=0, tiled=True)
 
     partial_kv = jnp.concatenate(
         [project(b) for b in (tokens, t_up, t_up2, t_top, t_bottom, t_down2, t_down)], axis=0
     )
     kv = lax.psum(partial_kv, ("y", "core"))
     kv = kv.astype(jnp.bfloat16)
-    all_queries = jnp.concatenate([queries, q_up, q_up2, q_far, q_down2, q_down], axis=0)
 
     def products(base, gap, units):
         attn = attend(base, gap, units, ids, doc_lengths, block_order, all_queries, kv)

time: 229 us -> 233 us (1.017)
  starting transfers between devices: 85.1 us -> 52.3 us
  waiting for transfers between devices: 26.5 us -> 53.4 us
  between operations: 0.45 us -> 13.9 us
  local copies, waits for them, and re-layouts: 7.03 us -> 2.58 us
    ppermute x17 -> x12, waiting for transfers between devices: 25.5 us -> 52.4 us  [shift(): return lax.ppermute(x, axis, [(i, (i + by) % RING) for i in range(RING)])]
    ppermute x17 -> x12, starting transfers between devices: 66.4 us -> 46.8 us  [shift(): return lax.ppermute(x, axis, [(i, (i + by) % RING) for i in range(RING)])]
    ppermute x2, starting transfers between devices: 18.7 us -> 5.54 us  [swap(): return lax.ppermute(x, 'core', [(0, 1), (1, 0)])]
    dot_general x7, matrix products: 7.64 us -> 3.54 us  [project(): return jnp.dot(block, key_value_weight, preferred_element_type=jnp.float32)]
    unnamed x19 -> x26, local copies, waits for them, and re-layouts: 4.05 us -> 0.05 us
  transfers between devices with their start and end apart: 19 -> 15, of which waited for: 5 -> 9; matrix products, arithmetic and copies ran while one was open for 10% -> 5% of each run, Pallas kernels for 15% -> 12%
where the time goes in v3:
time: 233 us; the launch traced here: 232 us
  blocking collectives  61.4 us (26%)
  waiting for transfers between devices  53.4 us (23%)
  starting transfers between devices  52.3 us (22%)
  Pallas kernels  33.5 us (14%)
  between operations  13.9 us (6%)
  matrix products  10.9 us (5%)
  other arithmetic  3.96 us (2%)
  local copies, waits for them, and re-layouts  2.58 us (1%)
    psum x1, blocking collectives, local(): kv = lax.psum(partial_kv, ('y', 'core'))  61.4 us
    ppermute x12, waiting for transfers between devices, shift(): return lax.ppermute(x, axis, [(i, (i + by) % RING) for i in range(RING)])  52.4 us
    ppermute x12, starting transfers between devices, shift(): return lax.ppermute(x, axis, [(i, (i + by) % RING) for i in range(RING)])  46.8 us
    pallas_call x3, Pallas kernels, attend(): pl.pallas_call(functools.partial(attend_kernel, base, gap), out_shape=jax...  33.5 us
    dot_general x6, matrix products, products(): jnp.dot(attn, w, preferred_element_type=jnp.float32)  7.31 us
    ppermute x2, starting transfers between devices, swap(): return lax.ppermute(x, 'core', [(0, 1), (1, 0)])  5.54 us
  transfers between devices with their start and end apart: 15, of which 9 were waited for; matrix products, arithmetic and copies ran while one was open for 5% of the time, Pallas kernels for 12%

profile of v3, /device:TPU:31, one launch (start us, length us, event | category | flops | bytes accessed | tf_op | source)
XLA Modules:
  0.0 232.0 jit_solution(6524546333759337360)
XLA Ops:
  6.5 10.8 %collective-permute-start = (bf16[256,512]{1,0:T(8,128)(2,1)}, bf16[256,512]{1,0:T(8,128)(2,1)S(1)}, u32[]{:S(2)}, u32[]{:S(2)}) collective-permute-start(bf16[256,512]{1,0:T(8,128)(2,1)} %param.6), channel_id=1, source_target_pairs={{0,7},{1,0},{2,1},{3,2},{4,3},{5,4},{6,5},{7,6},{8,15},{9,8},{10,9... | collective-permute-start | bytes 786440 | tf_op jit(solution)/shard_map/ppermute | solution.py:112
  17.3 1.9 collective-permute-start.2
  19.3 2.9 %collective-permute-start.6 = (bf16[1024,512]{1,0:T(8,128)(2,1)}, bf16[1024,512]{1,0:T(8,128)(2,1)S(1)}, u32[]{:S(2)}, u32[]{:S(2)}) collective-permute-start(bf16[1024,512]{1,0:T(8,128)(2,1)} %param.9), channel_id=1, source_target_pairs={{0,8},{8,0},{1,9},{9,1},{2,10},{10,2},{3,11},{11,3},{4,12},{12,4},... | collective-permute-start | bytes 3145736 | tf_op jit(solution)/shard_map/ppermute | solution.py:116
  22.6 4.9 %collective-permute-done.2 = bf16[256,512]{1,0:T(8,128)(2,1)S(1)} collective-permute-done((bf16[256,512]{1,0:T(8,128)(2,1)}, bf16[256,512]{1,0:T(8,128)(2,1)S(1)}, u32[]{:S(2)}, u32[]{:S(2)}) %collective-permute-start.2) | collective-permute-done | bytes 262176 | tf_op jit(solution)/shard_map/ppermute | solution.py:112
  27.6 1.2 pad_maximum_fusion.1
  28.8 1.9 collective-permute-start.1
  30.7 4.3 %collective-permute-start.3 = (bf16[512,512]{1,0:T(8,128)(2,1)S(1)}, bf16[512,512]{1,0:T(8,128)(2,1)S(1)}, u32[]{:S(2)}, u32[]{:S(2)}) collective-permute-start(bf16[512,512]{1,0:T(8,128)(2,1)S(1)} %get-tuple-element.21), channel_id=1, source_target_pairs={{0,2},{1,3},{2,4},{3,5},{4,6},{5,7},{6,0},{7,1},{8,10},{9,11},{10,... | collective-permute-start | bytes 1572872 | tf_op jit(solution)/shard_map/ppermute | solution.py:112
  35.0 1.2 convolution_dynamic-update-slice_fusion.4
  36.8 1.2 convolution_dynamic-update-slice_fusion.3
  38.0 20.5 %collective-permute-done.3 = bf16[512,512]{1,0:T(8,128)(2,1)S(1)} collective-permute-done((bf16[512,512]{1,0:T(8,128)(2,1)S(1)}, bf16[512,512]{1,0:T(8,128)(2,1)S(1)}, u32[]{:S(2)}, u32[]{:S(2)}) %collective-permute-start.3) | collective-permute-done | bytes 524320 | tf_op jit(solution)/shard_map/ppermute | solution.py:112
  58.5 1.9 collective-permute-start.4
  60.4 4.6 %collective-permute-start.5 = (bf16[128,512]{1,0:T(8,128)(2,1)S(1)}, bf16[128,512]{1,0:T(8,128)(2,1)S(1)}, u32[]{:S(2)}, u32[]{:S(2)}) collective-permute-start(bf16[128,512]{1,0:T(8,128)(2,1)S(1)} %slice.93), channel_id=1, source_target_pairs={{0,7},{1,0},{2,1},{3,2},{4,3},{5,4},{6,5},{7,6},{8,15},{9,8},{10,9... | collective-permute-start | bytes 393224 | tf_op jit(solution)/shard_map/ppermute | solution.py:112
  67.7 61.4 %all-reduce.3.kv_ref = bf16[2048,256]{1,0:T(8,128)(2,1)} all-reduce(f32[2048,256]{1,0:T(8,128)S(1)} %convolution_dynamic-update-slice_fusion.2), channel_id=1, replica_groups=mesh['dp'=4,'y'=8,'core'=2,'z'=8] {'y','core'}, use_global_device_ids=true, to_apply=%region_0.0 | all-reduce | flops 524288 | bytes 3145728 | tf_op jit(solution)/shard_map/psum | solution.py:139
  129.1 15.2 %attend.4 = bf16[512,1024]{1,0:T(8,128)(2,1)} custom-call(s32[2]{0:T(128)} %pad_add_fusion.ids, s32[8]{0:T(128)} %lengths.5, s32[32]{0:T(128)} %order.5, bf16[1024,1024]{1,0:T(8,128)(2,1)} %all-gather.2.cloned.1.call-done.q_ref, bf16[2048,256]{1,0:T(8,128)(2,1)} %all-reduce.3.kv_ref), custom_call_target="tpu_custom_call" | custom-call | flops 2400000000 | bytes 4000000 | tf_op jit(solution)/shard_map/attend/pallas_call | solution.py:88
  144.3 2.0 fusion.15
  147.0 0.8 fusion.9
  148.7 5.5 %attend.5 = bf16[128,1024]{1,0:T(8,128)(2,1)} custom-call(s32[2]{0:T(128)} %pad_add_fusion.ids, s32[8]{0:T(128)} %lengths.5, s32[32]{0:T(128)} %order.5, bf16[1024,1024]{1,0:T(8,128)(2,1)} %all-gather.2.cloned.1.call-done.q_ref, bf16[2048,256]{1,0:T(8,128)(2,1)} %all-reduce.3.kv_ref), custom_call_target="tpu_custom_call" | custom-call | flops 600000000 | bytes 1000000 | tf_op jit(solution)/shard_map/attend/pallas_call | solution.py:88
  154.2 1.9 convolution_convert_fusion.1
  156.1 3.2 %collective-permute-start.7 = (bf16[128,512]{1,0:T(8,128)(2,1)}, bf16[128,512]{1,0:T(8,128)(2,1)}, u32[]{:S(2)}, u32[]{:S(2)}) collective-permute-start(bf16[128,512]{1,0:T(8,128)(2,1)} %convolution_convert_fusion.1), channel_id=1, source_target_pairs={{0,1},{1,2},{2,3},{3,4},{4,5},{5,6},{6,7},{7,0},{8,9},{9,10},{10,1... | collective-permute-start | bytes 393224 | tf_op jit(solution)/shard_map/ppermute | solution.py:112
  159.9 12.9 %attend.3 = bf16[384,1024]{1,0:T(8,128)(2,1)} custom-call(s32[2]{0:T(128)} %pad_add_fusion.ids, s32[8]{0:T(128)} %lengths.5, s32[32]{0:T(128)} %order.5, bf16[1024,1024]{1,0:T(8,128)(2,1)} %all-gather.2.cloned.1.call-done.q_ref, bf16[2048,256]{1,0:T(8,128)(2,1)} %all-reduce.3.kv_ref), custom_call_target="tpu_custom_call" | custom-call | flops 1800000000 | bytes 3000000 | tf_op jit(solution)/shard_map/attend/pallas_call | solution.py:88
  172.9 1.8 fusion.17
  175.0 3.4 %collective-permute-start.9 = (bf16[128,512]{1,0:T(8,128)(2,1)S(1)}, bf16[128,512]{1,0:T(8,128)(2,1)S(1)}, u32[]{:S(2)}, u32[]{:S(2)}) collective-permute-start(bf16[128,512]{1,0:T(8,128)(2,1)S(1)} %convolution_convert_fusion), channel_id=1, source_target_pairs={{0,7},{1,0},{2,1},{3,2},{4,3},{5,4},{6,5},{7,6},{8,15},{9,8},{10,9... | collective-permute-start | bytes 393224 | tf_op jit(solution)/shard_map/ppermute | solution.py:112
  179.1 0.9 fusion.4
  180.1 2.9 %collective-permute-start.8 = (bf16[256,1024]{1,0:T(8,128)(2,1)S(1)}, bf16[256,1024]{1,0:T(8,128)(2,1)S(1)}, u32[]{:S(2)}, u32[]{:S(2)}) collective-permute-start(bf16[256,1024]{1,0:T(8,128)(2,1)S(1)} %pad_maximum_fusion.2), channel_id=1, source_target_pairs={{0,2},{1,3},{2,4},{3,5},{4,6},{5,7},{6,0},{7,1},{8,10},{9,11},{10,... | collective-permute-start | bytes 1572872 | tf_op jit(solution)/shard_map/ppermute | solution.py:112
  183.2 4.5 %collective-permute-start.10 = (bf16[256,1024]{1,0:T(8,128)(2,1)S(1)}, bf16[256,1024]{1,0:T(8,128)(2,1)S(1)}, u32[]{:S(2)}, u32[]{:S(2)}) collective-permute-start(bf16[256,1024]{1,0:T(8,128)(2,1)S(1)} %pad_maximum_fusion.3), channel_id=1, source_target_pairs={{0,6},{1,7},{2,0},{3,1},{4,2},{5,3},{6,4},{7,5},{8,14},{9,15},{10,... | collective-permute-start | bytes 1572872 | tf_op jit(solution)/shard_map/ppermute | solution.py:112
  187.8 19.4 %collective-permute-done.8 = bf16[256,1024]{1,0:T(8,128)(2,1)S(1)} collective-permute-done((bf16[256,1024]{1,0:T(8,128)(2,1)S(1)}, bf16[256,1024]{1,0:T(8,128)(2,1)S(1)}, u32[]{:S(2)}, u32[]{:S(2)}) %collective-permute-start.8) | collective-permute-done | bytes 524320 | tf_op jit(solution)/shard_map/ppermute | solution.py:112
  207.2 1.9 collective-permute-start.11
  209.2 5.5 %collective-permute-start.12 = (bf16[128,1024]{1,0:T(8,128)(2,1)S(1)}, bf16[128,1024]{1,0:T(8,128)(2,1)S(1)}, u32[]{:S(2)}, u32[]{:S(2)}) collective-permute-start(bf16[128,1024]{1,0:T(8,128)(2,1)S(1)} %fusion.7), channel_id=1, source_target_pairs={{0,7},{1,0},{2,1},{3,2},{4,3},{5,4},{6,5},{7,6},{8,15},{9,8},{10,9... | collective-permute-start | bytes 786440 | tf_op jit(solution)/shard_map/ppermute | solution.py:112
  214.7 3.0 %collective-permute-done.11 = bf16[128,1024]{1,0:T(8,128)(2,1)S(1)} collective-permute-done((bf16[128,1024]{1,0:T(8,128)(2,1)S(1)}, bf16[128,1024]{1,0:T(8,128)(2,1)S(1)}, u32[]{:S(2)}, u32[]{:S(2)}) %collective-permute-start.11) | collective-permute-done | bytes 262176 | tf_op jit(solution)/shard_map/ppermute | solution.py:112
  217.8 2.7 %collective-permute-done.12 = bf16[128,1024]{1,0:T(8,128)(2,1)S(1)} collective-permute-done((bf16[128,1024]{1,0:T(8,128)(2,1)S(1)}, bf16[128,1024]{1,0:T(8,128)(2,1)S(1)}, u32[]{:S(2)}, u32[]{:S(2)}) %collective-permute-start.12) | collective-permute-done | bytes 262176 | tf_op jit(solution)/shard_map/ppermute | solution.py:112
  220.7 2.7 %collective-permute-start.13 = (bf16[128,512]{1,0:T(8,128)(2,1)S(1)}, bf16[128,512]{1,0:T(8,128)(2,1)S(1)}, u32[]{:S(2)}, u32[]{:S(2)}) collective-permute-start(bf16[128,512]{1,0:T(8,128)(2,1)S(1)} %get-tuple-element.20), channel_id=1, source_target_pairs={{0,8},{8,0},{1,9},{9,1},{2,10},{10,2},{3,11},{11,3},{4,12},{12,4},... | collective-permute-start | bytes 393224 | tf_op jit(solution)/shard_map/ppermute | solution.py:116
  223.4 1.0 collective-permute-done.13
  (61 shorter events, 8.3 us)
Async XLA Ops:
  6.5 28.4 %copy-start = (bf16[512,256]{1,0:T(8,128)(2,1)S(1)}, bf16[512,256]{1,0:T(8,128)(2,1)}, u32[]{:S(2)}) copy-start(bf16[512,256]{1,0:T(8,128)(2,1)} %param.8) | copy-start | bytes 786436
  6.5 122.5 %all-gather.2.cloned.1.call-start = ((), (), s32[]{:S(2)}) async-start(), calls=%async_computation | async-start | bytes 2359296 | tf_op jit(solution)/shard_map/all_gather | solution.py:134
  6.5 16.1 %collective-permute-start = (bf16[256,512]{1,0:T(8,128)(2,1)}, bf16[256,512]{1,0:T(8,128)(2,1)S(1)}, u32[]{:S(2)}, u32[]{:S(2)}) collective-permute-start(bf16[256,512]{1,0:T(8,128)(2,1)} %param.6), channel_id=1, source_target_pairs={{0,7},{1,0},{2,1},{3,2},{4,3},{5,4},{6,5},{7,6},{8,15},{9,8},{10,9... | collective-permute-start | bytes 786440 | tf_op jit(solution)/shard_map/ppermute | solution.py:112
  17.3 10.2 %collective-permute-start.2 = (bf16[256,512]{1,0:T(8,128)(2,1)}, bf16[256,512]{1,0:T(8,128)(2,1)S(1)}, u32[]{:S(2)}, u32[]{:S(2)}) collective-permute-start(bf16[256,512]{1,0:T(8,128)(2,1)} %param.6), channel_id=1, source_target_pairs={{0,1},{1,2},{2,3},{3,4},{4,5},{5,6},{6,7},{7,0},{8,9},{9,10},{10,1... | collective-permute-start | bytes 786440 | tf_op jit(solution)/shard_map/ppermute | solution.py:112
  19.3 127.0 %collective-permute-start.6 = (bf16[1024,512]{1,0:T(8,128)(2,1)}, bf16[1024,512]{1,0:T(8,128)(2,1)S(1)}, u32[]{:S(2)}, u32[]{:S(2)}) collective-permute-start(bf16[1024,512]{1,0:T(8,128)(2,1)} %param.9), channel_id=1, source_target_pairs={{0,8},{8,0},{1,9},{9,1},{2,10},{10,2},{3,11},{11,3},{4,12},{12,4},... | collective-permute-start | bytes 3145736 | tf_op jit(solution)/shard_map/ppermute | solution.py:116
  22.6 8.1 %copy-start.7 = (bf16[256,512]{1,0:T(8,128)(2,1)}, bf16[256,512]{1,0:T(8,128)(2,1)S(1)}, u32[]{:S(2)}) copy-start(bf16[256,512]{1,0:T(8,128)(2,1)S(1)} %collective-permute-done) | copy-start | bytes 786436
  27.6 3.1 %copy-start.5 = (bf16[256,512]{1,0:T(8,128)(2,1)}, bf16[256,512]{1,0:T(8,128)(2,1)S(1)}, u32[]{:S(2)}) copy-start(bf16[256,512]{1,0:T(8,128)(2,1)S(1)} %collective-permute-done.2) | copy-start | bytes 786436
  28.8 31.7 %collective-permute-start.1 = (bf16[512,512]{1,0:T(8,128)(2,1)S(1)}, bf16[512,512]{1,0:T(8,128)(2,1)S(1)}, u32[]{:S(2)}, u32[]{:S(2)}) collective-permute-start(bf16[512,512]{1,0:T(8,128)(2,1)S(1)} %get-tuple-element.22), channel_id=1, source_target_pairs={{0,6},{1,7},{2,0},{3,1},{4,2},{5,3},{6,4},{7,5},{8,14},{9,15},{10,... | collective-permute-start | bytes 1572872 | tf_op jit(solution)/shard_map/ppermute | solution.py:112
  30.7 27.8 %collective-permute-start.3 = (bf16[512,512]{1,0:T(8,128)(2,1)S(1)}, bf16[512,512]{1,0:T(8,128)(2,1)S(1)}, u32[]{:S(2)}, u32[]{:S(2)}) collective-permute-start(bf16[512,512]{1,0:T(8,128)(2,1)S(1)} %get-tuple-element.21), channel_id=1, source_target_pairs={{0,2},{1,3},{2,4},{3,5},{4,6},{5,7},{6,0},{7,1},{8,10},{9,11},{10,... | collective-permute-start | bytes 1572872 | tf_op jit(solution)/shard_map/ppermute | solution.py:112
  38.0 29.5 %copy-start.6 = (bf16[256,512]{1,0:T(8,128)(2,1)S(1)}, bf16[256,512]{1,0:T(8,128)(2,1)}, u32[]{:S(2)}) copy-start(bf16[256,512]{1,0:T(8,128)(2,1)} %copy-done.5) | copy-start | bytes 786436
  58.5 7.6 %collective-permute-start.4 = (bf16[128,512]{1,0:T(8,128)(2,1)S(1)}, bf16[128,512]{1,0:T(8,128)(2,1)S(1)}, u32[]{:S(2)}, u32[]{:S(2)}) collective-permute-start(bf16[128,512]{1,0:T(8,128)(2,1)S(1)} %slice.92), channel_id=1, source_target_pairs={{0,1},{1,2},{2,3},{3,4},{4,5},{5,6},{6,7},{7,0},{8,9},{9,10},{10,1... | collective-permute-start | bytes 393224 | tf_op jit(solution)/shard_map/ppermute | solution.py:112
  60.4 6.5 %collective-permute-start.5 = (bf16[128,512]{1,0:T(8,128)(2,1)S(1)}, bf16[128,512]{1,0:T(8,128)(2,1)S(1)}, u32[]{:S(2)}, u32[]{:S(2)}) collective-permute-start(bf16[128,512]{1,0:T(8,128)(2,1)S(1)} %slice.93), channel_id=1, source_target_pairs={{0,7},{1,0},{2,1},{3,2},{4,3},{5,4},{6,5},{7,6},{8,15},{9,8},{10,9... | collective-permute-start | bytes 393224 | tf_op jit(solution)/shard_map/ppermute | solution.py:112
  129.1 15.2 %copy-start.1 = (bf16[1024,512]{1,0:T(8,128)(2,1)S(1)}, bf16[1024,512]{1,0:T(8,128)(2,1)}, u32[]{:S(2)}) copy-start(bf16[1024,512]{1,0:T(8,128)(2,1)} %param.9) | copy-start | bytes 3145732
  144.3 2.0 copy-start.2
  156.1 23.0 %collective-permute-start.7 = (bf16[128,512]{1,0:T(8,128)(2,1)}, bf16[128,512]{1,0:T(8,128)(2,1)}, u32[]{:S(2)}, u32[]{:S(2)}) collective-permute-start(bf16[128,512]{1,0:T(8,128)(2,1)} %convolution_convert_fusion.1), channel_id=1, source_target_pairs={{0,1},{1,2},{2,3},{3,4},{4,5},{5,6},{6,7},{7,0},{8,9},{9,10},{10,1... | collective-permute-start | bytes 393224 | tf_op jit(solution)/shard_map/ppermute | solution.py:112
  172.9 1.8 copy-start.4
  172.9 5.6 %copy-start.3 = (bf16[384,1024]{1,0:T(8,128)(2,1)S(1)}, bf16[384,1024]{1,0:T(8,128)(2,1)}, u32[]{:S(2)}) copy-start(bf16[384,1024]{1,0:T(8,128)(2,1)} %attend.3) | copy-start | bytes 2359300
  174.7 4.4 %copy-start.10 = (f32[128,512]{1,0:T(8,128)S(1)}, f32[128,512]{1,0:T(8,128)}, u32[]{:S(2)}) copy-start(f32[128,512]{1,0:T(8,128)} %get-tuple-element.7) | copy-start | bytes 786436
  174.7 4.4 %copy-start.11 = (f32[128,512]{1,0:T(8,128)S(1)}, f32[128,512]{1,0:T(8,128)}, u32[]{:S(2)}) copy-start(f32[128,512]{1,0:T(8,128)} %get-tuple-element.5) | copy-start | bytes 786436
  175.0 5.1 %copy-start.12 = (bf16[128,512]{1,0:T(8,128)(2,1)S(1)}, bf16[128,512]{1,0:T(8,128)(2,1)}, u32[]{:S(2)}) copy-start(bf16[128,512]{1,0:T(8,128)(2,1)} %get-tuple-element.17) | copy-start | bytes 393220
  175.0 8.1 %copy-start.8 = (f32[128,512]{1,0:T(8,128)S(1)}, f32[128,512]{1,0:T(8,128)}, u32[]{:S(2)}) copy-start(f32[128,512]{1,0:T(8,128)} %get-tuple-element.8) | copy-start | bytes 786436
  175.0 8.1 %copy-start.9 = (f32[128,512]{1,0:T(8,128)S(1)}, f32[128,512]{1,0:T(8,128)}, u32[]{:S(2)}) copy-start(f32[128,512]{1,0:T(8,128)} %get-tuple-element.6) | copy-start | bytes 786436
  175.0 8.0 %collective-permute-start.9 = (bf16[128,512]{1,0:T(8,128)(2,1)S(1)}, bf16[128,512]{1,0:T(8,128)(2,1)S(1)}, u32[]{:S(2)}, u32[]{:S(2)}) collective-permute-start(bf16[128,512]{1,0:T(8,128)(2,1)S(1)} %convolution_convert_fusion), channel_id=1, source_target_pairs={{0,7},{1,0},{2,1},{3,2},{4,3},{5,4},{6,5},{7,6},{8,15},{9,8},{10,9... | collective-permute-start | bytes 393224 | tf_op jit(solution)/shard_map/ppermute | solution.py:112
  180.1 27.0 %collective-permute-start.8 = (bf16[256,1024]{1,0:T(8,128)(2,1)S(1)}, bf16[256,1024]{1,0:T(8,128)(2,1)S(1)}, u32[]{:S(2)}, u32[]{:S(2)}) collective-permute-start(bf16[256,1024]{1,0:T(8,128)(2,1)S(1)} %pad_maximum_fusion.2), channel_id=1, source_target_pairs={{0,2},{1,3},{2,4},{3,5},{4,6},{5,7},{6,0},{7,1},{8,10},{9,11},{10,... | collective-permute-start | bytes 1572872 | tf_op jit(solution)/shard_map/ppermute | solution.py:112
  183.2 26.0 %collective-permute-start.10 = (bf16[256,1024]{1,0:T(8,128)(2,1)S(1)}, bf16[256,1024]{1,0:T(8,128)(2,1)S(1)}, u32[]{:S(2)}, u32[]{:S(2)}) collective-permute-start(bf16[256,1024]{1,0:T(8,128)(2,1)S(1)} %pad_maximum_fusion.3), channel_id=1, source_target_pairs={{0,6},{1,7},{2,0},{3,1},{4,2},{5,3},{6,4},{7,5},{8,14},{9,15},{10,... | collective-permute-start | bytes 1572872 | tf_op jit(solution)/shard_map/ppermute | solution.py:112
  207.2 10.6 %collective-permute-start.11 = (bf16[128,1024]{1,0:T(8,128)(2,1)S(1)}, bf16[128,1024]{1,0:T(8,128)(2,1)S(1)}, u32[]{:S(2)}, u32[]{:S(2)}) collective-permute-start(bf16[128,1024]{1,0:T(8,128)(2,1)S(1)} %fusion.6), channel_id=1, source_target_pairs={{0,1},{1,2},{2,3},{3,4},{4,5},{5,6},{6,7},{7,0},{8,9},{9,10},{10,1... | collective-permute-start | bytes 786440 | tf_op jit(solution)/shard_map/ppermute | solution.py:112
  209.2 11.2 %collective-permute-start.12 = (bf16[128,1024]{1,0:T(8,128)(2,1)S(1)}, bf16[128,1024]{1,0:T(8,128)(2,1)S(1)}, u32[]{:S(2)}, u32[]{:S(2)}) collective-permute-start(bf16[128,1024]{1,0:T(8,128)(2,1)S(1)} %fusion.7), channel_id=1, source_target_pairs={{0,7},{1,0},{2,1},{3,2},{4,3},{5,4},{6,5},{7,6},{8,15},{9,8},{10,9... | collective-permute-start | bytes 786440 | tf_op jit(solution)/shard_map/ppermute | solution.py:112
  220.7 3.6 %collective-permute-start.13 = (bf16[128,512]{1,0:T(8,128)(2,1)S(1)}, bf16[128,512]{1,0:T(8,128)(2,1)S(1)}, u32[]{:S(2)}, u32[]{:S(2)}) collective-permute-start(bf16[128,512]{1,0:T(8,128)(2,1)S(1)} %get-tuple-element.20), channel_id=1, source_target_pairs={{0,8},{8,0},{1,9},{9,1},{2,10},{10,2},{3,11},{11,3},{4,12},{12,4},... | collective-permute-start | bytes 393224 | tf_op jit(solution)/shard_map/ppermute | solution.py:116
Sparse Core Ops, SparseCore 0:
  19.4 37.0 all-gather.1

commit v4 on v3

--- a/solution.py
+++ b/solution.py
@@ -17,11 +17,11 @@
 EXP_SCALE = math.log2(math.e) / math.sqrt(HEAD)
 
 
-def attend_kernel(base, gap, ids, lengths, order, q_ref, kv_ref, out_ref, acc_ref, top_ref):
+def attend_kernel(base, stride, ids, lengths, order, q_ref, kv_ref, out_ref, acc_ref, top_ref):
     step = pl.program_id(0)
     unit = step // 2
     z, core = ids[0], ids[1]
-    owner = (z + base + unit + gap * (unit // 2)) % RING
+    owner = (z + base + unit * stride) % RING
     first = order[(owner * 2 + core) * 2 + step % 2] * BLOCK
     heads = q_ref.shape[1] // HEAD
     rows = BLOCK * heads
@@ -47,7 +47,7 @@
     @pl.loop(0, last - lowest // KEYS + 1)
     def _(i):
         block = last - i
-        offset = pl.multiple_of(((block - z + RING) % RING) * KEYS, KEYS)
+        offset = pl.multiple_of(block * KEYS, KEYS)
         keys = kv_ref[pl.ds(offset, KEYS), :HEAD]
         values = kv_ref[pl.ds(offset, KEYS), HEAD:]
         scores = lax.dot_general(
@@ -76,17 +76,17 @@
         )
 
 
-def attend(base, gap, units, ids, lengths, order, queries, kv):
+def attend(base, stride, units, ids, lengths, order, queries, kv):
     width = queries.shape[1]
     heads = width // HEAD
 
     def q_map(i, ids, lengths, order):
         unit = i // 2
-        block = (ids[0] + base + unit + gap * (unit // 2)) % RING
+        block = (ids[0] + base + unit * stride - ids[2] + RING) % RING
         return (block * 2 + i % 2, 0)
 
     return pl.pallas_call(
-        functools.partial(attend_kernel, base, gap),
+        functools.partial(attend_kernel, base, stride),
         out_shape=jax.ShapeDtypeStruct((units * 2 * BLOCK, width), jnp.bfloat16),
         grid_spec=pltpu.PrefetchScalarGridSpec(
             num_scalar_prefetch=3,
@@ -116,61 +116,56 @@
     return lax.ppermute(x, "core", [(0, 1), (1, 0)])
 
 
+def ring_gather(x, axis):
+    half = x.shape[0] // 2
+    ups, downs = [x], [x]
+    for _ in range(3):
+        ups.append(shift(ups[-1], axis, -1))
+        downs.append(shift(downs[-1], axis, 1))
+    top = shift(downs[3][:half], axis, 1)
+    bottom = shift(ups[3][half:], axis, -1)
+    return jnp.concatenate([*ups, top, bottom, *downs[:0:-1]], axis=0)
+
+
 def local(tokens, queries, key_value_weight, out_weight, doc_lengths, block_order):
-    z, core = lax.axis_index("z"), lax.axis_index("core")
-    ids = jnp.stack([z, core]).astype(jnp.int32)
+    z, y, core = lax.axis_index("z"), lax.axis_index("y"), lax.axis_index("core")
+    ids = jnp.stack([z, core, y]).astype(jnp.int32)
+    all_tokens = lax.all_gather(tokens, "z", axis=0, tiled=True)
+    all_queries = ring_gather(queries, "y")
     other_weight = swap(out_weight)
+    partial_kv = jnp.dot(all_tokens, key_value_weight, preferred_element_type=jnp.float32)
+    partial_kv, all_queries, other_weight = lax.optimization_barrier(
+        (partial_kv, all_queries, other_weight)
+    )
+    kv = lax.psum(partial_kv, ("y", "core")).astype(jnp.bfloat16)
 
-    def project(block):
-        return jnp.dot(block, key_value_weight, preferred_element_type=jnp.float32)
+    f32, bf16 = jnp.float32, jnp.bfloat16
+    rows, width = queries.shape[0], out_weight.shape[1]
 
-    size = tokens.shape[0]
-    t_up, t_down = shift(tokens, "z", -1), shift(tokens, "z", 1)
-    t_up2 = shift(jnp.concatenate([tokens, t_up], axis=0), "z", -2)
-    t_down2 = shift(jnp.concatenate([t_down, tokens], axis=0), "z", 2)
-    t_top = shift(t_down2[: size // 2], "z", 1)
-    t_bottom = shift(t_up2[size + size // 2 :], "z", -1)
+    def products(base, stride, units):
+        attn = attend(
+            base, stride, units, ids, doc_lengths, block_order, all_queries, kv
+        )
+        parts = [
+            jnp.dot(attn, w, preferred_element_type=f32) for w in (out_weight, other_weight)
+        ]
+        return [
+            jnp.concatenate([p[i * rows : (i + 1) * rows] for p in parts], axis=1)
+            for i in range(units)
+        ]
 
-    all_queries = lax.all_gather(queries, "y", axis=0, tiled=True)
-
-    partial_kv = jnp.concatenate(
-        [project(b) for b in (tokens, t_up, t_up2, t_top, t_bottom, t_down2, t_down)], axis=0
-    )
-    kv = lax.psum(partial_kv, ("y", "core"))
-    kv = kv.astype(jnp.bfloat16)
-
-    def products(base, gap, units):
-        attn = attend(base, gap, units, ids, doc_lengths, block_order, all_queries, kv)
-        return tuple(
-            jnp.dot(attn, w, preferred_element_type=jnp.float32) for w in (out_weight, other_weight)
-        )
-
-    rows = queries.shape[0]
-    f32, bf16 = jnp.float32, jnp.bfloat16
-
-    def both(parts, unit):
-        return jnp.concatenate([p[unit * rows : (unit + 1) * rows] for p in parts], axis=1)
-
-    far = products(4, 0, 1)
-    far_up = shift(far[0].astype(bf16), "z", 1)
-    far_down = shift(far[1].astype(bf16), "z", -1)
-    middle = products(2, 1, 4)
-    width = far_up.shape[1]
-    zero = jnp.zeros((rows, width), f32)
-    third = both(middle, 1) + jnp.concatenate([far_up.astype(f32), zero], axis=1)
-    minus_third = both(middle, 2) + jnp.concatenate([zero, far_down.astype(f32)], axis=1)
-    up2 = shift(jnp.concatenate([both(middle, 0), third], axis=0).astype(bf16), "z", 2)
-    down2 = shift(jnp.concatenate([both(middle, 3), minus_third], axis=0).astype(bf16), "z", -2)
-    near = products(7, 0, 3)
-    up1 = shift((both(near, 2) + up2[rows:].astype(f32)).astype(bf16), "z", 1)
-    down1 = shift((both(near, 0) + down2[rows:].astype(f32)).astype(bf16), "z", -1)
-    total = (
-        both(near, 1)
-        + up2[:rows].astype(f32)
-        + down2[:rows].astype(f32)
-        + up1.astype(f32)
-        + down1.astype(f32)
-    ).astype(bf16)
+    far = products(4, 0, 1)[0].astype(bf16)
+    zero = jnp.zeros((rows, width), bf16)
+    up = shift(far[:, :width], "z", 1)
+    down = shift(far[:, width:], "z", -1)
+    up = jnp.concatenate([up, zero], axis=1)
+    down = jnp.concatenate([zero, down], axis=1)
+    for step in (3, 2, 1):
+        ahead, behind = products(step, RING - 2 * step, 2)
+        up = shift((ahead + up.astype(f32)).astype(bf16), "z", 1)
+        down = shift((behind + down.astype(f32)).astype(bf16), "z", -1)
+    own = products(0, 0, 1)[0]
+    total = (own + up.astype(f32) + down.astype(f32)).astype(bf16)
     mine, theirs = total[:, :width], swap(total[:, width:])
     return jnp.where(
         core == 0,

time: 233 us -> 224 us (0.961)
  waiting for transfers between devices: 53.4 us -> 21.1 us
  starting transfers between devices: 52.3 us -> 64.9 us
  local copies, waits for them, and re-layouts: 2.58 us -> 8.63 us
  Pallas kernels: 33.5 us -> 38.2 us
    ppermute x12 -> x16, waiting for transfers between devices: 52.4 us -> 19.4 us  [shift(): return lax.ppermute(x, axis, [(i, (i + by) % RING) for i in range(RING)])]
    ppermute x12 -> x16, starting transfers between devices: 46.8 us -> 58.4 us  [shift(): return lax.ppermute(x, axis, [(i, (i + by) % RING) for i in range(RING)])]
    unnamed x26 -> x32, local copies, waits for them, and re-layouts: 0.05 us -> 6.26 us
    pallas_call x3 -> x5, Pallas kernels: 33.5 us -> 38.2 us  [attend(): pl.pallas_call(functools.partial(attend_kernel, base, stride), out_shape=...]
    dot_general x13 -> x11, matrix products: 10.9 us -> 12.1 us  [the longest x10 9.85 us: products(): jnp.dot(attn, w, preferred_element_type=f32)]
  transfers between devices with their start and end apart: 15 -> 19, of which waited for: 9 -> 8; matrix products, arithmetic and copies ran while one was open for 5% -> 5% of each run, Pallas kernels for 12% -> 0%
where the time goes in v4:
time: 224 us; the launch traced here: 223 us
  starting transfers between devices  64.9 us (29%)
  blocking collectives  61.9 us (28%)
  Pallas kernels  38.2 us (17%)
  waiting for transfers between devices  21.1 us (9%)
  between operations  13.9 us (6%)
  matrix products  12.1 us (5%)
  local copies, waits for them, and re-layouts  8.63 us (4%)
    psum x1, blocking collectives, local(): kv = lax.psum(partial_kv, ('y', 'core')).astype(jnp.bfloat16)  61.9 us
    ppermute x16, starting transfers between devices, shift(): return lax.ppermute(x, axis, [(i, (i + by) % RING) for i in range(RING)])  58.4 us
    pallas_call x5, Pallas kernels, attend(): pl.pallas_call(functools.partial(attend_kernel, base, stride), out_shape=...  38.2 us
    ppermute x16, waiting for transfers between devices, shift(): return lax.ppermute(x, axis, [(i, (i + by) % RING) for i in range(RING)])  19.4 us
    dot_general x10, matrix products, products(): jnp.dot(attn, w, preferred_element_type=f32)  9.85 us
    ppermute x2, starting transfers between devices, swap(): return lax.ppermute(x, 'core', [(0, 1), (1, 0)])  6.46 us
    unnamed x32, local copies, waits for them, and re-layouts  6.26 us
  transfers between devices with their start and end apart: 19, of which 8 were waited for; matrix products, arithmetic and copies ran while one was open for 5% of the time, Pallas kernels for 0%

profile of v4, /device:TPU:31, one launch (start us, length us, event | category | flops | bytes accessed | tf_op | source)
XLA Modules:
  0.0 222.6 jit_solution(2500471344740040787)
XLA Ops:
  7.3 4.4 %collective-permute-start.3 = (bf16[128,1024]{1,0:T(8,128)(2,1)}, bf16[128,1024]{1,0:T(8,128)(2,1)S(1)}, u32[]{:S(2)}, u32[]{:S(2)}) collective-permute-start(bf16[128,1024]{1,0:T(8,128)(2,1)} %param.7), channel_id=1, source_target_pairs={{0,16},{16,32},{32,48},{48,64},{64,80},{80,96},{96,112},{112,0},{1... | collective-permute-start | bytes 786440 | tf_op jit(solution)/shard_map/ppermute | solution.py:112
  11.7 1.9 collective-permute-start
  13.6 3.4 %collective-permute-done.3 = bf16[128,1024]{1,0:T(8,128)(2,1)S(1)} collective-permute-done((bf16[128,1024]{1,0:T(8,128)(2,1)}, bf16[128,1024]{1,0:T(8,128)(2,1)S(1)}, u32[]{:S(2)}, u32[]{:S(2)}) %collective-permute-start.3) | collective-permute-done | bytes 262176 | tf_op jit(solution)/shard_map/ppermute | solution.py:112
  17.0 5.2 %collective-permute-start.4 = (bf16[128,1024]{1,0:T(8,128)(2,1)S(1)}, bf16[128,1024]{1,0:T(8,128)(2,1)}, u32[]{:S(2)}, u32[]{:S(2)}) collective-permute-start(bf16[128,1024]{1,0:T(8,128)(2,1)S(1)} %collective-permute-done.3), channel_id=1, source_target_pairs={{0,16},{16,32},{32,48},{48,64},{64,80},{80,96},{96,112},{112,0},{1... | collective-permute-start | bytes 786440 | tf_op jit(solution)/shard_map/ppermute | solution.py:112
  22.2 1.9 collective-permute-start.1
  24.1 3.7 %collective-permute-start.8 = (bf16[1024,512]{1,0:T(8,128)(2,1)}, bf16[1024,512]{1,0:T(8,128)(2,1)S(1)}, u32[]{:S(2)}, u32[]{:S(2)}) collective-permute-start(bf16[1024,512]{1,0:T(8,128)(2,1)} %param.9), channel_id=1, source_target_pairs={{0,8},{8,0},{1,9},{9,1},{2,10},{10,2},{3,11},{11,3},{4,12},{12,4},... | collective-permute-start | bytes 3145736 | tf_op jit(solution)/shard_map/ppermute | solution.py:116
  27.9 4.9 %collective-permute-start.5 = (bf16[128,1024]{1,0:T(8,128)(2,1)}, bf16[128,1024]{1,0:T(8,128)(2,1)}, u32[]{:S(2)}, u32[]{:S(2)}) collective-permute-start(bf16[128,1024]{1,0:T(8,128)(2,1)} %collective-permute-done.4), channel_id=1, source_target_pairs={{0,16},{16,32},{32,48},{48,64},{64,80},{80,96},{96,112},{112,0},{1... | collective-permute-start | bytes 786440 | tf_op jit(solution)/shard_map/ppermute | solution.py:112
  33.7 2.1 collective-permute-start.2
  38.4 5.2 %collective-permute-start.6 = (bf16[64,1024]{1,0:T(8,128)(2,1)S(1)}, bf16[64,1024]{1,0:T(8,128)(2,1)S(1)}, u32[]{:S(2)}, u32[]{:S(2)}) collective-permute-start(bf16[64,1024]{1,0:T(8,128)(2,1)S(1)} %slice.72), channel_id=1, source_target_pairs={{0,16},{16,32},{32,48},{48,64},{64,80},{80,96},{96,112},{112,0},{1... | collective-permute-start | bytes 393224 | tf_op jit(solution)/shard_map/ppermute | solution.py:112
  44.6 1.9 collective-permute-start.7
  46.6 4.9 %collective-permute-done.7 = bf16[64,1024]{1,0:T(8,128)(2,1)S(1)} collective-permute-done((bf16[64,1024]{1,0:T(8,128)(2,1)S(1)}, bf16[64,1024]{1,0:T(8,128)(2,1)S(1)}, u32[]{:S(2)}, u32[]{:S(2)}) %collective-permute-start.7) | collective-permute-done | bytes 131104 | tf_op jit(solution)/shard_map/ppermute | solution.py:112
  54.8 2.3 %fusion.15 = f32[2048,256]{1,0:T(8,128)S(1)} fusion(bf16[2048,512]{1,0:T(8,128)(2,1)} %all-gather.2.cloned.1.call-done, bf16[512,256]{1,0:T(8,128)(2,1)S(1)} %copy-done), kind=kOutput, calls=%fused_computation.35 | convolution fusion | flops 536870912 | bytes 4456448 | tf_op jit(solution)/shard_map/dot_general | solution.py:136
  57.1 61.9 %all-reduce.3.kv_ref = bf16[2048,256]{1,0:T(8,128)(2,1)} all-reduce(f32[2048,256]{1,0:T(8,128)S(1)} %fusion.15), channel_id=1, replica_groups=mesh['dp'=4,'y'=8,'core'=2,'z'=8] {'y','core'}, use_global_device_ids=true, to_apply=%region_0.0 | all-reduce | flops 524288 | bytes 3145728 | tf_op jit(solution)/shard_map/psum | solution.py:140
  119.0 7.6 %attend.8 = bf16[256,1024]{1,0:T(8,128)(2,1)} custom-call(s32[3]{0:T(128)} %pad_add_fusion.ids, s32[8]{0:T(128)} %lengths.9, s32[32]{0:T(128)} %order.9, bf16[1024,1024]{1,0:T(8,128)(2,1)} %copy-done.2, bf16[2048,256]{1,0:T(8,128)(2,1)} %all-reduce.3.kv_ref), custom_call_target="tpu_custom_call" | custom-call | flops 1200000000 | bytes 2000000 | tf_op jit(solution)/shard_map/attend/pallas_call | solution.py:88
  126.6 5.4 %attend.9 = bf16[128,1024]{1,0:T(8,128)(2,1)} custom-call(s32[3]{0:T(128)} %pad_add_fusion.ids, s32[8]{0:T(128)} %lengths.9, s32[32]{0:T(128)} %order.9, bf16[1024,1024]{1,0:T(8,128)(2,1)} %copy-done.2, bf16[2048,256]{1,0:T(8,128)(2,1)} %all-reduce.3.kv_ref), custom_call_target="tpu_custom_call" | custom-call | flops 600000000 | bytes 1000000 | tf_op jit(solution)/shard_map/attend/pallas_call | solution.py:88
  132.0 10.0 %attend.7 = bf16[256,1024]{1,0:T(8,128)(2,1)} custom-call(s32[3]{0:T(128)} %pad_add_fusion.ids, s32[8]{0:T(128)} %lengths.9, s32[32]{0:T(128)} %order.9, bf16[1024,1024]{1,0:T(8,128)(2,1)} %copy-done.2, bf16[2048,256]{1,0:T(8,128)(2,1)} %all-reduce.3.kv_ref), custom_call_target="tpu_custom_call" | custom-call | flops 1200000000 | bytes 2000000 | tf_op jit(solution)/shard_map/attend/pallas_call | solution.py:88
  147.0 11.3 %attend.6 = bf16[256,1024]{1,0:T(8,128)(2,1)} custom-call(s32[3]{0:T(128)} %pad_add_fusion.ids, s32[8]{0:T(128)} %lengths.9, s32[32]{0:T(128)} %order.9, bf16[1024,1024]{1,0:T(8,128)(2,1)} %copy-done.2, bf16[2048,256]{1,0:T(8,128)(2,1)} %all-reduce.3.kv_ref), custom_call_target="tpu_custom_call" | custom-call | flops 1200000000 | bytes 2000000 | tf_op jit(solution)/shard_map/attend/pallas_call | solution.py:88
  158.3 1.5 fusion.19
  161.7 3.9 %attend.5 = bf16[128,1024]{1,0:T(8,128)(2,1)} custom-call(s32[3]{0:T(128)} %pad_add_fusion.ids, s32[8]{0:T(128)} %lengths.9, s32[32]{0:T(128)} %order.9, bf16[1024,1024]{1,0:T(8,128)(2,1)} %copy-done.2, bf16[2048,256]{1,0:T(8,128)(2,1)} %all-reduce.3.kv_ref), custom_call_target="tpu_custom_call" | custom-call | flops 600000000 | bytes 1000000 | tf_op jit(solution)/shard_map/attend/pallas_call | solution.py:88
  165.6 3.1 %collective-permute-start.9 = (bf16[128,512]{1,0:T(8,128)(2,1)}, bf16[128,512]{1,0:T(8,128)(2,1)S(1)}, u32[]{:S(2)}, u32[]{:S(2)}) collective-permute-start(bf16[128,512]{1,0:T(8,128)(2,1)} %convolution_convert_fusion.1), channel_id=1, source_target_pairs={{0,1},{1,2},{2,3},{3,4},{4,5},{5,6},{6,7},{7,0},{8,9},{9,10},{10,1... | collective-permute-start | bytes 393224 | tf_op jit(solution)/shard_map/ppermute | solution.py:112
  168.7 7.6 %collective-permute-start.13 = (bf16[128,512]{1,0:T(8,128)(2,1)S(1)}, bf16[128,512]{1,0:T(8,128)(2,1)S(1)}, u32[]{:S(2)}, u32[]{:S(2)}) collective-permute-start(bf16[128,512]{1,0:T(8,128)(2,1)S(1)} %convolution_convert_fusion), channel_id=1, source_target_pairs={{0,7},{1,0},{2,1},{3,2},{4,3},{5,4},{6,5},{7,6},{8,15},{9,8},{10,9... | collective-permute-start | bytes 393224 | tf_op jit(solution)/shard_map/ppermute | solution.py:112
  178.9 1.9 collective-permute-start.10
  180.9 4.6 %collective-permute-start.14 = (bf16[128,1024]{1,0:T(8,128)(2,1)S(1)}, bf16[128,1024]{1,0:T(8,128)(2,1)S(1)}, u32[]{:S(2)}, u32[]{:S(2)}) collective-permute-start(bf16[128,1024]{1,0:T(8,128)(2,1)S(1)} %fusion.7), channel_id=1, source_target_pairs={{0,7},{1,0},{2,1},{3,2},{4,3},{5,4},{6,5},{7,6},{8,15},{9,8},{10,9... | collective-permute-start | bytes 786440 | tf_op jit(solution)/shard_map/ppermute | solution.py:112
  185.6 2.4 %collective-permute-done.10 = bf16[128,1024]{1,0:T(8,128)(2,1)S(1)} collective-permute-done((bf16[128,1024]{1,0:T(8,128)(2,1)S(1)}, bf16[128,1024]{1,0:T(8,128)(2,1)S(1)}, u32[]{:S(2)}, u32[]{:S(2)}) %collective-permute-start.10) | collective-permute-done | bytes 262176 | tf_op jit(solution)/shard_map/ppermute | solution.py:112
  188.0 1.9 collective-permute-start.11
  190.0 5.0 %collective-permute-start.15 = (bf16[128,1024]{1,0:T(8,128)(2,1)S(1)}, bf16[128,1024]{1,0:T(8,128)(2,1)S(1)}, u32[]{:S(2)}, u32[]{:S(2)}) collective-permute-start(bf16[128,1024]{1,0:T(8,128)(2,1)S(1)} %fusion.6), channel_id=1, source_target_pairs={{0,7},{1,0},{2,1},{3,2},{4,3},{5,4},{6,5},{7,6},{8,15},{9,8},{10,9... | collective-permute-start | bytes 786440 | tf_op jit(solution)/shard_map/ppermute | solution.py:112
  195.0 3.1 %collective-permute-done.11 = bf16[128,1024]{1,0:T(8,128)(2,1)S(1)} collective-permute-done((bf16[128,1024]{1,0:T(8,128)(2,1)S(1)}, bf16[128,1024]{1,0:T(8,128)(2,1)S(1)}, u32[]{:S(2)}, u32[]{:S(2)}) %collective-permute-start.11) | collective-permute-done | bytes 262176 | tf_op jit(solution)/shard_map/ppermute | solution.py:112
  198.2 1.9 collective-permute-start.12
  200.4 5.0 %collective-permute-start.16 = (bf16[128,1024]{1,0:T(8,128)(2,1)S(1)}, bf16[128,1024]{1,0:T(8,128)(2,1)S(1)}, u32[]{:S(2)}, u32[]{:S(2)}) collective-permute-start(bf16[128,1024]{1,0:T(8,128)(2,1)S(1)} %fusion.5), channel_id=1, source_target_pairs={{0,7},{1,0},{2,1},{3,2},{4,3},{5,4},{6,5},{7,6},{8,15},{9,8},{10,9... | collective-permute-start | bytes 786440 | tf_op jit(solution)/shard_map/ppermute | solution.py:112
  205.8 3.7 %collective-permute-done.12 = bf16[128,1024]{1,0:T(8,128)(2,1)S(1)} collective-permute-done((bf16[128,1024]{1,0:T(8,128)(2,1)S(1)}, bf16[128,1024]{1,0:T(8,128)(2,1)S(1)}, u32[]{:S(2)}, u32[]{:S(2)}) %collective-permute-start.12) | collective-permute-done | bytes 262176 | tf_op jit(solution)/shard_map/ppermute | solution.py:112
  209.5 1.7 collective-permute-done.16
  211.3 2.7 %collective-permute-start.17 = (bf16[128,512]{1,0:T(8,128)(2,1)S(1)}, bf16[128,512]{1,0:T(8,128)(2,1)S(1)}, u32[]{:S(2)}, u32[]{:S(2)}) collective-permute-start(bf16[128,512]{1,0:T(8,128)(2,1)S(1)} %get-tuple-element.24), channel_id=1, source_target_pairs={{0,8},{8,0},{1,9},{9,1},{2,10},{10,2},{3,11},{11,3},{4,12},{12,4},... | collective-permute-start | bytes 393224 | tf_op jit(solution)/shard_map/ppermute | solution.py:116
  (73 shorter events, 20.7 us)
Async XLA Ops:
  6.5 48.3 %copy-start = (bf16[512,256]{1,0:T(8,128)(2,1)S(1)}, bf16[512,256]{1,0:T(8,128)(2,1)}, u32[]{:S(2)}) copy-start(bf16[512,256]{1,0:T(8,128)(2,1)} %param.8) | copy-start | bytes 786436
  6.5 48.3 %all-gather.2.cloned.1.call-start = ((), (), s32[]{:S(2)}) async-start(), calls=%async_computation | async-start | bytes 2359296 | tf_op jit(solution)/shard_map/all_gather | solution.py:133
  7.3 9.7 %collective-permute-start.3 = (bf16[128,1024]{1,0:T(8,128)(2,1)}, bf16[128,1024]{1,0:T(8,128)(2,1)S(1)}, u32[]{:S(2)}, u32[]{:S(2)}) collective-permute-start(bf16[128,1024]{1,0:T(8,128)(2,1)} %param.7), channel_id=1, source_target_pairs={{0,16},{16,32},{32,48},{48,64},{64,80},{80,96},{96,112},{112,0},{1... | collective-permute-start | bytes 786440 | tf_op jit(solution)/shard_map/ppermute | solution.py:112
  11.7 10.5 %collective-permute-start = (bf16[128,1024]{1,0:T(8,128)(2,1)}, bf16[128,1024]{1,0:T(8,128)(2,1)}, u32[]{:S(2)}, u32[]{:S(2)}) collective-permute-start(bf16[128,1024]{1,0:T(8,128)(2,1)} %param.7), channel_id=1, source_target_pairs={{0,112},{16,0},{32,16},{48,32},{64,48},{80,64},{96,80},{112,96},{1... | collective-permute-start | bytes 786440 | tf_op jit(solution)/shard_map/ppermute | solution.py:112
  17.0 10.9 %copy-start.10 = (bf16[128,1024]{1,0:T(8,128)(2,1)}, bf16[128,1024]{1,0:T(8,128)(2,1)S(1)}, u32[]{:S(2)}) copy-start(bf16[128,1024]{1,0:T(8,128)(2,1)S(1)} %collective-permute-done.3) | copy-start | bytes 786436
  17.0 10.9 %collective-permute-start.4 = (bf16[128,1024]{1,0:T(8,128)(2,1)S(1)}, bf16[128,1024]{1,0:T(8,128)(2,1)}, u32[]{:S(2)}, u32[]{:S(2)}) collective-permute-start(bf16[128,1024]{1,0:T(8,128)(2,1)S(1)} %collective-permute-done.3), channel_id=1, source_target_pairs={{0,16},{16,32},{32,48},{48,64},{64,80},{80,96},{96,112},{112,0},{1... | collective-permute-start | bytes 786440 | tf_op jit(solution)/shard_map/ppermute | solution.py:112
  22.2 11.5 %collective-permute-start.1 = (bf16[128,1024]{1,0:T(8,128)(2,1)}, bf16[128,1024]{1,0:T(8,128)(2,1)}, u32[]{:S(2)}, u32[]{:S(2)}) collective-permute-start(bf16[128,1024]{1,0:T(8,128)(2,1)} %collective-permute-done), channel_id=1, source_target_pairs={{0,112},{16,0},{32,16},{48,32},{64,48},{80,64},{96,80},{112,96},{1... | collective-permute-start | bytes 786440 | tf_op jit(solution)/shard_map/ppermute | solution.py:112
  24.1 33.0 %collective-permute-start.8 = (bf16[1024,512]{1,0:T(8,128)(2,1)}, bf16[1024,512]{1,0:T(8,128)(2,1)S(1)}, u32[]{:S(2)}, u32[]{:S(2)}) collective-permute-start(bf16[1024,512]{1,0:T(8,128)(2,1)} %param.9), channel_id=1, source_target_pairs={{0,8},{8,0},{1,9},{9,1},{2,10},{10,2},{3,11},{11,3},{4,12},{12,4},... | collective-permute-start | bytes 3145736 | tf_op jit(solution)/shard_map/ppermute | solution.py:116
  27.9 9.6 %collective-permute-start.5 = (bf16[128,1024]{1,0:T(8,128)(2,1)}, bf16[128,1024]{1,0:T(8,128)(2,1)}, u32[]{:S(2)}, u32[]{:S(2)}) collective-permute-start(bf16[128,1024]{1,0:T(8,128)(2,1)} %collective-permute-done.4), channel_id=1, source_target_pairs={{0,16},{16,32},{32,48},{48,64},{64,80},{80,96},{96,112},{112,0},{1... | collective-permute-start | bytes 786440 | tf_op jit(solution)/shard_map/ppermute | solution.py:112
  33.7 19.7 %copy-start.11 = (bf16[128,1024]{1,0:T(8,128)(2,1)S(1)}, bf16[128,1024]{1,0:T(8,128)(2,1)}, u32[]{:S(2)}) copy-start(bf16[128,1024]{1,0:T(8,128)(2,1)} %copy-done.10) | copy-start | bytes 786436
  33.7 10.8 %collective-permute-start.2 = (bf16[128,1024]{1,0:T(8,128)(2,1)}, bf16[128,1024]{1,0:T(8,128)(2,1)S(1)}, u32[]{:S(2)}, u32[]{:S(2)}) collective-permute-start(bf16[128,1024]{1,0:T(8,128)(2,1)} %collective-permute-done.1), channel_id=1, source_target_pairs={{0,112},{16,0},{32,16},{48,32},{64,48},{80,64},{96,80},{112,96},{1... | collective-permute-start | bytes 786440 | tf_op jit(solution)/shard_map/ppermute | solution.py:112
  38.4 8.2 %collective-permute-start.6 = (bf16[64,1024]{1,0:T(8,128)(2,1)S(1)}, bf16[64,1024]{1,0:T(8,128)(2,1)S(1)}, u32[]{:S(2)}, u32[]{:S(2)}) collective-permute-start(bf16[64,1024]{1,0:T(8,128)(2,1)S(1)} %slice.72), channel_id=1, source_target_pairs={{0,16},{16,32},{32,48},{48,64},{64,80},{80,96},{96,112},{112,0},{1... | collective-permute-start | bytes 393224 | tf_op jit(solution)/shard_map/ppermute | solution.py:112
  44.6 6.9 %collective-permute-start.7 = (bf16[64,1024]{1,0:T(8,128)(2,1)S(1)}, bf16[64,1024]{1,0:T(8,128)(2,1)S(1)}, u32[]{:S(2)}, u32[]{:S(2)}) collective-permute-start(bf16[64,1024]{1,0:T(8,128)(2,1)S(1)} %slice.73), channel_id=1, source_target_pairs={{0,112},{16,0},{32,16},{48,32},{64,48},{80,64},{96,80},{112,96},{1... | collective-permute-start | bytes 393224 | tf_op jit(solution)/shard_map/ppermute | solution.py:112
  53.5 1.3 copy-start.2
  132.0 10.0 %copy-start.1 = (bf16[1024,512]{1,0:T(8,128)(2,1)S(1)}, bf16[1024,512]{1,0:T(8,128)(2,1)}, u32[]{:S(2)}) copy-start(bf16[1024,512]{1,0:T(8,128)(2,1)} %param.9) | copy-start | bytes 3145732
  132.0 10.0 %copy-start.8 = (bf16[256,1024]{1,0:T(8,128)(2,1)S(1)}, bf16[256,1024]{1,0:T(8,128)(2,1)}, u32[]{:S(2)}) copy-start(bf16[256,1024]{1,0:T(8,128)(2,1)} %attend.8) | copy-start | bytes 1572868
  142.0 2.5 %copy-start.7 = (bf16[256,1024]{1,0:T(8,128)(2,1)S(1)}, bf16[256,1024]{1,0:T(8,128)(2,1)}, u32[]{:S(2)}) copy-start(bf16[256,1024]{1,0:T(8,128)(2,1)} %attend.7) | copy-start | bytes 1572868
  158.3 1.6 copy-start.9
  158.3 2.0 copy-start.4
  165.6 13.2 %copy-start.5 = (f32[256,512]{1,0:T(8,128)S(1)}, f32[256,512]{1,0:T(8,128)}, u32[]{:S(2)}) copy-start(f32[256,512]{1,0:T(8,128)} %fusion.21) | copy-start | bytes 1572868
  165.6 13.2 %copy-start.6 = (f32[256,512]{1,0:T(8,128)S(1)}, f32[256,512]{1,0:T(8,128)}, u32[]{:S(2)}) copy-start(f32[256,512]{1,0:T(8,128)} %fusion.20) | copy-start | bytes 1572868
  165.6 13.3 %collective-permute-start.9 = (bf16[128,512]{1,0:T(8,128)(2,1)}, bf16[128,512]{1,0:T(8,128)(2,1)S(1)}, u32[]{:S(2)}, u32[]{:S(2)}) collective-permute-start(bf16[128,512]{1,0:T(8,128)(2,1)} %convolution_convert_fusion.1), channel_id=1, source_target_pairs={{0,1},{1,2},{2,3},{3,4},{4,5},{5,6},{6,7},{7,0},{8,9},{9,10},{10,1... | collective-permute-start | bytes 393224 | tf_op jit(solution)/shard_map/ppermute | solution.py:112
  168.7 12.2 %collective-permute-start.13 = (bf16[128,512]{1,0:T(8,128)(2,1)S(1)}, bf16[128,512]{1,0:T(8,128)(2,1)S(1)}, u32[]{:S(2)}, u32[]{:S(2)}) collective-permute-start(bf16[128,512]{1,0:T(8,128)(2,1)S(1)} %convolution_convert_fusion), channel_id=1, source_target_pairs={{0,7},{1,0},{2,1},{3,2},{4,3},{5,4},{6,5},{7,6},{8,15},{9,8},{10,9... | collective-permute-start | bytes 393224 | tf_op jit(solution)/shard_map/ppermute | solution.py:112
  178.9 9.0 %collective-permute-start.10 = (bf16[128,1024]{1,0:T(8,128)(2,1)S(1)}, bf16[128,1024]{1,0:T(8,128)(2,1)S(1)}, u32[]{:S(2)}, u32[]{:S(2)}) collective-permute-start(bf16[128,1024]{1,0:T(8,128)(2,1)S(1)} %fusion.4), channel_id=1, source_target_pairs={{0,1},{1,2},{2,3},{3,4},{4,5},{5,6},{6,7},{7,0},{8,9},{9,10},{10,1... | collective-permute-start | bytes 786440 | tf_op jit(solution)/shard_map/ppermute | solution.py:112
  180.9 9.0 %collective-permute-start.14 = (bf16[128,1024]{1,0:T(8,128)(2,1)S(1)}, bf16[128,1024]{1,0:T(8,128)(2,1)S(1)}, u32[]{:S(2)}, u32[]{:S(2)}) collective-permute-start(bf16[128,1024]{1,0:T(8,128)(2,1)S(1)} %fusion.7), channel_id=1, source_target_pairs={{0,7},{1,0},{2,1},{3,2},{4,3},{5,4},{6,5},{7,6},{8,15},{9,8},{10,9... | collective-permute-start | bytes 786440 | tf_op jit(solution)/shard_map/ppermute | solution.py:112
  188.0 10.1 %collective-permute-start.11 = (bf16[128,1024]{1,0:T(8,128)(2,1)S(1)}, bf16[128,1024]{1,0:T(8,128)(2,1)S(1)}, u32[]{:S(2)}, u32[]{:S(2)}) collective-permute-start(bf16[128,1024]{1,0:T(8,128)(2,1)S(1)} %fusion.3), channel_id=1, source_target_pairs={{0,1},{1,2},{2,3},{3,4},{4,5},{5,6},{6,7},{7,0},{8,9},{9,10},{10,1... | collective-permute-start | bytes 786440 | tf_op jit(solution)/shard_map/ppermute | solution.py:112
  189.9 15.5 %copy-start.3 = (bf16[128,1024]{1,0:T(8,128)(2,1)S(1)}, bf16[128,1024]{1,0:T(8,128)(2,1)}, u32[]{:S(2)}) copy-start(bf16[128,1024]{1,0:T(8,128)(2,1)} %attend.5) | copy-start | bytes 786436
  190.0 10.4 %collective-permute-start.15 = (bf16[128,1024]{1,0:T(8,128)(2,1)S(1)}, bf16[128,1024]{1,0:T(8,128)(2,1)S(1)}, u32[]{:S(2)}, u32[]{:S(2)}) collective-permute-start(bf16[128,1024]{1,0:T(8,128)(2,1)S(1)} %fusion.6), channel_id=1, source_target_pairs={{0,7},{1,0},{2,1},{3,2},{4,3},{5,4},{6,5},{7,6},{8,15},{9,8},{10,9... | collective-permute-start | bytes 786440 | tf_op jit(solution)/shard_map/ppermute | solution.py:112
  198.2 11.3 %collective-permute-start.12 = (bf16[128,1024]{1,0:T(8,128)(2,1)S(1)}, bf16[128,1024]{1,0:T(8,128)(2,1)S(1)}, u32[]{:S(2)}, u32[]{:S(2)}) collective-permute-start(bf16[128,1024]{1,0:T(8,128)(2,1)S(1)} %fusion.2), channel_id=1, source_target_pairs={{0,1},{1,2},{2,3},{3,4},{4,5},{5,6},{6,7},{7,0},{8,9},{9,10},{10,1... | collective-permute-start | bytes 786440 | tf_op jit(solution)/shard_map/ppermute | solution.py:112
  200.4 10.7 %collective-permute-start.16 = (bf16[128,1024]{1,0:T(8,128)(2,1)S(1)}, bf16[128,1024]{1,0:T(8,128)(2,1)S(1)}, u32[]{:S(2)}, u32[]{:S(2)}) collective-permute-start(bf16[128,1024]{1,0:T(8,128)(2,1)S(1)} %fusion.5), channel_id=1, source_target_pairs={{0,7},{1,0},{2,1},{3,2},{4,3},{5,4},{6,5},{7,6},{8,15},{9,8},{10,9... | collective-permute-start | bytes 786440 | tf_op jit(solution)/shard_map/ppermute | solution.py:112
  211.3 3.7 %collective-permute-start.17 = (bf16[128,512]{1,0:T(8,128)(2,1)S(1)}, bf16[128,512]{1,0:T(8,128)(2,1)S(1)}, u32[]{:S(2)}, u32[]{:S(2)}) collective-permute-start(bf16[128,512]{1,0:T(8,128)(2,1)S(1)} %get-tuple-element.24), channel_id=1, source_target_pairs={{0,8},{8,0},{1,9},{9,1},{2,10},{10,2},{3,11},{11,3},{4,12},{12,4},... | collective-permute-start | bytes 393224 | tf_op jit(solution)/shard_map/ppermute | solution.py:116
Sparse Core Ops, SparseCore 0:
  9.4 44.1 all-gather.1

commit v5 on v4

v5 whole, which is shorter than its diff:
```python
import functools
import math

import jax
import jax.numpy as jnp
from jax import lax
from jax.experimental import pallas as pl
from jax.experimental.pallas import tpu as pltpu
from jax.sharding import Mesh, PartitionSpec as P


HEAD = 128
RING = 8
BLOCK = 64
KEYS = 256
NEG = -1e30
EXP_SCALE = math.log2(math.e) / math.sqrt(HEAD)


def attend_kernel(base, ids, lengths, order, q_ref, kv_ref, out_ref, acc_ref):
    z, core = ids[0], ids[1]
    owner = (z + base) % RING
    first = order[(owner * 2 + core) * 2 + pl.program_id(0)] * BLOCK
    heads = q_ref.shape[1] // HEAD
    rows = BLOCK * heads

    row_pos = first + lax.broadcasted_iota(jnp.int32, (1, HEAD), 1) % BLOCK
    row_start = jnp.zeros((1, HEAD), jnp.int32)
    lowest = jnp.int32(0)
    end = jnp.int32(0)
    for j in range(lengths.shape[0]):
        end = end + lengths[j]
        row_start = jnp.where(row_pos >= end, end, row_start)
        lowest = jnp.where(first >= end, end, lowest)
    key_row = lax.broadcasted_iota(jnp.int32, (KEYS, HEAD), 0)

    query = jnp.concatenate(
        [q_ref[:, h * HEAD : (h + 1) * HEAD] for h in range(heads)], axis=0
    )
    acc_ref[...] = jnp.zeros_like(acc_ref)
    last = first // KEYS

    def visit(i, carry):
        top, total = carry
        block = last - i
        offset = pl.multiple_of(block * KEYS, KEYS)
        keys = kv_ref[pl.ds(offset, KEYS), :HEAD]
        values = kv_ref[pl.ds(offset, KEYS), HEAD:]
        scores = lax.dot_general(
            keys, query, (((1,), (1,)), ((), ())), preferred_element_type=jnp.float32
        )
        key_pos = block * KEYS + key_row
        bias = jnp.where(
            (key_pos >= row_start) & (key_pos <= row_pos), jnp.float32(0.0), jnp.float32(NEG)
        )
        scores = scores + jnp.concatenate([bias] * (rows // HEAD), axis=1)
        new = jnp.maximum(top, jnp.max(scores, axis=0, keepdims=True))
        keep = jnp.exp2((top - new) * EXP_SCALE)
        probs = jnp.exp2((scores - new) * EXP_SCALE)
        total = total * keep + jnp.sum(probs, axis=0, keepdims=True)
        acc_ref[...] = acc_ref[...] * keep + lax.dot_general(
            values,
            probs.astype(jnp.bfloat16),
            (((0,), (0,)), ((), ())),
            preferred_element_type=jnp.float32,
        )
        return new, total

    start = (jnp.full((1, rows), NEG, jnp.float32), jnp.zeros((1, rows), jnp.float32))
    _, total = lax.fori_loop(0, last - lowest // KEYS + 1, visit, start)
    scale = 1.0 / total
    for pair in range(heads // 2):
        lanes = slice(pair * HEAD, (pair + 1) * HEAD)
        turned = (acc_ref[:, lanes] * scale[:, lanes]).T.astype(out_ref.dtype)
        out_ref[:, 2 * pair * HEAD : (2 * pair + 1) * HEAD] = turned[:BLOCK]
        out_ref[:, (2 * pair + 1) * HEAD : (2 * pair + 2) * HEAD] = turned[BLOCK:]


def attend(base, ids, lengths, order, queries, kv):
    width = queries.shape[1]

    def q_map(i, ids, lengths, order):
        return ((ids[0] + base - ids[2] + RING) % RING * 2 + i, 0)

    return pl.pallas_call(
        functools.partial(attend_kernel, base),
        out_shape=jax.ShapeDtypeStruct((2 * BLOCK, width), jnp.bfloat16),
        grid_spec=pltpu.PrefetchScalarGridSpec(
            num_scalar_prefetch=3,
            grid=(2,),
            in_specs=[
                pl.BlockSpec((BLOCK, width), q_map),
                pl.BlockSpec(kv.shape, lambda i, *_: (0, 0)),
            ],
            out_specs=pl.BlockSpec((BLOCK, width), lambda i, *_: (i, 0)),
            scratch_shapes=[pltpu.VMEM((HEAD, BLOCK * (width // HEAD)), jnp.float32)],
        ),
        cost_estimate=pl.CostEstimate(
            flops=600_000_000, bytes_accessed=2_000_000, transcendentals=500_000
        ),
        name="attend",
    )(ids, lengths, order, queries, kv)


def shift(x, axis, by):
    return lax.ppermute(x, axis, [(i, (i + by) % RING) for i in range(RING)])


def swap(x):
    return lax.ppermute(x, "core", [(0, 1), (1, 0)])


def ring_gather(x, axis):
    ups, downs = [x], [x]
    for _ in range(3):
        ups.append(shift(ups[-1], axis, -1))
        downs.append(shift(downs[-1], axis, 1))
    far = shift(x, axis, RING // 2)
    return jnp.concatenate([*ups, far, *downs[:0:-1]], axis=0)


def local(tokens, queries, key_value_weight, out_weight, doc_lengths, block_order):
    z, y, core = lax.axis_index("z"), lax.axis_index("y"), lax.axis_index("core")
    ids = jnp.stack([z, core, y]).astype(jnp.int32)
    all_tokens = lax.all_gather(tokens, "z", axis=0, tiled=True)
    all_queries = ring_gather(queries, "y")
    other_weight = swap(out_weight)
    partial_kv = jnp.dot(all_tokens, key_value_weight, preferred_element_type=jnp.float32)
    partial_kv, all_queries, other_weight = lax.optimization_barrier(
        (partial_kv, all_queries, other_weight)
    )
    kv = lax.psum(partial_kv, ("y", "core")).astype(jnp.bfloat16)

    f32, bf16 = jnp.float32, jnp.bfloat16
    rows, width = queries.shape[0], out_weight.shape[1]

    def product(base):
        attn = attend(base, ids, doc_lengths, block_order, all_queries, kv)
        return jnp.concatenate(
            [jnp.dot(attn, w, preferred_element_type=f32) for w in (out_weight, other_weight)],
            axis=1,
        )

    far = product(4).astype(bf16)
    zero = jnp.zeros((rows, width), bf16)
    up = jnp.concatenate([shift(far[:, :width], "z", 1), zero], axis=1)
    down = jnp.concatenate([zero, shift(far[:, width:], "z", -1)], axis=1)
    for step in (3, 2, 1):
        up = shift((product(step) + up.astype(f32)).astype(bf16), "z", 1)
        down = shift((product(RING - step) + down.astype(f32)).astype(bf16), "z", -1)
    total = (product(0) + up.astype(f32) + down.astype(f32)).astype(bf16)
    mine, theirs = total[:, :width], swap(total[:, width:])
    return jnp.where(
        core == 0,
        jnp.concatenate([mine, theirs], axis=0),
        jnp.concatenate([theirs, mine], axis=0),
    )


def solution(mesh):
    fine = Mesh(mesh.devices.reshape(4, 8, 2, 8), ("dp", "y", "core", "z"))
    ctx = ("y", "core")
    in_specs = (
        P(("dp", "z"), ctx),
        P(("dp", "y", "core"), "z"),
        P(ctx, "z"),
        P("z", ctx),
        P("dp"),
        P("dp"),
    )
    return jax.shard_map(
        local, mesh=fine, in_specs=in_specs, out_specs=P(("dp", "z"), ctx), check_vma=False
    )
```

time: 224 us -> 244 us (1.089)
  the two profiles are of different devices: /device:TPU:31 before, /device:TPU:7 now
where the time goes in v5:
time: 244 us; the launch traced here: 242 us
  starting transfers between devices  69 us (28%)
  blocking collectives  57.9 us (24%)
  Pallas kernels  45.8 us (19%)
  matrix products  22.4 us (9%)
  waiting for transfers between devices  21.9 us (9%)
  between operations  13.8 us (6%)
  local copies, waits for them, and re-layouts  6.26 us (3%)
  other arithmetic  5.16 us (2%)
    psum x1, blocking collectives, local(): kv = lax.psum(partial_kv, ('y', 'core')).astype(jnp.bfloat16)  57.9 us
    ppermute x15, starting transfers between devices, shift(): return lax.ppermute(x, axis, [(i, (i + by) % RING) for i in range(RING)])  56.4 us
    pallas_call x8, Pallas kernels, attend(): pl.pallas_call(functools.partial(attend_kernel, base), out_shape=jax.Shap...  45.8 us
    ppermute x15, waiting for transfers between devices, shift(): return lax.ppermute(x, axis, [(i, (i + by) % RING) for i in range(RING)])  20.2 us
    dot_general x16, matrix products, product(): jnp.dot(attn, w, preferred_element_type=f32)  18 us
    ppermute x2, starting transfers between devices, swap(): return lax.ppermute(x, 'core', [(0, 1), (1, 0)])  12.5 us
    unnamed x39, local copies, waits for them, and re-layouts  5.27 us
  transfers between devices with their start and end apart: 18, of which 8 were waited for; matrix products, arithmetic and copies ran while one was open for 7% of the time, Pallas kernels for 2%

profile of v5, /device:TPU:7, one launch (start us, length us, event | category | flops | bytes accessed | tf_op | source)
XLA Modules:
  0.0 242.3 jit_solution(14921005850810641510)
XLA Ops:
  7.3 5.1 %collective-permute-start = (bf16[128,1024]{1,0:T(8,128)(2,1)}, bf16[128,1024]{1,0:T(8,128)(2,1)}, u32[]{:S(2)}, u32[]{:S(2)}) collective-permute-start(bf16[128,1024]{1,0:T(8,128)(2,1)} %param.7), channel_id=1, source_target_pairs={{0,112},{16,0},{32,16},{48,32},{64,48},{80,64},{96,80},{112,96},{1... | collective-permute-start | bytes 786440 | tf_op jit(solution)/shard_map/ppermute | solution.py:106
  14.3 3.4 %collective-permute-done = bf16[128,1024]{1,0:T(8,128)(2,1)} collective-permute-done((bf16[128,1024]{1,0:T(8,128)(2,1)}, bf16[128,1024]{1,0:T(8,128)(2,1)}, u32[]{:S(2)}, u32[]{:S(2)}) %collective-permute-start) | collective-permute-done | bytes 262176 | tf_op jit(solution)/shard_map/ppermute | solution.py:106
  17.6 5.3 %collective-permute-start.1 = (bf16[128,1024]{1,0:T(8,128)(2,1)}, bf16[128,1024]{1,0:T(8,128)(2,1)}, u32[]{:S(2)}, u32[]{:S(2)}) collective-permute-start(bf16[128,1024]{1,0:T(8,128)(2,1)} %collective-permute-done), channel_id=1, source_target_pairs={{0,112},{16,0},{32,16},{48,32},{64,48},{80,64},{96,80},{112,96},{1... | collective-permute-start | bytes 786440 | tf_op jit(solution)/shard_map/ppermute | solution.py:106
  23.0 4.4 %collective-permute-start.3 = (bf16[128,1024]{1,0:T(8,128)(2,1)}, bf16[128,1024]{1,0:T(8,128)(2,1)}, u32[]{:S(2)}, u32[]{:S(2)}) collective-permute-start(bf16[128,1024]{1,0:T(8,128)(2,1)} %param.7), channel_id=1, source_target_pairs={{0,64},{16,80},{32,96},{48,112},{64,0},{80,16},{96,32},{112,48},{1... | collective-permute-start | bytes 786440 | tf_op jit(solution)/shard_map/ppermute | solution.py:106
  27.4 4.0 %collective-permute-start.7 = (bf16[1024,512]{1,0:T(8,128)(2,1)}, bf16[1024,512]{1,0:T(8,128)(2,1)S(1)}, u32[]{:S(2)}, u32[]{:S(2)}) collective-permute-start(bf16[1024,512]{1,0:T(8,128)(2,1)} %param.9), channel_id=1, source_target_pairs={{0,8},{8,0},{1,9},{9,1},{2,10},{10,2},{3,11},{11,3},{4,12},{12,4},... | collective-permute-start | bytes 3145736 | tf_op jit(solution)/shard_map/ppermute | solution.py:110
  31.4 2.0 collective-permute-start.5
  34.4 4.5 %collective-permute-start.2 = (bf16[128,1024]{1,0:T(8,128)(2,1)}, bf16[128,1024]{1,0:T(8,128)(2,1)S(1)}, u32[]{:S(2)}, u32[]{:S(2)}) collective-permute-start(bf16[128,1024]{1,0:T(8,128)(2,1)} %collective-permute-done.1), channel_id=1, source_target_pairs={{0,112},{16,0},{32,16},{48,32},{64,48},{80,64},{96,80},{112,96},{1... | collective-permute-start | bytes 786440 | tf_op jit(solution)/shard_map/ppermute | solution.py:106
  40.5 7.0 %collective-permute-done.5 = bf16[128,1024]{1,0:T(8,128)(2,1)} collective-permute-done((bf16[128,1024]{1,0:T(8,128)(2,1)}, bf16[128,1024]{1,0:T(8,128)(2,1)}, u32[]{:S(2)}, u32[]{:S(2)}) %collective-permute-start.5) | collective-permute-done | bytes 262176 | tf_op jit(solution)/shard_map/ppermute | solution.py:106
  51.4 5.9 %collective-permute-done.6 = bf16[128,1024]{1,0:T(8,128)(2,1)S(1)} collective-permute-done((bf16[128,1024]{1,0:T(8,128)(2,1)}, bf16[128,1024]{1,0:T(8,128)(2,1)S(1)}, u32[]{:S(2)}, u32[]{:S(2)}) %collective-permute-start.6) | collective-permute-done | bytes 262176 | tf_op jit(solution)/shard_map/ppermute | solution.py:106
  59.3 4.4 %fusion.9 = f32[2048,256]{1,0:T(8,128)} fusion(bf16[2048,512]{1,0:T(8,128)(2,1)} %all-gather.2.cloned.1.call-done, bf16[512,256]{1,0:T(8,128)(2,1)S(1)} %copy-done), kind=kOutput, calls=%fused_computation.28 | convolution fusion | flops 536870912 | bytes 4456448 | tf_op jit(solution)/shard_map/dot_general | solution.py:128
  63.7 57.9 %all-reduce.3.kv_ref = bf16[2048,256]{1,0:T(8,128)(2,1)} all-reduce(f32[2048,256]{1,0:T(8,128)} %fusion.9), channel_id=1, replica_groups=mesh['dp'=4,'y'=8,'core'=2,'z'=8] {'y','core'}, use_global_device_ids=true, to_apply=%region_0.0 | all-reduce | flops 524288 | bytes 3145728 | tf_op jit(solution)/shard_map/psum | solution.py:132
  121.6 4.5 %attend.11 = bf16[128,1024]{1,0:T(8,128)(2,1)} custom-call(s32[3]{0:T(128)} %pad_add_fusion.ids, s32[8]{0:T(128)} %lengths.15, s32[32]{0:T(128)} %order.15, bf16[1024,1024]{1,0:T(8,128)(2,1)} %copy-done.1, bf16[2048,256]{1,0:T(8,128)(2,1)} %all-reduce.3.kv_ref), custom_call_target="tpu_custom_call" | custom-call | flops 600000000 | bytes 2000000 | tf_op jit(solution)/shard_map/attend/pallas_call | solution.py:85
  126.1 5.5 %attend.12 = bf16[128,1024]{1,0:T(8,128)(2,1)} custom-call(s32[3]{0:T(128)} %pad_add_fusion.ids, s32[8]{0:T(128)} %lengths.15, s32[32]{0:T(128)} %order.15, bf16[1024,1024]{1,0:T(8,128)(2,1)} %copy-done.1, bf16[2048,256]{1,0:T(8,128)(2,1)} %all-reduce.3.kv_ref), custom_call_target="tpu_custom_call" | custom-call | flops 600000000 | bytes 2000000 | tf_op jit(solution)/shard_map/attend/pallas_call | solution.py:85
  131.6 6.6 %attend.10 = bf16[128,1024]{1,0:T(8,128)(2,1)} custom-call(s32[3]{0:T(128)} %pad_add_fusion.ids, s32[8]{0:T(128)} %lengths.15, s32[32]{0:T(128)} %order.15, bf16[1024,1024]{1,0:T(8,128)(2,1)} %copy-done.1, bf16[2048,256]{1,0:T(8,128)(2,1)} %all-reduce.3.kv_ref), custom_call_target="tpu_custom_call" | custom-call | flops 600000000 | bytes 2000000 | tf_op jit(solution)/shard_map/attend/pallas_call | solution.py:85
  141.2 5.9 %attend.9 = bf16[128,1024]{1,0:T(8,128)(2,1)} custom-call(s32[3]{0:T(128)} %pad_add_fusion.ids, s32[8]{0:T(128)} %lengths.15, s32[32]{0:T(128)} %order.15, bf16[1024,1024]{1,0:T(8,128)(2,1)} %copy-done.1, bf16[2048,256]{1,0:T(8,128)(2,1)} %all-reduce.3.kv_ref), custom_call_target="tpu_custom_call" | custom-call | flops 600000000 | bytes 2000000 | tf_op jit(solution)/shard_map/attend/pallas_call | solution.py:85
  147.1 2.0 fusion.13
  149.1 2.0 fusion.12
  152.4 5.5 %attend.15 = bf16[128,1024]{1,0:T(8,128)(2,1)} custom-call(s32[3]{0:T(128)} %pad_add_fusion.ids, s32[8]{0:T(128)} %lengths.15, s32[32]{0:T(128)} %order.15, bf16[1024,1024]{1,0:T(8,128)(2,1)} %copy-done.1, bf16[2048,256]{1,0:T(8,128)(2,1)} %all-reduce.3.kv_ref), custom_call_target="tpu_custom_call" | custom-call | flops 600000000 | bytes 2000000 | tf_op jit(solution)/shard_map/attend/pallas_call | solution.py:85
  160.4 6.0 %attend.14 = bf16[128,1024]{1,0:T(8,128)(2,1)} custom-call(s32[3]{0:T(128)} %pad_add_fusion.ids, s32[8]{0:T(128)} %lengths.15, s32[32]{0:T(128)} %order.15, bf16[1024,1024]{1,0:T(8,128)(2,1)} %copy-done.1, bf16[2048,256]{1,0:T(8,128)(2,1)} %all-reduce.3.kv_ref), custom_call_target="tpu_custom_call" | custom-call | flops 600000000 | bytes 2000000 | tf_op jit(solution)/shard_map/attend/pallas_call | solution.py:85
  166.4 2.0 fusion.21
  168.3 2.0 fusion.20
  170.3 7.9 %attend.13 = bf16[128,1024]{1,0:T(8,128)(2,1)} custom-call(s32[3]{0:T(128)} %pad_add_fusion.ids, s32[8]{0:T(128)} %lengths.15, s32[32]{0:T(128)} %order.15, bf16[1024,1024]{1,0:T(8,128)(2,1)} %copy-done.1, bf16[2048,256]{1,0:T(8,128)(2,1)} %all-reduce.3.kv_ref), custom_call_target="tpu_custom_call" | custom-call | flops 600000000 | bytes 2000000 | tf_op jit(solution)/shard_map/attend/pallas_call | solution.py:85
  178.3 2.1 collective-permute-start.8
  180.4 6.6 %collective-permute-start.12 = (bf16[128,512]{1,0:T(8,128)(2,1)S(1)}, bf16[128,512]{1,0:T(8,128)(2,1)S(1)}, u32[]{:S(2)}, u32[]{:S(2)}) collective-permute-start(bf16[128,512]{1,0:T(8,128)(2,1)S(1)} %convolution_convert_fusion), channel_id=1, source_target_pairs={{0,7},{1,0},{2,1},{3,2},{4,3},{5,4},{6,5},{7,6},{8,15},{9,8},{10,9... | collective-permute-start | bytes 393224 | tf_op jit(solution)/shard_map/ppermute | solution.py:106
  187.0 2.0 fusion.19
  193.5 4.7 %collective-permute-start.13 = (bf16[128,1024]{1,0:T(8,128)(2,1)}, bf16[128,1024]{1,0:T(8,128)(2,1)}, u32[]{:S(2)}, u32[]{:S(2)}) collective-permute-start(bf16[128,1024]{1,0:T(8,128)(2,1)} %fusion.7), channel_id=1, source_target_pairs={{0,7},{1,0},{2,1},{3,2},{4,3},{5,4},{6,5},{7,6},{8,15},{9,8},{10,9... | collective-permute-start | bytes 786440 | tf_op jit(solution)/shard_map/ppermute | solution.py:106
  198.2 4.0 %attend.8 = bf16[128,1024]{1,0:T(8,128)(2,1)} custom-call(s32[3]{0:T(128)} %pad_add_fusion.ids, s32[8]{0:T(128)} %lengths.15, s32[32]{0:T(128)} %order.15, bf16[1024,1024]{1,0:T(8,128)(2,1)} %copy-done.1, bf16[2048,256]{1,0:T(8,128)(2,1)} %all-reduce.3.kv_ref), custom_call_target="tpu_custom_call" | custom-call | flops 600000000 | bytes 2000000 | tf_op jit(solution)/shard_map/attend/pallas_call | solution.py:85
  203.3 2.8 %collective-permute-start.10 = (bf16[128,1024]{1,0:T(8,128)(2,1)S(1)}, bf16[128,1024]{1,0:T(8,128)(2,1)S(1)}, u32[]{:S(2)}, u32[]{:S(2)}) collective-permute-start(bf16[128,1024]{1,0:T(8,128)(2,1)S(1)} %fusion.3), channel_id=1, source_target_pairs={{0,1},{1,2},{2,3},{3,4},{4,5},{5,6},{6,7},{7,0},{8,9},{9,10},{10,1... | collective-permute-start | bytes 786440 | tf_op jit(solution)/shard_map/ppermute | solution.py:106
  207.2 6.2 %collective-permute-start.14 = (bf16[128,1024]{1,0:T(8,128)(2,1)S(1)}, bf16[128,1024]{1,0:T(8,128)(2,1)S(1)}, u32[]{:S(2)}, u32[]{:S(2)}) collective-permute-start(bf16[128,1024]{1,0:T(8,128)(2,1)S(1)} %fusion.6), channel_id=1, source_target_pairs={{0,7},{1,0},{2,1},{3,2},{4,3},{5,4},{6,5},{7,6},{8,15},{9,8},{10,9... | collective-permute-start | bytes 786440 | tf_op jit(solution)/shard_map/ppermute | solution.py:106
  216.7 5.0 %collective-permute-start.15 = (bf16[128,1024]{1,0:T(8,128)(2,1)S(1)}, bf16[128,1024]{1,0:T(8,128)(2,1)S(1)}, u32[]{:S(2)}, u32[]{:S(2)}) collective-permute-start(bf16[128,1024]{1,0:T(8,128)(2,1)S(1)} %fusion.5), channel_id=1, source_target_pairs={{0,7},{1,0},{2,1},{3,2},{4,3},{5,4},{6,5},{7,6},{8,15},{9,8},{10,9... | collective-permute-start | bytes 786440 | tf_op jit(solution)/shard_map/ppermute | solution.py:106
  222.5 2.5 %collective-permute-done.15 = bf16[128,1024]{1,0:T(8,128)(2,1)S(1)} collective-permute-done((bf16[128,1024]{1,0:T(8,128)(2,1)S(1)}, bf16[128,1024]{1,0:T(8,128)(2,1)S(1)}, u32[]{:S(2)}, u32[]{:S(2)}) %collective-permute-start.15) | collective-permute-done | bytes 262176 | tf_op jit(solution)/shard_map/ppermute | solution.py:106
  225.2 8.5 %collective-permute-start.16 = (bf16[128,512]{1,0:T(8,128)(2,1)S(1)}, bf16[128,512]{1,0:T(8,128)(2,1)S(1)}, u32[]{:S(2)}, u32[]{:S(2)}) collective-permute-start(bf16[128,512]{1,0:T(8,128)(2,1)S(1)} %get-tuple-element.12), channel_id=1, source_target_pairs={{0,8},{8,0},{1,9},{9,1},{2,10},{10,2},{3,11},{11,3},{4,12},{12,4},... | collective-permute-start | bytes 393224 | tf_op jit(solution)/shard_map/ppermute | solution.py:110
  (81 shorter events, 30.3 us)
Async XLA Ops:
  6.5 52.8 %copy-start = (bf16[512,256]{1,0:T(8,128)(2,1)S(1)}, bf16[512,256]{1,0:T(8,128)(2,1)}, u32[]{:S(2)}) copy-start(bf16[512,256]{1,0:T(8,128)(2,1)} %param.8) | copy-start | bytes 786436
  6.5 52.8 %all-gather.2.cloned.1.call-start = ((), (), s32[]{:S(2)}) async-start(), calls=%async_computation | async-start | bytes 2359296 | tf_op jit(solution)/shard_map/all_gather | solution.py:125
  7.3 10.4 %collective-permute-start = (bf16[128,1024]{1,0:T(8,128)(2,1)}, bf16[128,1024]{1,0:T(8,128)(2,1)}, u32[]{:S(2)}, u32[]{:S(2)}) collective-permute-start(bf16[128,1024]{1,0:T(8,128)(2,1)} %param.7), channel_id=1, source_target_pairs={{0,112},{16,0},{32,16},{48,32},{64,48},{80,64},{96,80},{112,96},{1... | collective-permute-start | bytes 786440 | tf_op jit(solution)/shard_map/ppermute | solution.py:106
  12.4 19.1 %collective-permute-start.4 = (bf16[128,1024]{1,0:T(8,128)(2,1)}, bf16[128,1024]{1,0:T(8,128)(2,1)}, u32[]{:S(2)}, u32[]{:S(2)}) collective-permute-start(bf16[128,1024]{1,0:T(8,128)(2,1)} %param.7), channel_id=1, source_target_pairs={{0,16},{16,32},{32,48},{48,64},{64,80},{80,96},{96,112},{112,0},{1... | collective-permute-start | bytes 786440 | tf_op jit(solution)/shard_map/ppermute | solution.py:106
  17.6 16.8 %collective-permute-start.1 = (bf16[128,1024]{1,0:T(8,128)(2,1)}, bf16[128,1024]{1,0:T(8,128)(2,1)}, u32[]{:S(2)}, u32[]{:S(2)}) collective-permute-start(bf16[128,1024]{1,0:T(8,128)(2,1)} %collective-permute-done), channel_id=1, source_target_pairs={{0,112},{16,0},{32,16},{48,32},{64,48},{80,64},{96,80},{112,96},{1... | collective-permute-start | bytes 786440 | tf_op jit(solution)/shard_map/ppermute | solution.py:106
  23.0 27.4 %collective-permute-start.3 = (bf16[128,1024]{1,0:T(8,128)(2,1)}, bf16[128,1024]{1,0:T(8,128)(2,1)}, u32[]{:S(2)}, u32[]{:S(2)}) collective-permute-start(bf16[128,1024]{1,0:T(8,128)(2,1)} %param.7), channel_id=1, source_target_pairs={{0,64},{16,80},{32,96},{48,112},{64,0},{80,16},{96,32},{112,48},{1... | collective-permute-start | bytes 786440 | tf_op jit(solution)/shard_map/ppermute | solution.py:106
  27.4 36.3 %collective-permute-start.7 = (bf16[1024,512]{1,0:T(8,128)(2,1)}, bf16[1024,512]{1,0:T(8,128)(2,1)S(1)}, u32[]{:S(2)}, u32[]{:S(2)}) collective-permute-start(bf16[1024,512]{1,0:T(8,128)(2,1)} %param.9), channel_id=1, source_target_pairs={{0,8},{8,0},{1,9},{9,1},{2,10},{10,2},{3,11},{11,3},{4,12},{12,4},... | collective-permute-start | bytes 3145736 | tf_op jit(solution)/shard_map/ppermute | solution.py:110
  31.4 16.0 %collective-permute-start.5 = (bf16[128,1024]{1,0:T(8,128)(2,1)}, bf16[128,1024]{1,0:T(8,128)(2,1)}, u32[]{:S(2)}, u32[]{:S(2)}) collective-permute-start(bf16[128,1024]{1,0:T(8,128)(2,1)} %collective-permute-done.4), channel_id=1, source_target_pairs={{0,16},{16,32},{32,48},{48,64},{64,80},{80,96},{96,112},{112,0},{1... | collective-permute-start | bytes 786440 | tf_op jit(solution)/shard_map/ppermute | solution.py:106
  34.4 15.9 %collective-permute-start.2 = (bf16[128,1024]{1,0:T(8,128)(2,1)}, bf16[128,1024]{1,0:T(8,128)(2,1)S(1)}, u32[]{:S(2)}, u32[]{:S(2)}) collective-permute-start(bf16[128,1024]{1,0:T(8,128)(2,1)} %collective-permute-done.1), channel_id=1, source_target_pairs={{0,112},{16,0},{32,16},{48,32},{64,48},{80,64},{96,80},{112,96},{1... | collective-permute-start | bytes 786440 | tf_op jit(solution)/shard_map/ppermute | solution.py:106
  47.5 9.8 %collective-permute-start.6 = (bf16[128,1024]{1,0:T(8,128)(2,1)}, bf16[128,1024]{1,0:T(8,128)(2,1)S(1)}, u32[]{:S(2)}, u32[]{:S(2)}) collective-permute-start(bf16[128,1024]{1,0:T(8,128)(2,1)} %collective-permute-done.5), channel_id=1, source_target_pairs={{0,16},{16,32},{32,48},{48,64},{64,80},{80,96},{96,112},{112,0},{1... | collective-permute-start | bytes 786440 | tf_op jit(solution)/shard_map/ppermute | solution.py:106
  59.3 4.5 %copy-start.1 = (bf16[1024,1024]{1,0:T(8,128)(2,1)}, bf16[1024,1024]{1,0:T(8,128)(2,1)S(1)}, u32[]{:S(2)}) copy-start(bf16[1024,1024]{1,0:T(8,128)(2,1)S(1)} %constant_dynamic-update-slice_fusion.q_ref) | copy-start | bytes 6291460
  131.6 6.6 %copy-start.2 = (bf16[1024,512]{1,0:T(8,128)(2,1)S(1)}, bf16[1024,512]{1,0:T(8,128)(2,1)}, u32[]{:S(2)}) copy-start(bf16[1024,512]{1,0:T(8,128)(2,1)} %param.9) | copy-start | bytes 3145732
  131.6 6.6 %copy-start.7 = (bf16[128,1024]{1,0:T(8,128)(2,1)S(1)}, bf16[128,1024]{1,0:T(8,128)(2,1)}, u32[]{:S(2)}) copy-start(bf16[128,1024]{1,0:T(8,128)(2,1)} %attend.11) | copy-start | bytes 786436
  178.3 13.4 %copy-start.4 = (bf16[128,1024]{1,0:T(8,128)(2,1)S(1)}, bf16[128,1024]{1,0:T(8,128)(2,1)}, u32[]{:S(2)}) copy-start(bf16[128,1024]{1,0:T(8,128)(2,1)} %attend.13) | copy-start | bytes 786436
  178.3 10.7 %collective-permute-start.8 = (bf16[128,512]{1,0:T(8,128)(2,1)}, bf16[128,512]{1,0:T(8,128)(2,1)S(1)}, u32[]{:S(2)}, u32[]{:S(2)}) collective-permute-start(bf16[128,512]{1,0:T(8,128)(2,1)} %convolution_convert_fusion.1), channel_id=1, source_target_pairs={{0,1},{1,2},{2,3},{3,4},{4,5},{5,6},{6,7},{7,0},{8,9},{9,10},{10,1... | collective-permute-start | bytes 393224 | tf_op jit(solution)/shard_map/ppermute | solution.py:106
  180.4 12.3 %collective-permute-start.12 = (bf16[128,512]{1,0:T(8,128)(2,1)S(1)}, bf16[128,512]{1,0:T(8,128)(2,1)S(1)}, u32[]{:S(2)}, u32[]{:S(2)}) collective-permute-start(bf16[128,512]{1,0:T(8,128)(2,1)S(1)} %convolution_convert_fusion), channel_id=1, source_target_pairs={{0,7},{1,0},{2,1},{3,2},{4,3},{5,4},{6,5},{7,6},{8,15},{9,8},{10,9... | collective-permute-start | bytes 393224 | tf_op jit(solution)/shard_map/ppermute | solution.py:106
  189.7 12.4 %collective-permute-start.9 = (bf16[128,1024]{1,0:T(8,128)(2,1)}, bf16[128,1024]{1,0:T(8,128)(2,1)}, u32[]{:S(2)}, u32[]{:S(2)}) collective-permute-start(bf16[128,1024]{1,0:T(8,128)(2,1)} %fusion.4), channel_id=1, source_target_pairs={{0,1},{1,2},{2,3},{3,4},{4,5},{5,6},{6,7},{7,0},{8,9},{9,10},{10,1... | collective-permute-start | bytes 786440 | tf_op jit(solution)/shard_map/ppermute | solution.py:106
  192.7 9.5 %copy-start.11 = (f32[128,512]{1,0:T(8,128)S(1)}, f32[128,512]{1,0:T(8,128)}, u32[]{:S(2)}) copy-start(f32[128,512]{1,0:T(8,128)} %fusion.15) | copy-start | bytes 786436
  192.7 9.5 %copy-start.12 = (f32[128,512]{1,0:T(8,128)S(1)}, f32[128,512]{1,0:T(8,128)}, u32[]{:S(2)}) copy-start(f32[128,512]{1,0:T(8,128)} %fusion.14) | copy-start | bytes 786436
  193.5 12.7 %copy-start.14 = (f32[128,512]{1,0:T(8,128)S(1)}, f32[128,512]{1,0:T(8,128)}, u32[]{:S(2)}) copy-start(f32[128,512]{1,0:T(8,128)} %fusion.21) | copy-start | bytes 786436
  193.5 12.7 %copy-start.15 = (f32[128,512]{1,0:T(8,128)S(1)}, f32[128,512]{1,0:T(8,128)}, u32[]{:S(2)}) copy-start(f32[128,512]{1,0:T(8,128)} %fusion.20) | copy-start | bytes 786436
  193.5 12.7 %collective-permute-start.13 = (bf16[128,1024]{1,0:T(8,128)(2,1)}, bf16[128,1024]{1,0:T(8,128)(2,1)}, u32[]{:S(2)}, u32[]{:S(2)}) collective-permute-start(bf16[128,1024]{1,0:T(8,128)(2,1)} %fusion.7), channel_id=1, source_target_pairs={{0,7},{1,0},{2,1},{3,2},{4,3},{5,4},{6,5},{7,6},{8,15},{9,8},{10,9... | collective-permute-start | bytes 786440 | tf_op jit(solution)/shard_map/ppermute | solution.py:106
  202.2 11.2 %copy-start.3 = (bf16[128,1024]{1,0:T(8,128)(2,1)S(1)}, bf16[128,1024]{1,0:T(8,128)(2,1)}, u32[]{:S(2)}) copy-start(bf16[128,1024]{1,0:T(8,128)(2,1)} %attend.8) | copy-start | bytes 786436
  202.2 11.9 %copy-start.8 = (f32[128,512]{1,0:T(8,128)S(1)}, f32[128,512]{1,0:T(8,128)}, u32[]{:S(2)}) copy-start(f32[128,512]{1,0:T(8,128)} %fusion.13) | copy-start | bytes 786436
  202.2 12.0 %copy-start.9 = (f32[128,512]{1,0:T(8,128)S(1)}, f32[128,512]{1,0:T(8,128)}, u32[]{:S(2)}) copy-start(f32[128,512]{1,0:T(8,128)} %fusion.12) | copy-start | bytes 786436
  203.3 13.4 %copy-start.10 = (f32[128,512]{1,0:T(8,128)S(1)}, f32[128,512]{1,0:T(8,128)}, u32[]{:S(2)}) copy-start(f32[128,512]{1,0:T(8,128)} %fusion.19) | copy-start | bytes 786436
  203.3 13.3 %copy-start.13 = (f32[128,512]{1,0:T(8,128)S(1)}, f32[128,512]{1,0:T(8,128)}, u32[]{:S(2)}) copy-start(f32[128,512]{1,0:T(8,128)} %fusion.18) | copy-start | bytes 786436
  203.3 10.8 %collective-permute-start.10 = (bf16[128,1024]{1,0:T(8,128)(2,1)S(1)}, bf16[128,1024]{1,0:T(8,128)(2,1)S(1)}, u32[]{:S(2)}, u32[]{:S(2)}) collective-permute-start(bf16[128,1024]{1,0:T(8,128)(2,1)S(1)} %fusion.3), channel_id=1, source_target_pairs={{0,1},{1,2},{2,3},{3,4},{4,5},{5,6},{6,7},{7,0},{8,9},{9,10},{10,1... | collective-permute-start | bytes 786440 | tf_op jit(solution)/shard_map/ppermute | solution.py:106
  207.2 9.5 %collective-permute-start.14 = (bf16[128,1024]{1,0:T(8,128)(2,1)S(1)}, bf16[128,1024]{1,0:T(8,128)(2,1)S(1)}, u32[]{:S(2)}, u32[]{:S(2)}) collective-permute-start(bf16[128,1024]{1,0:T(8,128)(2,1)S(1)} %fusion.6), channel_id=1, source_target_pairs={{0,7},{1,0},{2,1},{3,2},{4,3},{5,4},{6,5},{7,6},{8,15},{9,8},{10,9... | collective-permute-start | bytes 786440 | tf_op jit(solution)/shard_map/ppermute | solution.py:106
  214.2 8.3 %collective-permute-start.11 = (bf16[128,1024]{1,0:T(8,128)(2,1)S(1)}, bf16[128,1024]{1,0:T(8,128)(2,1)S(1)}, u32[]{:S(2)}, u32[]{:S(2)}) collective-permute-start(bf16[128,1024]{1,0:T(8,128)(2,1)S(1)} %fusion.2), channel_id=1, source_target_pairs={{0,1},{1,2},{2,3},{3,4},{4,5},{5,6},{6,7},{7,0},{8,9},{9,10},{10,1... | collective-permute-start | bytes 786440 | tf_op jit(solution)/shard_map/ppermute | solution.py:106
  216.7 8.3 %collective-permute-start.15 = (bf16[128,1024]{1,0:T(8,128)(2,1)S(1)}, bf16[128,1024]{1,0:T(8,128)(2,1)S(1)}, u32[]{:S(2)}, u32[]{:S(2)}) collective-permute-start(bf16[128,1024]{1,0:T(8,128)(2,1)S(1)} %fusion.5), channel_id=1, source_target_pairs={{0,7},{1,0},{2,1},{3,2},{4,3},{5,4},{6,5},{7,6},{8,15},{9,8},{10,9... | collective-permute-start | bytes 786440 | tf_op jit(solution)/shard_map/ppermute | solution.py:106
  225.2 9.5 %collective-permute-start.16 = (bf16[128,512]{1,0:T(8,128)(2,1)S(1)}, bf16[128,512]{1,0:T(8,128)(2,1)S(1)}, u32[]{:S(2)}, u32[]{:S(2)}) collective-permute-start(bf16[128,512]{1,0:T(8,128)(2,1)S(1)} %get-tuple-element.12), channel_id=1, source_target_pairs={{0,8},{8,0},{1,9},{9,1},{2,10},{10,2},{3,11},{11,3},{4,12},{12,4},... | collective-permute-start | bytes 393224 | tf_op jit(solution)/shard_map/ppermute | solution.py:110
  (2 other events, 4.9 us)
Sparse Core Ops, SparseCore 0:
  9.4 44.3 all-gather.1

commit v6 on v5

--- a/solution.py
+++ b/solution.py
@@ -1,4 +1,3 @@
-import functools
 import math
 
 import jax
@@ -17,10 +16,11 @@
 EXP_SCALE = math.log2(math.e) / math.sqrt(HEAD)
 
 
-def attend_kernel(base, ids, lengths, order, q_ref, kv_ref, out_ref, acc_ref):
+def attend_kernel(ids, lengths, order, q_ref, kv_ref, out_ref, acc_ref):
     z, core = ids[0], ids[1]
-    owner = (z + base) % RING
-    first = order[(owner * 2 + core) * 2 + pl.program_id(0)] * BLOCK
+    step = pl.program_id(0)
+    owner = (z + step // 2) % RING
+    first = order[(owner * 2 + core) * 2 + step % 2] * BLOCK
     heads = q_ref.shape[1] // HEAD
     rows = BLOCK * heads
 
@@ -76,18 +76,18 @@
         out_ref[:, (2 * pair + 1) * HEAD : (2 * pair + 2) * HEAD] = turned[BLOCK:]
 
 
-def attend(base, ids, lengths, order, queries, kv):
-    width = queries.shape[1]
+def attend(ids, lengths, order, queries, kv):
+    total, width = queries.shape
 
     def q_map(i, ids, lengths, order):
-        return ((ids[0] + base - ids[2] + RING) % RING * 2 + i, 0)
+        return ((ids[0] + i // 2 - ids[2] + RING) % RING * 2 + i % 2, 0)
 
     return pl.pallas_call(
-        functools.partial(attend_kernel, base),
-        out_shape=jax.ShapeDtypeStruct((2 * BLOCK, width), jnp.bfloat16),
+        attend_kernel,
+        out_shape=jax.ShapeDtypeStruct(queries.shape, jnp.bfloat16),
         grid_spec=pltpu.PrefetchScalarGridSpec(
             num_scalar_prefetch=3,
-            grid=(2,),
+            grid=(total // BLOCK,),
             in_specs=[
                 pl.BlockSpec((BLOCK, width), q_map),
                 pl.BlockSpec(kv.shape, lambda i, *_: (0, 0)),
@@ -96,7 +96,7 @@
             scratch_shapes=[pltpu.VMEM((HEAD, BLOCK * (width // HEAD)), jnp.float32)],
         ),
         cost_estimate=pl.CostEstimate(
-            flops=600_000_000, bytes_accessed=2_000_000, transcendentals=500_000
+            flops=4_800_000_000, bytes_accessed=6_000_000, transcendentals=5_000_000
         ),
         name="attend",
     )(ids, lengths, order, queries, kv)
@@ -111,12 +111,14 @@
 
 
 def ring_gather(x, axis):
+    half = x.shape[0] // 2
     ups, downs = [x], [x]
     for _ in range(3):
         ups.append(shift(ups[-1], axis, -1))
         downs.append(shift(downs[-1], axis, 1))
-    far = shift(x, axis, RING // 2)
-    return jnp.concatenate([*ups, far, *downs[:0:-1]], axis=0)
+    top = shift(downs[3][:half], axis, 1)
+    bottom = shift(ups[3][half:], axis, -1)
+    return jnp.concatenate([*ups, top, bottom, *downs[:0:-1]], axis=0)
 
 
 def local(tokens, queries, key_value_weight, out_weight, doc_lengths, block_order):
@@ -134,17 +136,20 @@
     f32, bf16 = jnp.float32, jnp.bfloat16
     rows, width = queries.shape[0], out_weight.shape[1]
 
-    def product(base):
-        attn = attend(base, ids, doc_lengths, block_order, all_queries, kv)
-        return jnp.concatenate(
-            [jnp.dot(attn, w, preferred_element_type=f32) for w in (out_weight, other_weight)],
-            axis=1,
-        )
+    attn = attend(ids, doc_lengths, block_order, all_queries, kv)
+    out = [
+        jnp.dot(attn, w, preferred_element_type=f32).astype(bf16)
+        for w in (out_weight, other_weight)
+    ]
 
-    far = product(4).astype(bf16)
+    def product(step):
+        here = slice(step * rows, (step + 1) * rows)
+        return jnp.concatenate([part[here] for part in out], axis=1).astype(f32)
+
+    far = slice(4 * rows, 5 * rows)
     zero = jnp.zeros((rows, width), bf16)
-    up = jnp.concatenate([shift(far[:, :width], "z", 1), zero], axis=1)
-    down = jnp.concatenate([zero, shift(far[:, width:], "z", -1)], axis=1)
+    up = jnp.concatenate([shift(out[0][far], "z", 1), zero], axis=1)
+    down = jnp.concatenate([zero, shift(out[1][far], "z", -1)], axis=1)
     for step in (3, 2, 1):
         up = shift((product(step) + up.astype(f32)).astype(bf16), "z", 1)
         down = shift((product(RING - step) + down.astype(f32)).astype(bf16), "z", -1)

time: 244 us -> 208 us (0.85)
  the two profiles are of different devices: /device:TPU:7 before, /device:TPU:31 now
where the time goes in v6:
time: 208 us; the launch traced here: 207 us
  starting transfers between devices  63.2 us (30%)
  blocking collectives  63 us (30%)
  Pallas kernels  28.2 us (14%)
  waiting for transfers between devices  22.2 us (11%)
  between operations  13.7 us (7%)
  local copies, waits for them, and re-layouts  8.61 us (4%)
  matrix products  6.64 us (3%)
    psum x1, blocking collectives, local(): kv = lax.psum(partial_kv, ('y', 'core')).astype(jnp.bfloat16)  63 us
    ppermute x16, starting transfers between devices, shift(): return lax.ppermute(x, axis, [(i, (i + by) % RING) for i in range(RING)])  56.1 us
    pallas_call x1, Pallas kernels, attend(): pl.pallas_call(attend_kernel, out_shape=jax.ShapeDtypeStruct(queries.shap...  28.2 us
    ppermute x16, waiting for transfers between devices, shift(): return lax.ppermute(x, axis, [(i, (i + by) % RING) for i in range(RING)])  20.6 us
    ppermute x2, starting transfers between devices, swap(): return lax.ppermute(x, 'core', [(0, 1), (1, 0)])  7.07 us
    unnamed x14, local copies, waits for them, and re-layouts  6.61 us
    dot_general x2, matrix products, local(): jnp.dot(attn, w, preferred_element_type=f32).astype(bf16)  4.35 us
  transfers between devices with their start and end apart: 19, of which 9 were waited for; matrix products, arithmetic and copies ran while one was open for 5% of the time, Pallas kernels for 0%

profile of v6, /device:TPU:31, one launch (start us, length us, event | category | flops | bytes accessed | tf_op | source)
XLA Modules:
  0.0 206.8 jit_solution(2458006083261039810)
XLA Ops:
  7.3 4.4 %collective-permute-start.3 = (bf16[128,1024]{1,0:T(8,128)(2,1)}, bf16[128,1024]{1,0:T(8,128)(2,1)S(1)}, u32[]{:S(2)}, u32[]{:S(2)}) collective-permute-start(bf16[128,1024]{1,0:T(8,128)(2,1)} %param.7), channel_id=1, source_target_pairs={{0,16},{16,32},{32,48},{48,64},{64,80},{80,96},{96,112},{112,0},{1... | collective-permute-start | bytes 786440 | tf_op jit(solution)/shard_map/ppermute | solution.py:106
  11.7 1.9 collective-permute-start
  13.6 3.4 %collective-permute-done.3 = bf16[128,1024]{1,0:T(8,128)(2,1)S(1)} collective-permute-done((bf16[128,1024]{1,0:T(8,128)(2,1)}, bf16[128,1024]{1,0:T(8,128)(2,1)S(1)}, u32[]{:S(2)}, u32[]{:S(2)}) %collective-permute-start.3) | collective-permute-done | bytes 262176 | tf_op jit(solution)/shard_map/ppermute | solution.py:106
  17.0 5.2 %collective-permute-start.4 = (bf16[128,1024]{1,0:T(8,128)(2,1)S(1)}, bf16[128,1024]{1,0:T(8,128)(2,1)S(1)}, u32[]{:S(2)}, u32[]{:S(2)}) collective-permute-start(bf16[128,1024]{1,0:T(8,128)(2,1)S(1)} %collective-permute-done.3), channel_id=1, source_target_pairs={{0,16},{16,32},{32,48},{48,64},{64,80},{80,96},{96,112},{112,0},{1... | collective-permute-start | bytes 786440 | tf_op jit(solution)/shard_map/ppermute | solution.py:106
  22.2 1.9 collective-permute-start.1
  24.1 3.7 %collective-permute-start.8 = (bf16[1024,512]{1,0:T(8,128)(2,1)}, bf16[1024,512]{1,0:T(8,128)(2,1)S(1)}, u32[]{:S(2)}, u32[]{:S(2)}) collective-permute-start(bf16[1024,512]{1,0:T(8,128)(2,1)} %param.9), channel_id=1, source_target_pairs={{0,8},{8,0},{1,9},{9,1},{2,10},{10,2},{3,11},{11,3},{4,12},{12,4},... | collective-permute-start | bytes 3145736 | tf_op jit(solution)/shard_map/ppermute | solution.py:110
  27.9 4.9 %collective-permute-start.5 = (bf16[128,1024]{1,0:T(8,128)(2,1)S(1)}, bf16[128,1024]{1,0:T(8,128)(2,1)S(1)}, u32[]{:S(2)}, u32[]{:S(2)}) collective-permute-start(bf16[128,1024]{1,0:T(8,128)(2,1)S(1)} %collective-permute-done.4), channel_id=1, source_target_pairs={{0,16},{16,32},{32,48},{48,64},{64,80},{80,96},{96,112},{112,0},{1... | collective-permute-start | bytes 786440 | tf_op jit(solution)/shard_map/ppermute | solution.py:106
  32.7 1.7 constant_dynamic-update-slice_fusion.8
  34.4 1.9 collective-permute-start.2
  37.7 4.8 %collective-permute-start.6 = (bf16[64,1024]{1,0:T(8,128)(2,1)S(1)}, bf16[64,1024]{1,0:T(8,128)(2,1)S(1)}, u32[]{:S(2)}, u32[]{:S(2)}) collective-permute-start(bf16[64,1024]{1,0:T(8,128)(2,1)S(1)} %slice.80), channel_id=1, source_target_pairs={{0,16},{16,32},{32,48},{48,64},{64,80},{80,96},{96,112},{112,0},{1... | collective-permute-start | bytes 393224 | tf_op jit(solution)/shard_map/ppermute | solution.py:106
  43.8 1.9 collective-permute-start.7
  47.1 4.0 %collective-permute-done.7 = bf16[64,1024]{1,0:T(8,128)(2,1)S(1)} collective-permute-done((bf16[64,1024]{1,0:T(8,128)(2,1)S(1)}, bf16[64,1024]{1,0:T(8,128)(2,1)S(1)}, u32[]{:S(2)}, u32[]{:S(2)}) %collective-permute-start.7) | collective-permute-done | bytes 131104 | tf_op jit(solution)/shard_map/ppermute | solution.py:106
  53.9 2.3 %fusion.3 = f32[2048,256]{1,0:T(8,128)S(1)} fusion(bf16[2048,512]{1,0:T(8,128)(2,1)} %all-gather.2.cloned.1.call-done, bf16[512,256]{1,0:T(8,128)(2,1)S(1)} %copy-done), kind=kOutput, calls=%fused_computation.23 | convolution fusion | flops 536870912 | bytes 4456448 | tf_op jit(solution)/shard_map/dot_general | solution.py:130
  56.2 63.0 %all-reduce.3.kv_ref = bf16[2048,256]{1,0:T(8,128)(2,1)} all-reduce(f32[2048,256]{1,0:T(8,128)S(1)} %fusion.3), channel_id=1, replica_groups=mesh['dp'=4,'y'=8,'core'=2,'z'=8] {'y','core'}, use_global_device_ids=true, to_apply=%region_0.0 | all-reduce | flops 524288 | bytes 3145728 | tf_op jit(solution)/shard_map/psum | solution.py:134
  119.2 28.2 %attend.1 = bf16[1024,1024]{1,0:T(8,128)(2,1)} custom-call(s32[3]{0:T(128)} %pad_add_fusion.ids, s32[8]{0:T(128)} %lengths.1, s32[32]{0:T(128)} %order.1, bf16[1024,1024]{1,0:T(8,128)(2,1)} %constant_dynamic-update-slice_fusion.q_ref, bf16[2048,256]{1,0:T(8,128)(2,1)} %all-reduce.3.kv_ref), custom_call_target="tpu_custom_call" | custom-call | flops 4800000000 | bytes 6000000 | tf_op jit(solution)/shard_map/attend/pallas_call | solution.py:85
  147.4 3.0 %convolution_convert_fusion.1 = bf16[1024,512]{0,1:T(8,128)(2,1)S(1)} fusion(bf16[1024,1024]{1,0:T(8,128)(2,1)} %attend.1, bf16[1024,512]{1,0:T(8,128)(2,1)S(1)} %copy-done.1), kind=kOutput, calls=%fused_computation.1 | convolution fusion | flops 1074266112 | bytes 4194304 | tf_op jit(solution)/shard_map/dot_general | solution.py:141
  150.5 1.3 convolution_convert_fusion
  152.0 2.8 %collective-permute-start.9 = (bf16[128,512]{0,1:T(8,128)(2,1)S(1)}, bf16[128,512]{0,1:T(8,128)(2,1)S(1)}, u32[]{:S(2)}, u32[]{:S(2)}) collective-permute-start(bf16[128,512]{0,1:T(8,128)(2,1)S(1)} %get-tuple-element.15), channel_id=1, source_target_pairs={{0,1},{1,2},{2,3},{3,4},{4,5},{5,6},{6,7},{7,0},{8,9},{9,10},{10,1... | collective-permute-start | bytes 393224 | tf_op jit(solution)/shard_map/ppermute | solution.py:106
  155.0 5.9 %collective-permute-start.13 = (bf16[128,512]{0,1:T(8,128)(2,1)S(1)}, bf16[128,512]{0,1:T(8,128)(2,1)S(1)}, u32[]{:S(2)}, u32[]{:S(2)}) collective-permute-start(bf16[128,512]{0,1:T(8,128)(2,1)S(1)} %get-tuple-element.20), channel_id=1, source_target_pairs={{0,7},{1,0},{2,1},{3,2},{4,3},{5,4},{6,5},{7,6},{8,15},{9,8},{10,9... | collective-permute-start | bytes 393224 | tf_op jit(solution)/shard_map/ppermute | solution.py:106
  161.2 1.9 collective-permute-start.10
  163.2 4.7 %collective-permute-start.14 = (bf16[128,1024]{0,1:T(8,128)(2,1)S(1)}, bf16[128,1024]{0,1:T(8,128)(2,1)S(1)}, u32[]{:S(2)}, u32[]{:S(2)}) collective-permute-start(bf16[128,1024]{0,1:T(8,128)(2,1)S(1)} %add_convert_fusion.3), channel_id=1, source_target_pairs={{0,7},{1,0},{2,1},{3,2},{4,3},{5,4},{6,5},{7,6},{8,15},{9,8},{10,9... | collective-permute-start | bytes 786440 | tf_op jit(solution)/shard_map/ppermute | solution.py:106
  167.9 3.2 %collective-permute-done.10 = bf16[128,1024]{0,1:T(8,128)(2,1)S(1)} collective-permute-done((bf16[128,1024]{0,1:T(8,128)(2,1)S(1)}, bf16[128,1024]{0,1:T(8,128)(2,1)S(1)}, u32[]{:S(2)}, u32[]{:S(2)}) %collective-permute-start.10) | collective-permute-done | bytes 262176 | tf_op jit(solution)/shard_map/ppermute | solution.py:106
  171.2 1.9 collective-permute-start.11
  173.2 5.0 %collective-permute-start.15 = (bf16[128,1024]{0,1:T(8,128)(2,1)S(1)}, bf16[128,1024]{0,1:T(8,128)(2,1)S(1)}, u32[]{:S(2)}, u32[]{:S(2)}) collective-permute-start(bf16[128,1024]{0,1:T(8,128)(2,1)S(1)} %add_convert_fusion.2), channel_id=1, source_target_pairs={{0,7},{1,0},{2,1},{3,2},{4,3},{5,4},{6,5},{7,6},{8,15},{9,8},{10,9... | collective-permute-start | bytes 786440 | tf_op jit(solution)/shard_map/ppermute | solution.py:106
  178.2 4.2 %collective-permute-done.11 = bf16[128,1024]{0,1:T(8,128)(2,1)S(1)} collective-permute-done((bf16[128,1024]{0,1:T(8,128)(2,1)S(1)}, bf16[128,1024]{0,1:T(8,128)(2,1)S(1)}, u32[]{:S(2)}, u32[]{:S(2)}) %collective-permute-start.11) | collective-permute-done | bytes 262176 | tf_op jit(solution)/shard_map/ppermute | solution.py:106
  182.5 1.9 collective-permute-start.12
  184.5 5.0 %collective-permute-start.16 = (bf16[128,1024]{0,1:T(8,128)(2,1)S(1)}, bf16[128,1024]{0,1:T(8,128)(2,1)S(1)}, u32[]{:S(2)}, u32[]{:S(2)}) collective-permute-start(bf16[128,1024]{0,1:T(8,128)(2,1)S(1)} %add_convert_fusion.1), channel_id=1, source_target_pairs={{0,7},{1,0},{2,1},{3,2},{4,3},{5,4},{6,5},{7,6},{8,15},{9,8},{10,9... | collective-permute-start | bytes 786440 | tf_op jit(solution)/shard_map/ppermute | solution.py:106
  189.5 3.6 %collective-permute-done.12 = bf16[128,1024]{0,1:T(8,128)(2,1)S(1)} collective-permute-done((bf16[128,1024]{0,1:T(8,128)(2,1)S(1)}, bf16[128,1024]{0,1:T(8,128)(2,1)S(1)}, u32[]{:S(2)}, u32[]{:S(2)}) %collective-permute-start.12) | collective-permute-done | bytes 262176 | tf_op jit(solution)/shard_map/ppermute | solution.py:106
  193.1 1.5 collective-permute-done.16
  194.7 3.4 %collective-permute-start.17 = (bf16[128,512]{0,1:T(8,128)(2,1)S(1)}, bf16[128,512]{0,1:T(8,128)(2,1)S(1)}, u32[]{:S(2)}, u32[]{:S(2)}) collective-permute-start(bf16[128,512]{0,1:T(8,128)(2,1)S(1)} %get-tuple-element.28), channel_id=1, source_target_pairs={{0,8},{8,0},{1,9},{9,1},{2,10},{10,2},{3,11},{11,3},{4,12},{12,4},... | collective-permute-start | bytes 393224 | tf_op jit(solution)/shard_map/ppermute | solution.py:110
  198.1 1.0 collective-permute-done.17
  199.1 0.8 copy.7
  (42 shorter events, 8.8 us)
Async XLA Ops:
  6.5 47.4 %copy-start = (bf16[512,256]{1,0:T(8,128)(2,1)S(1)}, bf16[512,256]{1,0:T(8,128)(2,1)}, u32[]{:S(2)}) copy-start(bf16[512,256]{1,0:T(8,128)(2,1)} %param.8) | copy-start | bytes 786436
  6.5 47.4 %all-gather.2.cloned.1.call-start = ((), (), s32[]{:S(2)}) async-start(), calls=%async_computation | async-start | bytes 2359296 | tf_op jit(solution)/shard_map/all_gather | solution.py:127
  7.3 9.7 %collective-permute-start.3 = (bf16[128,1024]{1,0:T(8,128)(2,1)}, bf16[128,1024]{1,0:T(8,128)(2,1)S(1)}, u32[]{:S(2)}, u32[]{:S(2)}) collective-permute-start(bf16[128,1024]{1,0:T(8,128)(2,1)} %param.7), channel_id=1, source_target_pairs={{0,16},{16,32},{32,48},{48,64},{64,80},{80,96},{96,112},{112,0},{1... | collective-permute-start | bytes 786440 | tf_op jit(solution)/shard_map/ppermute | solution.py:106
  11.7 10.5 %collective-permute-start = (bf16[128,1024]{1,0:T(8,128)(2,1)}, bf16[128,1024]{1,0:T(8,128)(2,1)S(1)}, u32[]{:S(2)}, u32[]{:S(2)}) collective-permute-start(bf16[128,1024]{1,0:T(8,128)(2,1)} %param.7), channel_id=1, source_target_pairs={{0,112},{16,0},{32,16},{48,32},{64,48},{80,64},{96,80},{112,96},{1... | collective-permute-start | bytes 786440 | tf_op jit(solution)/shard_map/ppermute | solution.py:106
  17.0 10.9 %collective-permute-start.4 = (bf16[128,1024]{1,0:T(8,128)(2,1)S(1)}, bf16[128,1024]{1,0:T(8,128)(2,1)S(1)}, u32[]{:S(2)}, u32[]{:S(2)}) collective-permute-start(bf16[128,1024]{1,0:T(8,128)(2,1)S(1)} %collective-permute-done.3), channel_id=1, source_target_pairs={{0,16},{16,32},{32,48},{48,64},{64,80},{80,96},{96,112},{112,0},{1... | collective-permute-start | bytes 786440 | tf_op jit(solution)/shard_map/ppermute | solution.py:106
  22.2 12.2 %collective-permute-start.1 = (bf16[128,1024]{1,0:T(8,128)(2,1)S(1)}, bf16[128,1024]{1,0:T(8,128)(2,1)S(1)}, u32[]{:S(2)}, u32[]{:S(2)}) collective-permute-start(bf16[128,1024]{1,0:T(8,128)(2,1)S(1)} %collective-permute-done), channel_id=1, source_target_pairs={{0,112},{16,0},{32,16},{48,32},{64,48},{80,64},{96,80},{112,96},{1... | collective-permute-start | bytes 786440 | tf_op jit(solution)/shard_map/ppermute | solution.py:106
  24.1 32.1 %collective-permute-start.8 = (bf16[1024,512]{1,0:T(8,128)(2,1)}, bf16[1024,512]{1,0:T(8,128)(2,1)S(1)}, u32[]{:S(2)}, u32[]{:S(2)}) collective-permute-start(bf16[1024,512]{1,0:T(8,128)(2,1)} %param.9), channel_id=1, source_target_pairs={{0,8},{8,0},{1,9},{9,1},{2,10},{10,2},{3,11},{11,3},{4,12},{12,4},... | collective-permute-start | bytes 3145736 | tf_op jit(solution)/shard_map/ppermute | solution.py:110
  27.9 9.8 %collective-permute-start.5 = (bf16[128,1024]{1,0:T(8,128)(2,1)S(1)}, bf16[128,1024]{1,0:T(8,128)(2,1)S(1)}, u32[]{:S(2)}, u32[]{:S(2)}) collective-permute-start(bf16[128,1024]{1,0:T(8,128)(2,1)S(1)} %collective-permute-done.4), channel_id=1, source_target_pairs={{0,16},{16,32},{32,48},{48,64},{64,80},{80,96},{96,112},{112,0},{1... | collective-permute-start | bytes 786440 | tf_op jit(solution)/shard_map/ppermute | solution.py:106
  34.4 9.4 %collective-permute-start.2 = (bf16[128,1024]{1,0:T(8,128)(2,1)S(1)}, bf16[128,1024]{1,0:T(8,128)(2,1)S(1)}, u32[]{:S(2)}, u32[]{:S(2)}) collective-permute-start(bf16[128,1024]{1,0:T(8,128)(2,1)S(1)} %collective-permute-done.1), channel_id=1, source_target_pairs={{0,112},{16,0},{32,16},{48,32},{64,48},{80,64},{96,80},{112,96},{1... | collective-permute-start | bytes 786440 | tf_op jit(solution)/shard_map/ppermute | solution.py:106
  37.7 8.7 %collective-permute-start.6 = (bf16[64,1024]{1,0:T(8,128)(2,1)S(1)}, bf16[64,1024]{1,0:T(8,128)(2,1)S(1)}, u32[]{:S(2)}, u32[]{:S(2)}) collective-permute-start(bf16[64,1024]{1,0:T(8,128)(2,1)S(1)} %slice.80), channel_id=1, source_target_pairs={{0,16},{16,32},{32,48},{48,64},{64,80},{80,96},{96,112},{112,0},{1... | collective-permute-start | bytes 393224 | tf_op jit(solution)/shard_map/ppermute | solution.py:106
  43.8 7.3 %collective-permute-start.7 = (bf16[64,1024]{1,0:T(8,128)(2,1)S(1)}, bf16[64,1024]{1,0:T(8,128)(2,1)S(1)}, u32[]{:S(2)}, u32[]{:S(2)}) collective-permute-start(bf16[64,1024]{1,0:T(8,128)(2,1)S(1)} %slice.81), channel_id=1, source_target_pairs={{0,112},{16,0},{32,16},{48,32},{64,48},{80,64},{96,80},{112,96},{1... | collective-permute-start | bytes 393224 | tf_op jit(solution)/shard_map/ppermute | solution.py:106
  119.2 28.2 %copy-start.1 = (bf16[1024,512]{1,0:T(8,128)(2,1)S(1)}, bf16[1024,512]{1,0:T(8,128)(2,1)}, u32[]{:S(2)}) copy-start(bf16[1024,512]{1,0:T(8,128)(2,1)} %param.9) | copy-start | bytes 3145732
  147.4 3.0 %copy-start.2 = (bf16[1024,1024]{1,0:T(8,128)(2,1)S(1)}, bf16[1024,1024]{1,0:T(8,128)(2,1)}, u32[]{:S(2)}) copy-start(bf16[1024,1024]{1,0:T(8,128)(2,1)} %attend.1) | copy-start | bytes 6291460
  152.0 9.2 %collective-permute-start.9 = (bf16[128,512]{0,1:T(8,128)(2,1)S(1)}, bf16[128,512]{0,1:T(8,128)(2,1)S(1)}, u32[]{:S(2)}, u32[]{:S(2)}) collective-permute-start(bf16[128,512]{0,1:T(8,128)(2,1)S(1)} %get-tuple-element.15), channel_id=1, source_target_pairs={{0,1},{1,2},{2,3},{3,4},{4,5},{5,6},{6,7},{7,0},{8,9},{9,10},{10,1... | collective-permute-start | bytes 393224 | tf_op jit(solution)/shard_map/ppermute | solution.py:106
  155.0 8.1 %collective-permute-start.13 = (bf16[128,512]{0,1:T(8,128)(2,1)S(1)}, bf16[128,512]{0,1:T(8,128)(2,1)S(1)}, u32[]{:S(2)}, u32[]{:S(2)}) collective-permute-start(bf16[128,512]{0,1:T(8,128)(2,1)S(1)} %get-tuple-element.20), channel_id=1, source_target_pairs={{0,7},{1,0},{2,1},{3,2},{4,3},{5,4},{6,5},{7,6},{8,15},{9,8},{10,9... | collective-permute-start | bytes 393224 | tf_op jit(solution)/shard_map/ppermute | solution.py:106
  161.2 9.9 %collective-permute-start.10 = (bf16[128,1024]{0,1:T(8,128)(2,1)S(1)}, bf16[128,1024]{0,1:T(8,128)(2,1)S(1)}, u32[]{:S(2)}, u32[]{:S(2)}) collective-permute-start(bf16[128,1024]{0,1:T(8,128)(2,1)S(1)} %add_convert_fusion.6), channel_id=1, source_target_pairs={{0,1},{1,2},{2,3},{3,4},{4,5},{5,6},{6,7},{7,0},{8,9},{9,10},{10,1... | collective-permute-start | bytes 786440 | tf_op jit(solution)/shard_map/ppermute | solution.py:106
  163.2 9.9 %collective-permute-start.14 = (bf16[128,1024]{0,1:T(8,128)(2,1)S(1)}, bf16[128,1024]{0,1:T(8,128)(2,1)S(1)}, u32[]{:S(2)}, u32[]{:S(2)}) collective-permute-start(bf16[128,1024]{0,1:T(8,128)(2,1)S(1)} %add_convert_fusion.3), channel_id=1, source_target_pairs={{0,7},{1,0},{2,1},{3,2},{4,3},{5,4},{6,5},{7,6},{8,15},{9,8},{10,9... | collective-permute-start | bytes 786440 | tf_op jit(solution)/shard_map/ppermute | solution.py:106
  171.2 11.2 %collective-permute-start.11 = (bf16[128,1024]{0,1:T(8,128)(2,1)S(1)}, bf16[128,1024]{0,1:T(8,128)(2,1)S(1)}, u32[]{:S(2)}, u32[]{:S(2)}) collective-permute-start(bf16[128,1024]{0,1:T(8,128)(2,1)S(1)} %add_convert_fusion.5), channel_id=1, source_target_pairs={{0,1},{1,2},{2,3},{3,4},{4,5},{5,6},{6,7},{7,0},{8,9},{9,10},{10,1... | collective-permute-start | bytes 786440 | tf_op jit(solution)/shard_map/ppermute | solution.py:106
  173.2 11.2 %collective-permute-start.15 = (bf16[128,1024]{0,1:T(8,128)(2,1)S(1)}, bf16[128,1024]{0,1:T(8,128)(2,1)S(1)}, u32[]{:S(2)}, u32[]{:S(2)}) collective-permute-start(bf16[128,1024]{0,1:T(8,128)(2,1)S(1)} %add_convert_fusion.2), channel_id=1, source_target_pairs={{0,7},{1,0},{2,1},{3,2},{4,3},{5,4},{6,5},{7,6},{8,15},{9,8},{10,9... | collective-permute-start | bytes 786440 | tf_op jit(solution)/shard_map/ppermute | solution.py:106
  182.5 10.6 %collective-permute-start.12 = (bf16[128,1024]{0,1:T(8,128)(2,1)S(1)}, bf16[128,1024]{0,1:T(8,128)(2,1)S(1)}, u32[]{:S(2)}, u32[]{:S(2)}) collective-permute-start(bf16[128,1024]{0,1:T(8,128)(2,1)S(1)} %add_convert_fusion.4), channel_id=1, source_target_pairs={{0,1},{1,2},{2,3},{3,4},{4,5},{5,6},{6,7},{7,0},{8,9},{9,10},{10,1... | collective-permute-start | bytes 786440 | tf_op jit(solution)/shard_map/ppermute | solution.py:106
  184.5 10.0 %collective-permute-start.16 = (bf16[128,1024]{0,1:T(8,128)(2,1)S(1)}, bf16[128,1024]{0,1:T(8,128)(2,1)S(1)}, u32[]{:S(2)}, u32[]{:S(2)}) collective-permute-start(bf16[128,1024]{0,1:T(8,128)(2,1)S(1)} %add_convert_fusion.1), channel_id=1, source_target_pairs={{0,7},{1,0},{2,1},{3,2},{4,3},{5,4},{6,5},{7,6},{8,15},{9,8},{10,9... | collective-permute-start | bytes 786440 | tf_op jit(solution)/shard_map/ppermute | solution.py:106
  194.7 4.3 %collective-permute-start.17 = (bf16[128,512]{0,1:T(8,128)(2,1)S(1)}, bf16[128,512]{0,1:T(8,128)(2,1)S(1)}, u32[]{:S(2)}, u32[]{:S(2)}) collective-permute-start(bf16[128,512]{0,1:T(8,128)(2,1)S(1)} %get-tuple-element.28), channel_id=1, source_target_pairs={{0,8},{8,0},{1,9},{9,1},{2,10},{10,2},{3,11},{11,3},{4,12},{12,4},... | collective-permute-start | bytes 393224 | tf_op jit(solution)/shard_map/ppermute | solution.py:110
Sparse Core Ops, SparseCore 0:
  9.4 44.1 all-gather.1

commit v7 on v6

--- a/solution.py
+++ b/solution.py
@@ -16,13 +16,29 @@
 EXP_SCALE = math.log2(math.e) / math.sqrt(HEAD)
 
 
-def attend_kernel(ids, lengths, order, q_ref, kv_ref, out_ref, acc_ref):
+def attend_kernel(ids, lengths, order, *refs):
+    *pieces, kv_ref, out_ref, acc_ref, q_ref, sems = refs
     z, core = ids[0], ids[1]
     step = pl.program_id(0)
     owner = (z + step // 2) % RING
     first = order[(owner * 2 + core) * 2 + step % 2] * BLOCK
     heads = q_ref.shape[1] // HEAD
     rows = BLOCK * heads
+
+    @pl.when(step == 0)
+    def _():
+        copies, place = [], 0
+        for i, piece in enumerate(pieces):
+            here = q_ref.at[pl.ds(place, piece.shape[0])]
+            copies.append(pltpu.make_async_copy(piece, here, sems.at[i]))
+            place += piece.shape[0]
+        for copy in copies:
+            copy.start()
+        for copy in copies:
+            copy.wait()
+
+    near = (owner - ids[2] + RING) % RING * 2 + step % 2
+    here = pl.ds(pl.multiple_of(near * BLOCK, BLOCK), BLOCK)
 
     row_pos = first + lax.broadcasted_iota(jnp.int32, (1, HEAD), 1) % BLOCK
     row_start = jnp.zeros((1, HEAD), jnp.int32)
@@ -35,7 +51,7 @@
     key_row = lax.broadcasted_iota(jnp.int32, (KEYS, HEAD), 0)
 
     query = jnp.concatenate(
-        [q_ref[:, h * HEAD : (h + 1) * HEAD] for h in range(heads)], axis=0
+        [q_ref[here, h * HEAD : (h + 1) * HEAD] for h in range(heads)], axis=0
     )
     acc_ref[...] = jnp.zeros_like(acc_ref)
     last = first // KEYS
@@ -49,9 +65,11 @@
         scores = lax.dot_general(
             keys, query, (((1,), (1,)), ((), ())), preferred_element_type=jnp.float32
         )
-        key_pos = block * KEYS + key_row
+        base = block * KEYS
         bias = jnp.where(
-            (key_pos >= row_start) & (key_pos <= row_pos), jnp.float32(0.0), jnp.float32(NEG)
+            (key_row >= row_start - base) & (key_row <= row_pos - base),
+            jnp.float32(0.0),
+            jnp.float32(NEG),
         )
         scores = scores + jnp.concatenate([bias] * (rows // HEAD), axis=1)
         new = jnp.maximum(top, jnp.max(scores, axis=0, keepdims=True))
@@ -76,30 +94,29 @@
         out_ref[:, (2 * pair + 1) * HEAD : (2 * pair + 2) * HEAD] = turned[BLOCK:]
 
 
-def attend(ids, lengths, order, queries, kv):
-    total, width = queries.shape
-
-    def q_map(i, ids, lengths, order):
-        return ((ids[0] + i // 2 - ids[2] + RING) % RING * 2 + i % 2, 0)
-
+def attend(ids, lengths, order, pieces, kv):
+    width = pieces[0].shape[1]
+    total = sum(piece.shape[0] for piece in pieces)
     return pl.pallas_call(
         attend_kernel,
-        out_shape=jax.ShapeDtypeStruct(queries.shape, jnp.bfloat16),
+        out_shape=jax.ShapeDtypeStruct((total, width), jnp.bfloat16),
         grid_spec=pltpu.PrefetchScalarGridSpec(
             num_scalar_prefetch=3,
             grid=(total // BLOCK,),
-            in_specs=[
-                pl.BlockSpec((BLOCK, width), q_map),
-                pl.BlockSpec(kv.shape, lambda i, *_: (0, 0)),
+            in_specs=[pl.BlockSpec(memory_space=pl.ANY)] * len(pieces)
+            + [pl.BlockSpec(kv.shape, lambda i, *_: (0, 0))],
+            out_specs=pl.BlockSpec((BLOCK, width), lambda i, *_: (i, 0)),
+            scratch_shapes=[
+                pltpu.VMEM((HEAD, BLOCK * (width // HEAD)), jnp.float32),
+                pltpu.VMEM((total, width), jnp.bfloat16),
+                pltpu.SemaphoreType.DMA((len(pieces),)),
             ],
-            out_specs=pl.BlockSpec((BLOCK, width), lambda i, *_: (i, 0)),
-            scratch_shapes=[pltpu.VMEM((HEAD, BLOCK * (width // HEAD)), jnp.float32)],
         ),
         cost_estimate=pl.CostEstimate(
             flops=4_800_000_000, bytes_accessed=6_000_000, transcendentals=5_000_000
         ),
         name="attend",
-    )(ids, lengths, order, queries, kv)
+    )(ids, lengths, order, *pieces, kv)
 
 
 def shift(x, axis, by):
@@ -118,7 +135,7 @@
         downs.append(shift(downs[-1], axis, 1))
     top = shift(downs[3][:half], axis, 1)
     bottom = shift(ups[3][half:], axis, -1)
-    return jnp.concatenate([*ups, top, bottom, *downs[:0:-1]], axis=0)
+    return [*ups, top, bottom, *downs[:0:-1]]
 
 
 def local(tokens, queries, key_value_weight, out_weight, doc_lengths, block_order):
@@ -128,15 +145,18 @@
     all_queries = ring_gather(queries, "y")
     other_weight = swap(out_weight)
     partial_kv = jnp.dot(all_tokens, key_value_weight, preferred_element_type=jnp.float32)
-    partial_kv, all_queries, other_weight = lax.optimization_barrier(
-        (partial_kv, all_queries, other_weight)
-    )
+    partial_kv, other_weight = lax.optimization_barrier((partial_kv, other_weight))
     kv = lax.psum(partial_kv, ("y", "core")).astype(jnp.bfloat16)
 
     f32, bf16 = jnp.float32, jnp.bfloat16
     rows, width = queries.shape[0], out_weight.shape[1]
 
     attn = attend(ids, doc_lengths, block_order, all_queries, kv)
+    far = slice(4 * rows, 5 * rows)
+    first = [
+        jnp.dot(attn[far], w, preferred_element_type=f32).astype(bf16)
+        for w in (out_weight, other_weight)
+    ]
     out = [
         jnp.dot(attn, w, preferred_element_type=f32).astype(bf16)
         for w in (out_weight, other_weight)
@@ -146,10 +166,9 @@
         here = slice(step * rows, (step + 1) * rows)
         return jnp.concatenate([part[here] for part in out], axis=1).astype(f32)
 
-    far = slice(4 * rows, 5 * rows)
     zero = jnp.zeros((rows, width), bf16)
-    up = jnp.concatenate([shift(out[0][far], "z", 1), zero], axis=1)
-    down = jnp.concatenate([zero, shift(out[1][far], "z", -1)], axis=1)
+    up = jnp.concatenate([shift(first[0], "z", 1), zero], axis=1)
+    down = jnp.concatenate([zero, shift(first[1], "z", -1)], axis=1)
     for step in (3, 2, 1):
         up = shift((product(step) + up.astype(f32)).astype(bf16), "z", 1)
         down = shift((product(RING - step) + down.astype(f32)).astype(bf16), "z", -1)

time: 208 us -> 214 us (1.029)
  waiting for transfers between devices: 22.2 us -> 33.6 us
  local copies, waits for them, and re-layouts: 8.61 us -> 2.09 us
  starting transfers between devices: 63.2 us -> 61 us
    all_gather x1, waiting for transfers between devices: 0.01 us -> 10.4 us  [local(): all_tokens = lax.all_gather(tokens, 'z', axis=0, tiled=True)]
    unnamed x14 -> x18, local copies, waits for them, and re-layouts: 6.61 us -> 0.04 us
    ppermute x16, starting transfers between devices: 56.1 us -> 53.8 us  [shift(): return lax.ppermute(x, axis, [(i, (i + by) % RING) for i in range(RING)])]
  transfers between devices with their start and end apart: 19 -> 19, of which waited for: 9 -> 12; matrix products, arithmetic and copies ran while one was open for 5% -> 2% of each run, Pallas kernels for 0% -> 0%
where the time goes in v7:
time: 214 us; the launch traced here: 213 us
  blocking collectives  63.3 us (30%)
  starting transfers between devices  61 us (29%)
  waiting for transfers between devices  33.6 us (16%)
  Pallas kernels  29.2 us (14%)
  between operations  13.8 us (6%)
  matrix products  8.63 us (4%)
    psum x1, blocking collectives, local(): kv = lax.psum(partial_kv, ('y', 'core')).astype(jnp.bfloat16)  63.3 us
    ppermute x16, starting transfers between devices, shift(): return lax.ppermute(x, axis, [(i, (i + by) % RING) for i in range(RING)])  53.8 us
    pallas_call x1, Pallas kernels, attend(): pl.pallas_call(attend_kernel, out_shape=jax.ShapeDtypeStruct((total, widt...  29.2 us
    ppermute x16, waiting for transfers between devices, shift(): return lax.ppermute(x, axis, [(i, (i + by) % RING) for i in range(RING)])  21.5 us
    all_gather x1, waiting for transfers between devices, local(): all_tokens = lax.all_gather(tokens, 'z', axis=0, tiled=True)  10.4 us
    ppermute x2, starting transfers between devices, swap(): return lax.ppermute(x, 'core', [(0, 1), (1, 0)])  7.16 us
    dot_general x2, matrix products, local(): jnp.dot(attn, w, preferred_element_type=f32).astype(bf16)  4.33 us
  transfers between devices with their start and end apart: 19, of which 12 were waited for; matrix products, arithmetic and copies ran while one was open for 2% of the time, Pallas kernels for 0%

profile of v7, /device:TPU:31, one launch (start us, length us, event | category | flops | bytes accessed | tf_op | source)
XLA Modules:
  0.0 212.8 jit_solution(14594657053073768294)
XLA Ops:
  7.3 2.1 collective-permute-start
  9.3 4.4 %collective-permute-start.3 = (bf16[128,1024]{1,0:T(8,128)(2,1)}, bf16[128,1024]{1,0:T(8,128)(2,1)S(1)}, u32[]{:S(2)}, u32[]{:S(2)}) collective-permute-start(bf16[128,1024]{1,0:T(8,128)(2,1)} %refs_0_.1), channel_id=1, source_target_pairs={{0,16},{16,32},{32,48},{48,64},{64,80},{80,96},{96,112},{112,0},{1... | collective-permute-start | bytes 786440 | tf_op jit(solution)/shard_map/ppermute | solution.py:123
  13.8 3.1 %collective-permute-start.8 = (bf16[1024,512]{1,0:T(8,128)(2,1)}, bf16[1024,512]{1,0:T(8,128)(2,1)S(1)}, u32[]{:S(2)}, u32[]{:S(2)}) collective-permute-start(bf16[1024,512]{1,0:T(8,128)(2,1)} %param.9), channel_id=1, source_target_pairs={{0,8},{8,0},{1,9},{9,1},{2,10},{10,2},{3,11},{11,3},{4,12},{12,4},... | collective-permute-start | bytes 3145736 | tf_op jit(solution)/shard_map/ppermute | solution.py:127
  17.8 1.9 collective-permute-start.1
  19.7 4.6 %collective-permute-start.4 = (bf16[128,1024]{1,0:T(8,128)(2,1)S(1)}, bf16[128,1024]{1,0:T(8,128)(2,1)S(1)}, u32[]{:S(2)}, u32[]{:S(2)}) collective-permute-start(bf16[128,1024]{1,0:T(8,128)(2,1)S(1)} %collective-permute-done.3.refs_8_), channel_id=1, source_target_pairs={{0,16},{16,32},{32,48},{48,64},{64,80},{80,96},{96,112},{112,0},{1... | collective-permute-start | bytes 786440 | tf_op jit(solution)/shard_map/ppermute | solution.py:123
  24.3 2.9 %collective-permute-done.1.refs_2_ = bf16[128,1024]{1,0:T(8,128)(2,1)S(1)} collective-permute-done((bf16[128,1024]{1,0:T(8,128)(2,1)S(1)}, bf16[128,1024]{1,0:T(8,128)(2,1)S(1)}, u32[]{:S(2)}, u32[]{:S(2)}) %collective-permute-start.1) | collective-permute-done | bytes 262176 | tf_op jit(solution)/shard_map/ppermute | solution.py:123
  27.2 1.9 collective-permute-start.2
  29.2 4.6 %collective-permute-start.5 = (bf16[128,1024]{1,0:T(8,128)(2,1)S(1)}, bf16[128,1024]{1,0:T(8,128)(2,1)S(1)}, u32[]{:S(2)}, u32[]{:S(2)}) collective-permute-start(bf16[128,1024]{1,0:T(8,128)(2,1)S(1)} %collective-permute-done.4.refs_7_), channel_id=1, source_target_pairs={{0,16},{16,32},{32,48},{48,64},{64,80},{80,96},{96,112},{112,0},{1... | collective-permute-start | bytes 786440 | tf_op jit(solution)/shard_map/ppermute | solution.py:123
  34.4 1.1 collective-permute-done.2.refs_3_
  35.5 1.9 collective-permute-start.7
  38.2 5.0 %collective-permute-start.6 = (bf16[64,1024]{1,0:T(8,128)(2,1)}, bf16[64,1024]{1,0:T(8,128)(2,1)}, u32[]{:S(2)}, u32[]{:S(2)}) collective-permute-start(bf16[64,1024]{1,0:T(8,128)(2,1)} %slice.77), channel_id=1, source_target_pairs={{0,16},{16,32},{32,48},{48,64},{64,80},{80,96},{96,112},{112,0},{1... | collective-permute-start | bytes 393224 | tf_op jit(solution)/shard_map/ppermute | solution.py:123
  43.2 10.4 %all-gather.2.cloned.1.call-done = bf16[2048,512]{1,0:T(8,128)(2,1)} async-done(((bf16[256,512]{1,0:T(8,128)(2,1)}), bf16[2048,512]{1,0:T(8,128)(2,1)}) %all-gather.2.cloned.1.call-update) | async-done | bytes 2097168 | tf_op jit(solution)/shard_map/all_gather | solution.py:144
  53.6 2.3 %fusion.5 = f32[2048,256]{1,0:T(8,128)S(1)} fusion(bf16[2048,512]{1,0:T(8,128)(2,1)} %all-gather.2.cloned.1.call-done, bf16[512,256]{1,0:T(8,128)(2,1)S(1)} %copy-done), kind=kOutput, calls=%fused_computation.18 | convolution fusion | flops 536870912 | bytes 4456448 | tf_op jit(solution)/shard_map/dot_general | solution.py:147
  55.9 63.3 %all-reduce.3.refs_9_ = bf16[2048,256]{1,0:T(8,128)(2,1)} all-reduce(f32[2048,256]{1,0:T(8,128)S(1)} %fusion.5), channel_id=1, replica_groups=mesh['dp'=4,'y'=8,'core'=2,'z'=8] {'y','core'}, use_global_device_ids=true, to_apply=%region_0.0 | all-reduce | flops 524288 | bytes 3145728 | tf_op jit(solution)/shard_map/psum | solution.py:149
  119.2 29.2 %attend.1 = bf16[1024,1024]{1,0:T(8,128)(2,1)} custom-call(s32[3]{0:T(128)} %pad_add_fusion.ids, s32[8]{0:T(128)} %lengths.1, s32[32]{0:T(128)} %order.1, bf16[128,1024]{1,0:T(8,128)(2,1)} %refs_0_.1, bf16[128,1024]{1,0:T(8,128)(2,1)} %copy-done.5, bf16[128,1024]{1,0:T(8,128)(2,1)} %copy-done.7, bf16[128,1024]{1,0:T(8,128)(2,1)} %copy-done.3, ...), custom_call_target="tpu_custom_call" | custom-call | flops 4800000000 | bytes 6000000 | tf_op jit(solution)/shard_map/attend/pallas_call | solution.py:100
  148.4 1.5 convolution_convert_fusion.2
  149.9 3.0 %convolution_convert_fusion = bf16[1024,512]{0,1:T(8,128)(2,1)S(1)} fusion(bf16[1024,1024]{1,0:T(8,128)(2,1)} %attend.1, bf16[1024,512]{1,0:T(8,128)(2,1)S(1)} %collective-permute-done.8), kind=kOutput, calls=%fused_computation | convolution fusion | flops 1074266112 | bytes 4194304 | tf_op jit(solution)/shard_map/dot_general | solution.py:161
  153.5 1.3 convolution_convert_fusion.1
  154.8 2.8 %collective-permute-start.9 = (bf16[128,512]{0,1:T(8,128)(2,1)S(1)}, bf16[128,512]{0,1:T(8,128)(2,1)S(1)}, u32[]{:S(2)}, u32[]{:S(2)}) collective-permute-start(bf16[128,512]{0,1:T(8,128)(2,1)S(1)} %convolution_convert_fusion.3), channel_id=1, source_target_pairs={{0,1},{1,2},{2,3},{3,4},{4,5},{5,6},{6,7},{7,0},{8,9},{9,10},{10,1... | collective-permute-start | bytes 393224 | tf_op jit(solution)/shard_map/ppermute | solution.py:123
  157.6 3.7 %collective-permute-start.13 = (bf16[128,512]{0,1:T(8,128)(2,1)S(1)}, bf16[128,512]{0,1:T(8,128)(2,1)S(1)}, u32[]{:S(2)}, u32[]{:S(2)}) collective-permute-start(bf16[128,512]{0,1:T(8,128)(2,1)S(1)} %convolution_convert_fusion.2), channel_id=1, source_target_pairs={{0,7},{1,0},{2,1},{3,2},{4,3},{5,4},{6,5},{7,6},{8,15},{9,8},{10,9... | collective-permute-start | bytes 393224 | tf_op jit(solution)/shard_map/ppermute | solution.py:123
  161.8 1.6 collective-permute-done.13
  163.4 4.9 %collective-permute-start.14 = (bf16[128,1024]{0,1:T(8,128)(2,1)S(1)}, bf16[128,1024]{0,1:T(8,128)(2,1)S(1)}, u32[]{:S(2)}, u32[]{:S(2)}) collective-permute-start(bf16[128,1024]{0,1:T(8,128)(2,1)S(1)} %add_convert_fusion.3), channel_id=1, source_target_pairs={{0,7},{1,0},{2,1},{3,2},{4,3},{5,4},{6,5},{7,6},{8,15},{9,8},{10,9... | collective-permute-start | bytes 786440 | tf_op jit(solution)/shard_map/ppermute | solution.py:123
  168.3 1.9 collective-permute-start.10
  170.3 3.7 %collective-permute-done.14 = bf16[128,1024]{0,1:T(8,128)(2,1)S(1)} collective-permute-done((bf16[128,1024]{0,1:T(8,128)(2,1)S(1)}, bf16[128,1024]{0,1:T(8,128)(2,1)S(1)}, u32[]{:S(2)}, u32[]{:S(2)}) %collective-permute-start.14) | collective-permute-done | bytes 262176 | tf_op jit(solution)/shard_map/ppermute | solution.py:123
  174.0 5.0 %collective-permute-start.15 = (bf16[128,1024]{0,1:T(8,128)(2,1)S(1)}, bf16[128,1024]{0,1:T(8,128)(2,1)S(1)}, u32[]{:S(2)}, u32[]{:S(2)}) collective-permute-start(bf16[128,1024]{0,1:T(8,128)(2,1)S(1)} %add_convert_fusion.2), channel_id=1, source_target_pairs={{0,7},{1,0},{2,1},{3,2},{4,3},{5,4},{6,5},{7,6},{8,15},{9,8},{10,9... | collective-permute-start | bytes 786440 | tf_op jit(solution)/shard_map/ppermute | solution.py:123
  179.5 1.9 collective-permute-start.11
  181.4 3.0 %collective-permute-done.15 = bf16[128,1024]{0,1:T(8,128)(2,1)S(1)} collective-permute-done((bf16[128,1024]{0,1:T(8,128)(2,1)S(1)}, bf16[128,1024]{0,1:T(8,128)(2,1)S(1)}, u32[]{:S(2)}, u32[]{:S(2)}) %collective-permute-start.15) | collective-permute-done | bytes 262176 | tf_op jit(solution)/shard_map/ppermute | solution.py:123
  184.5 5.3 %collective-permute-start.16 = (bf16[128,1024]{0,1:T(8,128)(2,1)S(1)}, bf16[128,1024]{0,1:T(8,128)(2,1)S(1)}, u32[]{:S(2)}, u32[]{:S(2)}) collective-permute-start(bf16[128,1024]{0,1:T(8,128)(2,1)S(1)} %add_convert_fusion.1), channel_id=1, source_target_pairs={{0,7},{1,0},{2,1},{3,2},{4,3},{5,4},{6,5},{7,6},{8,15},{9,8},{10,9... | collective-permute-start | bytes 786440 | tf_op jit(solution)/shard_map/ppermute | solution.py:123
  190.2 1.9 collective-permute-start.12
  192.1 2.3 %collective-permute-done.16 = bf16[128,1024]{0,1:T(8,128)(2,1)S(1)} collective-permute-done((bf16[128,1024]{0,1:T(8,128)(2,1)S(1)}, bf16[128,1024]{0,1:T(8,128)(2,1)S(1)}, u32[]{:S(2)}, u32[]{:S(2)}) %collective-permute-start.16) | collective-permute-done | bytes 262176 | tf_op jit(solution)/shard_map/ppermute | solution.py:123
  194.4 5.5 %collective-permute-done.12 = bf16[128,1024]{0,1:T(8,128)(2,1)S(1)} collective-permute-done((bf16[128,1024]{0,1:T(8,128)(2,1)S(1)}, bf16[128,1024]{0,1:T(8,128)(2,1)S(1)}, u32[]{:S(2)}, u32[]{:S(2)}) %collective-permute-start.12) | collective-permute-done | bytes 262176 | tf_op jit(solution)/shard_map/ppermute | solution.py:123
  200.0 4.0 %collective-permute-start.17 = (bf16[128,512]{0,1:T(8,128)(2,1)S(1)}, bf16[128,512]{0,1:T(8,128)(2,1)S(1)}, u32[]{:S(2)}, u32[]{:S(2)}) collective-permute-start(bf16[128,512]{0,1:T(8,128)(2,1)S(1)} %get-tuple-element.24), channel_id=1, source_target_pairs={{0,8},{8,0},{1,9},{9,1},{2,10},{10,2},{3,11},{11,3},{4,12},{12,4},... | collective-permute-start | bytes 393224 | tf_op jit(solution)/shard_map/ppermute | solution.py:127
  (46 shorter events, 7.0 us)
Async XLA Ops:
  6.5 47.0 %copy-start = (bf16[512,256]{1,0:T(8,128)(2,1)S(1)}, bf16[512,256]{1,0:T(8,128)(2,1)}, u32[]{:S(2)}) copy-start(bf16[512,256]{1,0:T(8,128)(2,1)} %param.8) | copy-start | bytes 786436
  6.5 47.0 %all-gather.2.cloned.1.call-start = ((), (), s32[]{:S(2)}) async-start(), calls=%async_computation | async-start | bytes 2359296 | tf_op jit(solution)/shard_map/all_gather | solution.py:144
  7.3 10.5 %collective-permute-start = (bf16[128,1024]{1,0:T(8,128)(2,1)}, bf16[128,1024]{1,0:T(8,128)(2,1)S(1)}, u32[]{:S(2)}, u32[]{:S(2)}) collective-permute-start(bf16[128,1024]{1,0:T(8,128)(2,1)} %refs_0_.1), channel_id=1, source_target_pairs={{0,112},{16,0},{32,16},{48,32},{64,48},{80,64},{96,80},{112,96},{1... | collective-permute-start | bytes 786440 | tf_op jit(solution)/shard_map/ppermute | solution.py:123
  9.3 10.3 %collective-permute-start.3 = (bf16[128,1024]{1,0:T(8,128)(2,1)}, bf16[128,1024]{1,0:T(8,128)(2,1)S(1)}, u32[]{:S(2)}, u32[]{:S(2)}) collective-permute-start(bf16[128,1024]{1,0:T(8,128)(2,1)} %refs_0_.1), channel_id=1, source_target_pairs={{0,16},{16,32},{32,48},{48,64},{64,80},{80,96},{96,112},{112,0},{1... | collective-permute-start | bytes 786440 | tf_op jit(solution)/shard_map/ppermute | solution.py:123
  13.8 42.1 %collective-permute-start.8 = (bf16[1024,512]{1,0:T(8,128)(2,1)}, bf16[1024,512]{1,0:T(8,128)(2,1)S(1)}, u32[]{:S(2)}, u32[]{:S(2)}) collective-permute-start(bf16[1024,512]{1,0:T(8,128)(2,1)} %param.9), channel_id=1, source_target_pairs={{0,8},{8,0},{1,9},{9,1},{2,10},{10,2},{3,11},{11,3},{4,12},{12,4},... | collective-permute-start | bytes 3145736 | tf_op jit(solution)/shard_map/ppermute | solution.py:127
  17.8 11.4 %copy-start.5 = (bf16[128,1024]{1,0:T(8,128)(2,1)}, bf16[128,1024]{1,0:T(8,128)(2,1)S(1)}, u32[]{:S(2)}) copy-start(bf16[128,1024]{1,0:T(8,128)(2,1)S(1)} %collective-permute-done.refs_1_) | copy-start | bytes 786436
  17.8 9.4 %collective-permute-start.1 = (bf16[128,1024]{1,0:T(8,128)(2,1)S(1)}, bf16[128,1024]{1,0:T(8,128)(2,1)S(1)}, u32[]{:S(2)}, u32[]{:S(2)}) collective-permute-start(bf16[128,1024]{1,0:T(8,128)(2,1)S(1)} %collective-permute-done.refs_1_), channel_id=1, source_target_pairs={{0,112},{16,0},{32,16},{48,32},{64,48},{80,64},{96,80},{112,96},{1... | collective-permute-start | bytes 786440 | tf_op jit(solution)/shard_map/ppermute | solution.py:123
  19.7 9.4 %copy-start.6 = (bf16[128,1024]{1,0:T(8,128)(2,1)}, bf16[128,1024]{1,0:T(8,128)(2,1)S(1)}, u32[]{:S(2)}) copy-start(bf16[128,1024]{1,0:T(8,128)(2,1)S(1)} %collective-permute-done.3.refs_8_) | copy-start | bytes 786436
  19.7 9.4 %collective-permute-start.4 = (bf16[128,1024]{1,0:T(8,128)(2,1)S(1)}, bf16[128,1024]{1,0:T(8,128)(2,1)S(1)}, u32[]{:S(2)}, u32[]{:S(2)}) collective-permute-start(bf16[128,1024]{1,0:T(8,128)(2,1)S(1)} %collective-permute-done.3.refs_8_), channel_id=1, source_target_pairs={{0,16},{16,32},{32,48},{48,64},{64,80},{80,96},{96,112},{112,0},{1... | collective-permute-start | bytes 786440 | tf_op jit(solution)/shard_map/ppermute | solution.py:123
  27.2 16.0 %copy-start.7 = (bf16[128,1024]{1,0:T(8,128)(2,1)}, bf16[128,1024]{1,0:T(8,128)(2,1)S(1)}, u32[]{:S(2)}) copy-start(bf16[128,1024]{1,0:T(8,128)(2,1)S(1)} %collective-permute-done.1.refs_2_) | copy-start | bytes 786436
  27.2 8.3 %collective-permute-start.2 = (bf16[128,1024]{1,0:T(8,128)(2,1)S(1)}, bf16[128,1024]{1,0:T(8,128)(2,1)S(1)}, u32[]{:S(2)}, u32[]{:S(2)}) collective-permute-start(bf16[128,1024]{1,0:T(8,128)(2,1)S(1)} %collective-permute-done.1.refs_2_), channel_id=1, source_target_pairs={{0,112},{16,0},{32,16},{48,32},{64,48},{80,64},{96,80},{112,96},{1... | collective-permute-start | bytes 786440 | tf_op jit(solution)/shard_map/ppermute | solution.py:123
  29.1 14.0 %copy-start.8 = (bf16[128,1024]{1,0:T(8,128)(2,1)}, bf16[128,1024]{1,0:T(8,128)(2,1)S(1)}, u32[]{:S(2)}) copy-start(bf16[128,1024]{1,0:T(8,128)(2,1)S(1)} %collective-permute-done.4.refs_7_) | copy-start | bytes 786436
  29.2 8.3 %collective-permute-start.5 = (bf16[128,1024]{1,0:T(8,128)(2,1)S(1)}, bf16[128,1024]{1,0:T(8,128)(2,1)S(1)}, u32[]{:S(2)}, u32[]{:S(2)}) collective-permute-start(bf16[128,1024]{1,0:T(8,128)(2,1)S(1)} %collective-permute-done.4.refs_7_), channel_id=1, source_target_pairs={{0,16},{16,32},{32,48},{48,64},{64,80},{80,96},{96,112},{112,0},{1... | collective-permute-start | bytes 786440 | tf_op jit(solution)/shard_map/ppermute | solution.py:123
  35.5 7.7 %copy-start.3 = (bf16[128,1024]{1,0:T(8,128)(2,1)}, bf16[128,1024]{1,0:T(8,128)(2,1)S(1)}, u32[]{:S(2)}) copy-start(bf16[128,1024]{1,0:T(8,128)(2,1)S(1)} %collective-permute-done.2.refs_3_) | copy-start | bytes 786436
  35.5 83.7 %collective-permute-start.7 = (bf16[64,1024]{1,0:T(8,128)(2,1)S(1)}, bf16[64,1024]{1,0:T(8,128)(2,1)}, u32[]{:S(2)}, u32[]{:S(2)}) collective-permute-start(bf16[64,1024]{1,0:T(8,128)(2,1)S(1)} %slice.78), channel_id=1, source_target_pairs={{0,112},{16,0},{32,16},{48,32},{64,48},{80,64},{96,80},{112,96},{1... | collective-permute-start | bytes 393224 | tf_op jit(solution)/shard_map/ppermute | solution.py:123
  37.5 5.7 %copy-start.4 = (bf16[128,1024]{1,0:T(8,128)(2,1)}, bf16[128,1024]{1,0:T(8,128)(2,1)S(1)}, u32[]{:S(2)}) copy-start(bf16[128,1024]{1,0:T(8,128)(2,1)S(1)} %collective-permute-done.5.refs_6_) | copy-start | bytes 786436
  38.2 81.0 %collective-permute-start.6 = (bf16[64,1024]{1,0:T(8,128)(2,1)}, bf16[64,1024]{1,0:T(8,128)(2,1)}, u32[]{:S(2)}, u32[]{:S(2)}) collective-permute-start(bf16[64,1024]{1,0:T(8,128)(2,1)} %slice.77), channel_id=1, source_target_pairs={{0,16},{16,32},{32,48},{48,64},{64,80},{80,96},{96,112},{112,0},{1... | collective-permute-start | bytes 393224 | tf_op jit(solution)/shard_map/ppermute | solution.py:123
  149.9 3.1 %copy-start.1 = (bf16[1024,512]{1,0:T(8,128)(2,1)S(1)}, bf16[1024,512]{1,0:T(8,128)(2,1)}, u32[]{:S(2)}) copy-start(bf16[1024,512]{1,0:T(8,128)(2,1)} %param.9) | copy-start | bytes 3145732
  149.9 3.1 %copy-start.2 = (bf16[1024,1024]{1,0:T(8,128)(2,1)S(1)}, bf16[1024,1024]{1,0:T(8,128)(2,1)}, u32[]{:S(2)}) copy-start(bf16[1024,1024]{1,0:T(8,128)(2,1)} %attend.1) | copy-start | bytes 6291460
  154.8 13.5 %collective-permute-start.9 = (bf16[128,512]{0,1:T(8,128)(2,1)S(1)}, bf16[128,512]{0,1:T(8,128)(2,1)S(1)}, u32[]{:S(2)}, u32[]{:S(2)}) collective-permute-start(bf16[128,512]{0,1:T(8,128)(2,1)S(1)} %convolution_convert_fusion.3), channel_id=1, source_target_pairs={{0,1},{1,2},{2,3},{3,4},{4,5},{5,6},{6,7},{7,0},{8,9},{9,10},{10,1... | collective-permute-start | bytes 393224 | tf_op jit(solution)/shard_map/ppermute | solution.py:123
  157.6 5.7 %collective-permute-start.13 = (bf16[128,512]{0,1:T(8,128)(2,1)S(1)}, bf16[128,512]{0,1:T(8,128)(2,1)S(1)}, u32[]{:S(2)}, u32[]{:S(2)}) collective-permute-start(bf16[128,512]{0,1:T(8,128)(2,1)S(1)} %convolution_convert_fusion.2), channel_id=1, source_target_pairs={{0,7},{1,0},{2,1},{3,2},{4,3},{5,4},{6,5},{7,6},{8,15},{9,8},{10,9... | collective-permute-start | bytes 393224 | tf_op jit(solution)/shard_map/ppermute | solution.py:123
  163.4 10.6 %collective-permute-start.14 = (bf16[128,1024]{0,1:T(8,128)(2,1)S(1)}, bf16[128,1024]{0,1:T(8,128)(2,1)S(1)}, u32[]{:S(2)}, u32[]{:S(2)}) collective-permute-start(bf16[128,1024]{0,1:T(8,128)(2,1)S(1)} %add_convert_fusion.3), channel_id=1, source_target_pairs={{0,7},{1,0},{2,1},{3,2},{4,3},{5,4},{6,5},{7,6},{8,15},{9,8},{10,9... | collective-permute-start | bytes 786440 | tf_op jit(solution)/shard_map/ppermute | solution.py:123
  168.3 11.1 %collective-permute-start.10 = (bf16[128,1024]{0,1:T(8,128)(2,1)S(1)}, bf16[128,1024]{0,1:T(8,128)(2,1)S(1)}, u32[]{:S(2)}, u32[]{:S(2)}) collective-permute-start(bf16[128,1024]{0,1:T(8,128)(2,1)S(1)} %add_convert_fusion.6), channel_id=1, source_target_pairs={{0,1},{1,2},{2,3},{3,4},{4,5},{5,6},{6,7},{7,0},{8,9},{9,10},{10,1... | collective-permute-start | bytes 786440 | tf_op jit(solution)/shard_map/ppermute | solution.py:123
  174.0 10.4 %collective-permute-start.15 = (bf16[128,1024]{0,1:T(8,128)(2,1)S(1)}, bf16[128,1024]{0,1:T(8,128)(2,1)S(1)}, u32[]{:S(2)}, u32[]{:S(2)}) collective-permute-start(bf16[128,1024]{0,1:T(8,128)(2,1)S(1)} %add_convert_fusion.2), channel_id=1, source_target_pairs={{0,7},{1,0},{2,1},{3,2},{4,3},{5,4},{6,5},{7,6},{8,15},{9,8},{10,9... | collective-permute-start | bytes 786440 | tf_op jit(solution)/shard_map/ppermute | solution.py:123
  179.5 10.6 %collective-permute-start.11 = (bf16[128,1024]{0,1:T(8,128)(2,1)S(1)}, bf16[128,1024]{0,1:T(8,128)(2,1)S(1)}, u32[]{:S(2)}, u32[]{:S(2)}) collective-permute-start(bf16[128,1024]{0,1:T(8,128)(2,1)S(1)} %add_convert_fusion.5), channel_id=1, source_target_pairs={{0,1},{1,2},{2,3},{3,4},{4,5},{5,6},{6,7},{7,0},{8,9},{9,10},{10,1... | collective-permute-start | bytes 786440 | tf_op jit(solution)/shard_map/ppermute | solution.py:123
  184.5 9.9 %collective-permute-start.16 = (bf16[128,1024]{0,1:T(8,128)(2,1)S(1)}, bf16[128,1024]{0,1:T(8,128)(2,1)S(1)}, u32[]{:S(2)}, u32[]{:S(2)}) collective-permute-start(bf16[128,1024]{0,1:T(8,128)(2,1)S(1)} %add_convert_fusion.1), channel_id=1, source_target_pairs={{0,7},{1,0},{2,1},{3,2},{4,3},{5,4},{6,5},{7,6},{8,15},{9,8},{10,9... | collective-permute-start | bytes 786440 | tf_op jit(solution)/shard_map/ppermute | solution.py:123
  190.2 9.7 %collective-permute-start.12 = (bf16[128,1024]{0,1:T(8,128)(2,1)S(1)}, bf16[128,1024]{0,1:T(8,128)(2,1)S(1)}, u32[]{:S(2)}, u32[]{:S(2)}) collective-permute-start(bf16[128,1024]{0,1:T(8,128)(2,1)S(1)} %add_convert_fusion.4), channel_id=1, source_target_pairs={{0,1},{1,2},{2,3},{3,4},{4,5},{5,6},{6,7},{7,0},{8,9},{9,10},{10,1... | collective-permute-start | bytes 786440 | tf_op jit(solution)/shard_map/ppermute | solution.py:123
  200.0 5.0 %collective-permute-start.17 = (bf16[128,512]{0,1:T(8,128)(2,1)S(1)}, bf16[128,512]{0,1:T(8,128)(2,1)S(1)}, u32[]{:S(2)}, u32[]{:S(2)}) collective-permute-start(bf16[128,512]{0,1:T(8,128)(2,1)S(1)} %get-tuple-element.24), channel_id=1, source_target_pairs={{0,8},{8,0},{1,9},{9,1},{2,10},{10,2},{3,11},{11,3},{4,12},{12,4},... | collective-permute-start | bytes 393224 | tf_op jit(solution)/shard_map/ppermute | solution.py:127
Sparse Core Ops, SparseCore 0:
  9.4 44.1 all-gather.1

commit v8 on v7

--- a/solution.py
+++ b/solution.py
@@ -54,20 +54,20 @@
         [q_ref[here, h * HEAD : (h + 1) * HEAD] for h in range(heads)], axis=0
     )
     acc_ref[...] = jnp.zeros_like(acc_ref)
-    last = first // KEYS
+    stop = first + BLOCK
 
     def visit(i, carry):
         top, total = carry
-        block = last - i
-        offset = pl.multiple_of(block * KEYS, KEYS)
-        keys = kv_ref[pl.ds(offset, KEYS), :HEAD]
-        values = kv_ref[pl.ds(offset, KEYS), HEAD:]
+        limit = stop - i * KEYS
+        base = pl.multiple_of(jnp.maximum(limit - KEYS, 0), BLOCK)
+        keys = kv_ref[pl.ds(base, KEYS), :HEAD]
+        values = kv_ref[pl.ds(base, KEYS), HEAD:]
         scores = lax.dot_general(
             keys, query, (((1,), (1,)), ((), ())), preferred_element_type=jnp.float32
         )
-        base = block * KEYS
+        newest = jnp.minimum(row_pos, limit - 1) - base
         bias = jnp.where(
-            (key_row >= row_start - base) & (key_row <= row_pos - base),
+            (key_row >= row_start - base) & (key_row <= newest),
             jnp.float32(0.0),
             jnp.float32(NEG),
         )
@@ -85,11 +85,11 @@
         return new, total
 
     start = (jnp.full((1, rows), NEG, jnp.float32), jnp.zeros((1, rows), jnp.float32))
-    _, total = lax.fori_loop(0, last - lowest // KEYS + 1, visit, start)
+    _, total = lax.fori_loop(0, (stop - lowest + KEYS - 1) // KEYS, visit, start)
     scale = 1.0 / total
     for pair in range(heads // 2):
         lanes = slice(pair * HEAD, (pair + 1) * HEAD)
-        turned = (acc_ref[:, lanes] * scale[:, lanes]).T.astype(out_ref.dtype)
+        turned = (acc_ref[:, lanes] * scale[:, lanes]).astype(out_ref.dtype).T
         out_ref[:, 2 * pair * HEAD : (2 * pair + 1) * HEAD] = turned[:BLOCK]
         out_ref[:, (2 * pair + 1) * HEAD : (2 * pair + 2) * HEAD] = turned[BLOCK:]
 

time: 214 us -> 210 us (0.981)
  the two profiles are of different devices: /device:TPU:31 before, /device:TPU:1 now
where the time goes in v8:
time: 210 us; the launch traced here: 209 us
  starting transfers between devices  72.2 us (34%)
  blocking collectives  59.9 us (29%)
  waiting for transfers between devices  30.7 us (15%)
  Pallas kernels  20.5 us (10%)
  between operations  13.8 us (7%)
  matrix products  8.64 us (4%)
    psum x1, blocking collectives, local(): kv = lax.psum(partial_kv, ('y', 'core')).astype(jnp.bfloat16)  59.9 us
    ppermute x16, starting transfers between devices, shift(): return lax.ppermute(x, axis, [(i, (i + by) % RING) for i in range(RING)])  53.2 us
    ppermute x16, waiting for transfers between devices, shift(): return lax.ppermute(x, axis, [(i, (i + by) % RING) for i in range(RING)])  21.5 us
    pallas_call x1, Pallas kernels, attend(): pl.pallas_call(attend_kernel, out_shape=jax.ShapeDtypeStruct((total, widt...  20.5 us
    ppermute x2, starting transfers between devices, swap(): return lax.ppermute(x, 'core', [(0, 1), (1, 0)])  18.9 us
    all_gather x1, waiting for transfers between devices, local(): all_tokens = lax.all_gather(tokens, 'z', axis=0, tiled=True)  7.48 us
    dot_general x2, matrix products, local(): jnp.dot(attn, w, preferred_element_type=f32).astype(bf16)  4.33 us
  transfers between devices with their start and end apart: 19, of which 10 were waited for; matrix products, arithmetic and copies ran while one was open for 2% of the time, Pallas kernels for 0%

profile of v8, /device:TPU:1, one launch (start us, length us, event | category | flops | bytes accessed | tf_op | source)
XLA Modules:
  0.0 209.0 jit_solution(6568084358137174197)
XLA Ops:
  7.3 5.9 %collective-permute-start = (bf16[128,1024]{1,0:T(8,128)(2,1)}, bf16[128,1024]{1,0:T(8,128)(2,1)S(1)}, u32[]{:S(2)}, u32[]{:S(2)}) collective-permute-start(bf16[128,1024]{1,0:T(8,128)(2,1)} %refs_0_.1), channel_id=1, source_target_pairs={{0,112},{16,0},{32,16},{48,32},{64,48},{80,64},{96,80},{112,96},{1... | collective-permute-start | bytes 786440 | tf_op jit(solution)/shard_map/ppermute | solution.py:123
  13.2 1.9 collective-permute-start.3
  15.1 6.8 %collective-permute-start.8 = (bf16[1024,512]{1,0:T(8,128)(2,1)}, bf16[1024,512]{1,0:T(8,128)(2,1)S(1)}, u32[]{:S(2)}, u32[]{:S(2)}) collective-permute-start(bf16[1024,512]{1,0:T(8,128)(2,1)} %param.9), channel_id=1, source_target_pairs={{0,8},{8,0},{1,9},{9,1},{2,10},{10,2},{3,11},{11,3},{4,12},{12,4},... | collective-permute-start | bytes 3145736 | tf_op jit(solution)/shard_map/ppermute | solution.py:127
  21.9 2.9 %collective-permute-start.1 = (bf16[128,1024]{1,0:T(8,128)(2,1)S(1)}, bf16[128,1024]{1,0:T(8,128)(2,1)S(1)}, u32[]{:S(2)}, u32[]{:S(2)}) collective-permute-start(bf16[128,1024]{1,0:T(8,128)(2,1)S(1)} %collective-permute-done.refs_1_), channel_id=1, source_target_pairs={{0,112},{16,0},{32,16},{48,32},{64,48},{80,64},{96,80},{112,96},{1... | collective-permute-start | bytes 786440 | tf_op jit(solution)/shard_map/ppermute | solution.py:123
  24.8 2.4 %collective-permute-start.4 = (bf16[128,1024]{1,0:T(8,128)(2,1)S(1)}, bf16[128,1024]{1,0:T(8,128)(2,1)S(1)}, u32[]{:S(2)}, u32[]{:S(2)}) collective-permute-start(bf16[128,1024]{1,0:T(8,128)(2,1)S(1)} %collective-permute-done.3.refs_8_), channel_id=1, source_target_pairs={{0,16},{16,32},{32,48},{48,64},{64,80},{80,96},{96,112},{112,0},{1... | collective-permute-start | bytes 786440 | tf_op jit(solution)/shard_map/ppermute | solution.py:123
  27.2 3.8 %collective-permute-done.1.refs_2_ = bf16[128,1024]{1,0:T(8,128)(2,1)S(1)} collective-permute-done((bf16[128,1024]{1,0:T(8,128)(2,1)S(1)}, bf16[128,1024]{1,0:T(8,128)(2,1)S(1)}, u32[]{:S(2)}, u32[]{:S(2)}) %collective-permute-start.1) | collective-permute-done | bytes 262176 | tf_op jit(solution)/shard_map/ppermute | solution.py:123
  31.0 4.0 %collective-permute-start.2 = (bf16[128,1024]{1,0:T(8,128)(2,1)S(1)}, bf16[128,1024]{1,0:T(8,128)(2,1)S(1)}, u32[]{:S(2)}, u32[]{:S(2)}) collective-permute-start(bf16[128,1024]{1,0:T(8,128)(2,1)S(1)} %collective-permute-done.1.refs_2_), channel_id=1, source_target_pairs={{0,112},{16,0},{32,16},{48,32},{64,48},{80,64},{96,80},{112,96},{1... | collective-permute-start | bytes 786440 | tf_op jit(solution)/shard_map/ppermute | solution.py:123
  35.1 1.9 collective-permute-start.5
  37.7 1.6 collective-permute-done.2.refs_3_
  39.3 5.3 %collective-permute-start.7 = (bf16[64,1024]{1,0:T(8,128)(2,1)S(1)}, bf16[64,1024]{1,0:T(8,128)(2,1)}, u32[]{:S(2)}, u32[]{:S(2)}) collective-permute-start(bf16[64,1024]{1,0:T(8,128)(2,1)S(1)} %slice.78), channel_id=1, source_target_pairs={{0,112},{16,0},{32,16},{48,32},{64,48},{80,64},{96,80},{112,96},{1... | collective-permute-start | bytes 393224 | tf_op jit(solution)/shard_map/ppermute | solution.py:123
  45.4 1.9 collective-permute-start.6
  47.3 7.5 %all-gather.2.cloned.1.call-done = bf16[2048,512]{1,0:T(8,128)(2,1)} async-done(((bf16[256,512]{1,0:T(8,128)(2,1)}), bf16[2048,512]{1,0:T(8,128)(2,1)}) %all-gather.2.cloned.1.call-update) | async-done | bytes 2097168 | tf_op jit(solution)/shard_map/all_gather | solution.py:144
  54.8 2.3 %fusion.5 = f32[2048,256]{1,0:T(8,128)S(1)} fusion(bf16[2048,512]{1,0:T(8,128)(2,1)} %all-gather.2.cloned.1.call-done, bf16[512,256]{1,0:T(8,128)(2,1)S(1)} %copy-done), kind=kOutput, calls=%fused_computation.18 | convolution fusion | flops 536870912 | bytes 4456448 | tf_op jit(solution)/shard_map/dot_general | solution.py:147
  57.1 59.9 %all-reduce.3.refs_9_ = bf16[2048,256]{1,0:T(8,128)(2,1)} all-reduce(f32[2048,256]{1,0:T(8,128)S(1)} %fusion.5), channel_id=1, replica_groups=mesh['dp'=4,'y'=8,'core'=2,'z'=8] {'y','core'}, use_global_device_ids=true, to_apply=%region_0.0 | all-reduce | flops 524288 | bytes 3145728 | tf_op jit(solution)/shard_map/psum | solution.py:149
  117.0 20.5 %attend.1 = bf16[1024,1024]{1,0:T(8,128)(2,1)} custom-call(s32[3]{0:T(128)} %pad_add_fusion.ids, s32[8]{0:T(128)} %lengths.1, s32[32]{0:T(128)} %order.1, bf16[128,1024]{1,0:T(8,128)(2,1)} %refs_0_.1, bf16[128,1024]{1,0:T(8,128)(2,1)} %copy-done.5, bf16[128,1024]{1,0:T(8,128)(2,1)} %copy-done.7, bf16[128,1024]{1,0:T(8,128)(2,1)} %copy-done.3, ...), custom_call_target="tpu_custom_call" | custom-call | flops 4800000000 | bytes 6000000 | tf_op jit(solution)/shard_map/attend/pallas_call | solution.py:100
  137.5 1.5 convolution_convert_fusion.2
  139.0 3.0 %convolution_convert_fusion = bf16[1024,512]{0,1:T(8,128)(2,1)S(1)} fusion(bf16[1024,1024]{1,0:T(8,128)(2,1)} %attend.1, bf16[1024,512]{1,0:T(8,128)(2,1)S(1)} %collective-permute-done.8), kind=kOutput, calls=%fused_computation | convolution fusion | flops 1074266112 | bytes 4194304 | tf_op jit(solution)/shard_map/dot_general | solution.py:161
  142.6 1.3 convolution_convert_fusion.1
  143.9 2.9 %collective-permute-start.9 = (bf16[128,512]{0,1:T(8,128)(2,1)S(1)}, bf16[128,512]{0,1:T(8,128)(2,1)S(1)}, u32[]{:S(2)}, u32[]{:S(2)}) collective-permute-start(bf16[128,512]{0,1:T(8,128)(2,1)S(1)} %convolution_convert_fusion.3), channel_id=1, source_target_pairs={{0,1},{1,2},{2,3},{3,4},{4,5},{5,6},{6,7},{7,0},{8,9},{9,10},{10,1... | collective-permute-start | bytes 393224 | tf_op jit(solution)/shard_map/ppermute | solution.py:123
  146.8 3.6 %collective-permute-start.13 = (bf16[128,512]{0,1:T(8,128)(2,1)S(1)}, bf16[128,512]{0,1:T(8,128)(2,1)S(1)}, u32[]{:S(2)}, u32[]{:S(2)}) collective-permute-start(bf16[128,512]{0,1:T(8,128)(2,1)S(1)} %convolution_convert_fusion.2), channel_id=1, source_target_pairs={{0,7},{1,0},{2,1},{3,2},{4,3},{5,4},{6,5},{7,6},{8,15},{9,8},{10,9... | collective-permute-start | bytes 393224 | tf_op jit(solution)/shard_map/ppermute | solution.py:123
  150.8 1.7 collective-permute-done.13
  152.6 4.8 %collective-permute-start.14 = (bf16[128,1024]{0,1:T(8,128)(2,1)S(1)}, bf16[128,1024]{0,1:T(8,128)(2,1)S(1)}, u32[]{:S(2)}, u32[]{:S(2)}) collective-permute-start(bf16[128,1024]{0,1:T(8,128)(2,1)S(1)} %add_convert_fusion.3), channel_id=1, source_target_pairs={{0,7},{1,0},{2,1},{3,2},{4,3},{5,4},{6,5},{7,6},{8,15},{9,8},{10,9... | collective-permute-start | bytes 786440 | tf_op jit(solution)/shard_map/ppermute | solution.py:123
  157.4 1.9 collective-permute-start.10
  159.3 1.9 collective-permute-done.14
  161.3 5.0 %collective-permute-start.15 = (bf16[128,1024]{0,1:T(8,128)(2,1)S(1)}, bf16[128,1024]{0,1:T(8,128)(2,1)S(1)}, u32[]{:S(2)}, u32[]{:S(2)}) collective-permute-start(bf16[128,1024]{0,1:T(8,128)(2,1)S(1)} %add_convert_fusion.2), channel_id=1, source_target_pairs={{0,7},{1,0},{2,1},{3,2},{4,3},{5,4},{6,5},{7,6},{8,15},{9,8},{10,9... | collective-permute-start | bytes 786440 | tf_op jit(solution)/shard_map/ppermute | solution.py:123
  166.4 1.9 collective-permute-start.11
  168.3 3.1 %collective-permute-done.15 = bf16[128,1024]{0,1:T(8,128)(2,1)S(1)} collective-permute-done((bf16[128,1024]{0,1:T(8,128)(2,1)S(1)}, bf16[128,1024]{0,1:T(8,128)(2,1)S(1)}, u32[]{:S(2)}, u32[]{:S(2)}) %collective-permute-start.15) | collective-permute-done | bytes 262176 | tf_op jit(solution)/shard_map/ppermute | solution.py:123
  171.5 4.9 %collective-permute-start.16 = (bf16[128,1024]{0,1:T(8,128)(2,1)S(1)}, bf16[128,1024]{0,1:T(8,128)(2,1)S(1)}, u32[]{:S(2)}, u32[]{:S(2)}) collective-permute-start(bf16[128,1024]{0,1:T(8,128)(2,1)S(1)} %add_convert_fusion.1), channel_id=1, source_target_pairs={{0,7},{1,0},{2,1},{3,2},{4,3},{5,4},{6,5},{7,6},{8,15},{9,8},{10,9... | collective-permute-start | bytes 786440 | tf_op jit(solution)/shard_map/ppermute | solution.py:123
  176.7 1.9 collective-permute-start.12
  178.7 3.8 %collective-permute-done.16 = bf16[128,1024]{0,1:T(8,128)(2,1)S(1)} collective-permute-done((bf16[128,1024]{0,1:T(8,128)(2,1)S(1)}, bf16[128,1024]{0,1:T(8,128)(2,1)S(1)}, u32[]{:S(2)}, u32[]{:S(2)}) %collective-permute-start.16) | collective-permute-done | bytes 262176 | tf_op jit(solution)/shard_map/ppermute | solution.py:123
  182.5 5.4 %collective-permute-done.12 = bf16[128,1024]{0,1:T(8,128)(2,1)S(1)} collective-permute-done((bf16[128,1024]{0,1:T(8,128)(2,1)S(1)}, bf16[128,1024]{0,1:T(8,128)(2,1)S(1)}, u32[]{:S(2)}, u32[]{:S(2)}) %collective-permute-start.12) | collective-permute-done | bytes 262176 | tf_op jit(solution)/shard_map/ppermute | solution.py:123
  188.0 12.2 %collective-permute-start.17 = (bf16[128,512]{0,1:T(8,128)(2,1)S(1)}, bf16[128,512]{0,1:T(8,128)(2,1)S(1)}, u32[]{:S(2)}, u32[]{:S(2)}) collective-permute-start(bf16[128,512]{0,1:T(8,128)(2,1)S(1)} %get-tuple-element.24), channel_id=1, source_target_pairs={{0,8},{8,0},{1,9},{9,1},{2,10},{10,2},{3,11},{11,3},{4,12},{12,4},... | collective-permute-start | bytes 393224 | tf_op jit(solution)/shard_map/ppermute | solution.py:127
  (46 shorter events, 5.8 us)
Async XLA Ops:
  6.5 48.3 %copy-start = (bf16[512,256]{1,0:T(8,128)(2,1)S(1)}, bf16[512,256]{1,0:T(8,128)(2,1)}, u32[]{:S(2)}) copy-start(bf16[512,256]{1,0:T(8,128)(2,1)} %param.8) | copy-start | bytes 786436
  6.5 48.3 %all-gather.2.cloned.1.call-start = ((), (), s32[]{:S(2)}) async-start(), calls=%async_computation | async-start | bytes 2359296 | tf_op jit(solution)/shard_map/all_gather | solution.py:144
  7.3 14.6 %collective-permute-start = (bf16[128,1024]{1,0:T(8,128)(2,1)}, bf16[128,1024]{1,0:T(8,128)(2,1)S(1)}, u32[]{:S(2)}, u32[]{:S(2)}) collective-permute-start(bf16[128,1024]{1,0:T(8,128)(2,1)} %refs_0_.1), channel_id=1, source_target_pairs={{0,112},{16,0},{32,16},{48,32},{64,48},{80,64},{96,80},{112,96},{1... | collective-permute-start | bytes 786440 | tf_op jit(solution)/shard_map/ppermute | solution.py:123
  13.2 11.6 %collective-permute-start.3 = (bf16[128,1024]{1,0:T(8,128)(2,1)}, bf16[128,1024]{1,0:T(8,128)(2,1)S(1)}, u32[]{:S(2)}, u32[]{:S(2)}) collective-permute-start(bf16[128,1024]{1,0:T(8,128)(2,1)} %refs_0_.1), channel_id=1, source_target_pairs={{0,16},{16,32},{32,48},{48,64},{64,80},{80,96},{96,112},{112,0},{1... | collective-permute-start | bytes 786440 | tf_op jit(solution)/shard_map/ppermute | solution.py:123
  15.1 42.0 %collective-permute-start.8 = (bf16[1024,512]{1,0:T(8,128)(2,1)}, bf16[1024,512]{1,0:T(8,128)(2,1)S(1)}, u32[]{:S(2)}, u32[]{:S(2)}) collective-permute-start(bf16[1024,512]{1,0:T(8,128)(2,1)} %param.9), channel_id=1, source_target_pairs={{0,8},{8,0},{1,9},{9,1},{2,10},{10,2},{3,11},{11,3},{4,12},{12,4},... | collective-permute-start | bytes 3145736 | tf_op jit(solution)/shard_map/ppermute | solution.py:127
  21.9 13.2 %copy-start.5 = (bf16[128,1024]{1,0:T(8,128)(2,1)}, bf16[128,1024]{1,0:T(8,128)(2,1)S(1)}, u32[]{:S(2)}) copy-start(bf16[128,1024]{1,0:T(8,128)(2,1)S(1)} %collective-permute-done.refs_1_) | copy-start | bytes 786436
  21.9 9.1 %collective-permute-start.1 = (bf16[128,1024]{1,0:T(8,128)(2,1)S(1)}, bf16[128,1024]{1,0:T(8,128)(2,1)S(1)}, u32[]{:S(2)}, u32[]{:S(2)}) collective-permute-start(bf16[128,1024]{1,0:T(8,128)(2,1)S(1)} %collective-permute-done.refs_1_), channel_id=1, source_target_pairs={{0,112},{16,0},{32,16},{48,32},{64,48},{80,64},{96,80},{112,96},{1... | collective-permute-start | bytes 786440 | tf_op jit(solution)/shard_map/ppermute | solution.py:123
  24.8 10.3 %copy-start.6 = (bf16[128,1024]{1,0:T(8,128)(2,1)}, bf16[128,1024]{1,0:T(8,128)(2,1)S(1)}, u32[]{:S(2)}) copy-start(bf16[128,1024]{1,0:T(8,128)(2,1)S(1)} %collective-permute-done.3.refs_8_) | copy-start | bytes 786436
  24.8 10.3 %collective-permute-start.4 = (bf16[128,1024]{1,0:T(8,128)(2,1)S(1)}, bf16[128,1024]{1,0:T(8,128)(2,1)S(1)}, u32[]{:S(2)}, u32[]{:S(2)}) collective-permute-start(bf16[128,1024]{1,0:T(8,128)(2,1)S(1)} %collective-permute-done.3.refs_8_), channel_id=1, source_target_pairs={{0,16},{16,32},{32,48},{48,64},{64,80},{80,96},{96,112},{112,0},{1... | collective-permute-start | bytes 786440 | tf_op jit(solution)/shard_map/ppermute | solution.py:123
  31.0 16.3 %copy-start.7 = (bf16[128,1024]{1,0:T(8,128)(2,1)}, bf16[128,1024]{1,0:T(8,128)(2,1)S(1)}, u32[]{:S(2)}) copy-start(bf16[128,1024]{1,0:T(8,128)(2,1)S(1)} %collective-permute-done.1.refs_2_) | copy-start | bytes 786436
  31.0 8.3 %collective-permute-start.2 = (bf16[128,1024]{1,0:T(8,128)(2,1)S(1)}, bf16[128,1024]{1,0:T(8,128)(2,1)S(1)}, u32[]{:S(2)}, u32[]{:S(2)}) collective-permute-start(bf16[128,1024]{1,0:T(8,128)(2,1)S(1)} %collective-permute-done.1.refs_2_), channel_id=1, source_target_pairs={{0,112},{16,0},{32,16},{48,32},{64,48},{80,64},{96,80},{112,96},{1... | collective-permute-start | bytes 786440 | tf_op jit(solution)/shard_map/ppermute | solution.py:123
  35.1 12.2 %copy-start.8 = (bf16[128,1024]{1,0:T(8,128)(2,1)}, bf16[128,1024]{1,0:T(8,128)(2,1)S(1)}, u32[]{:S(2)}) copy-start(bf16[128,1024]{1,0:T(8,128)(2,1)S(1)} %collective-permute-done.4.refs_7_) | copy-start | bytes 786436
  35.1 9.5 %collective-permute-start.5 = (bf16[128,1024]{1,0:T(8,128)(2,1)S(1)}, bf16[128,1024]{1,0:T(8,128)(2,1)S(1)}, u32[]{:S(2)}, u32[]{:S(2)}) collective-permute-start(bf16[128,1024]{1,0:T(8,128)(2,1)S(1)} %collective-permute-done.4.refs_7_), channel_id=1, source_target_pairs={{0,16},{16,32},{32,48},{48,64},{64,80},{80,96},{96,112},{112,0},{1... | collective-permute-start | bytes 786440 | tf_op jit(solution)/shard_map/ppermute | solution.py:123
  39.3 8.0 %copy-start.3 = (bf16[128,1024]{1,0:T(8,128)(2,1)}, bf16[128,1024]{1,0:T(8,128)(2,1)S(1)}, u32[]{:S(2)}) copy-start(bf16[128,1024]{1,0:T(8,128)(2,1)S(1)} %collective-permute-done.2.refs_3_) | copy-start | bytes 786436
  39.3 77.7 %collective-permute-start.7 = (bf16[64,1024]{1,0:T(8,128)(2,1)S(1)}, bf16[64,1024]{1,0:T(8,128)(2,1)}, u32[]{:S(2)}, u32[]{:S(2)}) collective-permute-start(bf16[64,1024]{1,0:T(8,128)(2,1)S(1)} %slice.78), channel_id=1, source_target_pairs={{0,112},{16,0},{32,16},{48,32},{64,48},{80,64},{96,80},{112,96},{1... | collective-permute-start | bytes 393224 | tf_op jit(solution)/shard_map/ppermute | solution.py:123
  44.6 2.7 %copy-start.4 = (bf16[128,1024]{1,0:T(8,128)(2,1)}, bf16[128,1024]{1,0:T(8,128)(2,1)S(1)}, u32[]{:S(2)}) copy-start(bf16[128,1024]{1,0:T(8,128)(2,1)S(1)} %collective-permute-done.5.refs_6_) | copy-start | bytes 786436
  45.4 71.6 %collective-permute-start.6 = (bf16[64,1024]{1,0:T(8,128)(2,1)}, bf16[64,1024]{1,0:T(8,128)(2,1)}, u32[]{:S(2)}, u32[]{:S(2)}) collective-permute-start(bf16[64,1024]{1,0:T(8,128)(2,1)} %slice.77), channel_id=1, source_target_pairs={{0,16},{16,32},{32,48},{48,64},{64,80},{80,96},{96,112},{112,0},{1... | collective-permute-start | bytes 393224 | tf_op jit(solution)/shard_map/ppermute | solution.py:123
  138.9 3.1 %copy-start.1 = (bf16[1024,512]{1,0:T(8,128)(2,1)S(1)}, bf16[1024,512]{1,0:T(8,128)(2,1)}, u32[]{:S(2)}) copy-start(bf16[1024,512]{1,0:T(8,128)(2,1)} %param.9) | copy-start | bytes 3145732
  139.0 3.1 %copy-start.2 = (bf16[1024,1024]{1,0:T(8,128)(2,1)S(1)}, bf16[1024,1024]{1,0:T(8,128)(2,1)}, u32[]{:S(2)}) copy-start(bf16[1024,1024]{1,0:T(8,128)(2,1)} %attend.1) | copy-start | bytes 6291460
  143.9 13.5 %collective-permute-start.9 = (bf16[128,512]{0,1:T(8,128)(2,1)S(1)}, bf16[128,512]{0,1:T(8,128)(2,1)S(1)}, u32[]{:S(2)}, u32[]{:S(2)}) collective-permute-start(bf16[128,512]{0,1:T(8,128)(2,1)S(1)} %convolution_convert_fusion.3), channel_id=1, source_target_pairs={{0,1},{1,2},{2,3},{3,4},{4,5},{5,6},{6,7},{7,0},{8,9},{9,10},{10,1... | collective-permute-start | bytes 393224 | tf_op jit(solution)/shard_map/ppermute | solution.py:123
  146.8 5.7 %collective-permute-start.13 = (bf16[128,512]{0,1:T(8,128)(2,1)S(1)}, bf16[128,512]{0,1:T(8,128)(2,1)S(1)}, u32[]{:S(2)}, u32[]{:S(2)}) collective-permute-start(bf16[128,512]{0,1:T(8,128)(2,1)S(1)} %convolution_convert_fusion.2), channel_id=1, source_target_pairs={{0,7},{1,0},{2,1},{3,2},{4,3},{5,4},{6,5},{7,6},{8,15},{9,8},{10,9... | collective-permute-start | bytes 393224 | tf_op jit(solution)/shard_map/ppermute | solution.py:123
  152.6 8.7 %collective-permute-start.14 = (bf16[128,1024]{0,1:T(8,128)(2,1)S(1)}, bf16[128,1024]{0,1:T(8,128)(2,1)S(1)}, u32[]{:S(2)}, u32[]{:S(2)}) collective-permute-start(bf16[128,1024]{0,1:T(8,128)(2,1)S(1)} %add_convert_fusion.3), channel_id=1, source_target_pairs={{0,7},{1,0},{2,1},{3,2},{4,3},{5,4},{6,5},{7,6},{8,15},{9,8},{10,9... | collective-permute-start | bytes 786440 | tf_op jit(solution)/shard_map/ppermute | solution.py:123
  157.4 8.9 %collective-permute-start.10 = (bf16[128,1024]{0,1:T(8,128)(2,1)S(1)}, bf16[128,1024]{0,1:T(8,128)(2,1)S(1)}, u32[]{:S(2)}, u32[]{:S(2)}) collective-permute-start(bf16[128,1024]{0,1:T(8,128)(2,1)S(1)} %add_convert_fusion.6), channel_id=1, source_target_pairs={{0,1},{1,2},{2,3},{3,4},{4,5},{5,6},{6,7},{7,0},{8,9},{9,10},{10,1... | collective-permute-start | bytes 786440 | tf_op jit(solution)/shard_map/ppermute | solution.py:123
  161.3 10.2 %collective-permute-start.15 = (bf16[128,1024]{0,1:T(8,128)(2,1)S(1)}, bf16[128,1024]{0,1:T(8,128)(2,1)S(1)}, u32[]{:S(2)}, u32[]{:S(2)}) collective-permute-start(bf16[128,1024]{0,1:T(8,128)(2,1)S(1)} %add_convert_fusion.2), channel_id=1, source_target_pairs={{0,7},{1,0},{2,1},{3,2},{4,3},{5,4},{6,5},{7,6},{8,15},{9,8},{10,9... | collective-permute-start | bytes 786440 | tf_op jit(solution)/shard_map/ppermute | solution.py:123
  166.4 10.3 %collective-permute-start.11 = (bf16[128,1024]{0,1:T(8,128)(2,1)S(1)}, bf16[128,1024]{0,1:T(8,128)(2,1)S(1)}, u32[]{:S(2)}, u32[]{:S(2)}) collective-permute-start(bf16[128,1024]{0,1:T(8,128)(2,1)S(1)} %add_convert_fusion.5), channel_id=1, source_target_pairs={{0,1},{1,2},{2,3},{3,4},{4,5},{5,6},{6,7},{7,0},{8,9},{9,10},{10,1... | collective-permute-start | bytes 786440 | tf_op jit(solution)/shard_map/ppermute | solution.py:123
  171.5 11.0 %collective-permute-start.16 = (bf16[128,1024]{0,1:T(8,128)(2,1)S(1)}, bf16[128,1024]{0,1:T(8,128)(2,1)S(1)}, u32[]{:S(2)}, u32[]{:S(2)}) collective-permute-start(bf16[128,1024]{0,1:T(8,128)(2,1)S(1)} %add_convert_fusion.1), channel_id=1, source_target_pairs={{0,7},{1,0},{2,1},{3,2},{4,3},{5,4},{6,5},{7,6},{8,15},{9,8},{10,9... | collective-permute-start | bytes 786440 | tf_op jit(solution)/shard_map/ppermute | solution.py:123
  176.7 11.2 %collective-permute-start.12 = (bf16[128,1024]{0,1:T(8,128)(2,1)S(1)}, bf16[128,1024]{0,1:T(8,128)(2,1)S(1)}, u32[]{:S(2)}, u32[]{:S(2)}) collective-permute-start(bf16[128,1024]{0,1:T(8,128)(2,1)S(1)} %add_convert_fusion.4), channel_id=1, source_target_pairs={{0,1},{1,2},{2,3},{3,4},{4,5},{5,6},{6,7},{7,0},{8,9},{9,10},{10,1... | collective-permute-start | bytes 786440 | tf_op jit(solution)/shard_map/ppermute | solution.py:123
  188.0 13.1 %collective-permute-start.17 = (bf16[128,512]{0,1:T(8,128)(2,1)S(1)}, bf16[128,512]{0,1:T(8,128)(2,1)S(1)}, u32[]{:S(2)}, u32[]{:S(2)}) collective-permute-start(bf16[128,512]{0,1:T(8,128)(2,1)S(1)} %get-tuple-element.24), channel_id=1, source_target_pairs={{0,8},{8,0},{1,9},{9,1},{2,10},{10,2},{3,11},{11,3},{4,12},{12,4},... | collective-permute-start | bytes 393224 | tf_op jit(solution)/shard_map/ppermute | solution.py:127
Sparse Core Ops, SparseCore 0:
  9.4 45.3 all-gather.1

commit v9 on v8

--- a/solution.py
+++ b/solution.py
@@ -1,3 +1,4 @@
+import functools
 import math
 
 import jax
@@ -16,28 +17,28 @@
 EXP_SCALE = math.log2(math.e) / math.sqrt(HEAD)
 
 
-def attend_kernel(ids, lengths, order, *refs):
+def attend_kernel(half, from_self, ids, lengths, order, *refs):
     *pieces, kv_ref, out_ref, acc_ref, q_ref, sems = refs
     z, core = ids[0], ids[1]
     step = pl.program_id(0)
-    owner = (z + step // 2) % RING
-    first = order[(owner * 2 + core) * 2 + step % 2] * BLOCK
+    owner = (z + step) % RING if from_self else step
+    first = order[(owner * 2 + core) * 2 + half] * BLOCK
     heads = q_ref.shape[1] // HEAD
     rows = BLOCK * heads
 
     @pl.when(step == 0)
     def _():
-        copies, place = [], 0
+        copies = []
         for i, piece in enumerate(pieces):
-            here = q_ref.at[pl.ds(place, piece.shape[0])]
-            copies.append(pltpu.make_async_copy(piece, here, sems.at[i]))
-            place += piece.shape[0]
+            rows_here = pl.ds(half * BLOCK if piece.shape[0] > BLOCK else 0, BLOCK)
+            target = q_ref.at[pl.ds(i * BLOCK, BLOCK)]
+            copies.append(pltpu.make_async_copy(piece.at[rows_here], target, sems.at[i]))
         for copy in copies:
             copy.start()
         for copy in copies:
             copy.wait()
 
-    near = (owner - ids[2] + RING) % RING * 2 + step % 2
+    near = (owner - ids[2] + RING) % RING
     here = pl.ds(pl.multiple_of(near * BLOCK, BLOCK), BLOCK)
 
     row_pos = first + lax.broadcasted_iota(jnp.int32, (1, HEAD), 1) % BLOCK
@@ -94,11 +95,11 @@
         out_ref[:, (2 * pair + 1) * HEAD : (2 * pair + 2) * HEAD] = turned[BLOCK:]
 
 
-def attend(ids, lengths, order, pieces, kv):
+def attend(half, from_self, ids, lengths, order, pieces, kv):
     width = pieces[0].shape[1]
-    total = sum(piece.shape[0] for piece in pieces)
+    total = len(pieces) * BLOCK
     return pl.pallas_call(
-        attend_kernel,
+        functools.partial(attend_kernel, half, from_self),
         out_shape=jax.ShapeDtypeStruct((total, width), jnp.bfloat16),
         grid_spec=pltpu.PrefetchScalarGridSpec(
             num_scalar_prefetch=3,
@@ -113,7 +114,7 @@
             ],
         ),
         cost_estimate=pl.CostEstimate(
-            flops=4_800_000_000, bytes_accessed=6_000_000, transcendentals=5_000_000
+            flops=2_400_000_000, bytes_accessed=4_000_000, transcendentals=2_500_000
         ),
         name="attend",
     )(ids, lengths, order, *pieces, kv)
@@ -135,7 +136,7 @@
         downs.append(shift(downs[-1], axis, 1))
     top = shift(downs[3][:half], axis, 1)
     bottom = shift(ups[3][half:], axis, -1)
-    return [*ups, top, bottom, *downs[:0:-1]]
+    return [[*ups, far, *downs[:0:-1]] for far in (top, bottom)]
 
 
 def local(tokens, queries, key_value_weight, out_weight, doc_lengths, block_order):
@@ -149,17 +150,23 @@
     kv = lax.psum(partial_kv, ("y", "core")).astype(jnp.bfloat16)
 
     f32, bf16 = jnp.float32, jnp.bfloat16
-    rows, width = queries.shape[0], out_weight.shape[1]
-
-    attn = attend(ids, doc_lengths, block_order, all_queries, kv)
+    rows, width = BLOCK, out_weight.shape[1]
+
+    weights = (out_weight, other_weight)
+    early = attend(0, False, ids, doc_lengths, block_order, all_queries[0], kv)
+    early_out = jnp.concatenate(
+        [jnp.dot(early, w, preferred_element_type=f32).astype(bf16) for w in weights], axis=1
+    )
+    early_sum = lax.psum_scatter(early_out, "z", scatter_dimension=0, tiled=True)
+    attn = attend(1, True, ids, doc_lengths, block_order, all_queries[1], kv)
     far = slice(4 * rows, 5 * rows)
     first = [
         jnp.dot(attn[far], w, preferred_element_type=f32).astype(bf16)
-        for w in (out_weight, other_weight)
+        for w in weights
     ]
     out = [
         jnp.dot(attn, w, preferred_element_type=f32).astype(bf16)
-        for w in (out_weight, other_weight)
+        for w in weights
     ]
 
     def product(step):
@@ -173,6 +180,7 @@
         up = shift((product(step) + up.astype(f32)).astype(bf16), "z", 1)
         down = shift((product(RING - step) + down.astype(f32)).astype(bf16), "z", -1)
     total = (product(0) + up.astype(f32) + down.astype(f32)).astype(bf16)
+    total = jnp.concatenate([early_sum, total], axis=0)
     mine, theirs = total[:, :width], swap(total[:, width:])
     return jnp.where(
         core == 0,

time: 210 us -> 212 us (level)
  starting transfers between devices: 72.2 us -> 67.2 us
  matrix products: 8.64 us -> 12.8 us
  Pallas kernels: 20.5 us -> 24.1 us
  waiting for transfers between devices: 30.7 us -> 28.3 us
    reduce_scatter x0 -> x1, waiting for transfers between devices: none -> 4.48 us  [local(): lax.psum_scatter(early_out, 'z', scatter_dimension=0, tiled=True)]
    dot_general x0 -> x2, matrix products: none -> 4.43 us  [local(): jnp.dot(early, w, preferred_element_type=f32).astype(bf16)]
    ppermute x2, starting transfers between devices: 18.9 us -> 14.5 us  [swap(): return lax.ppermute(x, 'core', [(0, 1), (1, 0)])]
    ppermute x16, waiting for transfers between devices: 21.5 us -> 17.7 us  [shift(): return lax.ppermute(x, axis, [(i, (i + by) % RING) for i in range(RING)])]
    pallas_call x1 -> x2, Pallas kernels: 20.5 us -> 24.1 us  [attend(): pl.pallas_call(functools.partial(attend_kernel, half, from_self), out_sha...]
    all_gather x1, waiting for transfers between devices: 7.48 us -> 4.45 us  [local(): all_tokens = lax.all_gather(tokens, 'z', axis=0, tiled=True)]
  transfers between devices with their start and end apart: 19 -> 20, of which waited for: 10 -> 9; matrix products, arithmetic and copies ran while one was open for 2% -> 5% of each run, Pallas kernels for 0% -> 6%
where the time goes in v9:
time: 212 us; the launch traced here: 211 us
  starting transfers between devices  67.2 us (32%)
  blocking collectives  60.1 us (28%)
  waiting for transfers between devices  28.3 us (13%)
  Pallas kernels  24.1 us (11%)
  between operations  13.9 us (7%)
  matrix products  12.8 us (6%)
  other arithmetic  2.57 us (1%)
  local copies, waits for them, and re-layouts  2.18 us (1%)
    psum x1, blocking collectives, local(): kv = lax.psum(partial_kv, ('y', 'core')).astype(jnp.bfloat16)  60.1 us
    ppermute x16, starting transfers between devices, shift(): return lax.ppermute(x, axis, [(i, (i + by) % RING) for i in range(RING)])  52.7 us
    pallas_call x2, Pallas kernels, attend(): pl.pallas_call(functools.partial(attend_kernel, half, from_self), out_sha...  24.1 us
    ppermute x16, waiting for transfers between devices, shift(): return lax.ppermute(x, axis, [(i, (i + by) % RING) for i in range(RING)])  17.7 us
    ppermute x2, starting transfers between devices, swap(): return lax.ppermute(x, 'core', [(0, 1), (1, 0)])  14.5 us
    reduce_scatter x1, waiting for transfers between devices, local(): lax.psum_scatter(early_out, 'z', scatter_dimension=0, tiled=True)  4.48 us
    all_gather x1, waiting for transfers between devices, local(): all_tokens = lax.all_gather(tokens, 'z', axis=0, tiled=True)  4.45 us
    dot_general x2, matrix products, local(): jnp.dot(early, w, preferred_element_type=f32).astype(bf16)  4.43 us
  transfers between devices with their start and end apart: 20, of which 9 were waited for; matrix products, arithmetic and copies ran while one was open for 5% of the time, Pallas kernels for 6%

profile of v9, /device:TPU:1, one launch (start us, length us, event | category | flops | bytes accessed | tf_op | source)
XLA Modules:
  0.0 211.1 jit_solution(11109237450127937524)
XLA Ops:
  7.3 4.0 %collective-permute-start.3 = (bf16[128,1024]{1,0:T(8,128)(2,1)}, bf16[128,1024]{1,0:T(8,128)(2,1)S(1)}, u32[]{:S(2)}, u32[]{:S(2)}) collective-permute-start(bf16[128,1024]{1,0:T(8,128)(2,1)} %refs_0_.3), channel_id=1, source_target_pairs={{0,16},{16,32},{32,48},{48,64},{64,80},{80,96},{96,112},{112,0},{1... | collective-permute-start | bytes 786440 | tf_op jit(solution)/shard_map/ppermute | solution.py:124
  11.3 3.8 %collective-permute-start = (bf16[128,1024]{1,0:T(8,128)(2,1)}, bf16[128,1024]{1,0:T(8,128)(2,1)S(1)}, u32[]{:S(2)}, u32[]{:S(2)}) collective-permute-start(bf16[128,1024]{1,0:T(8,128)(2,1)} %refs_0_.3), channel_id=1, source_target_pairs={{0,112},{16,0},{32,16},{48,32},{64,48},{80,64},{96,80},{112,96},{1... | collective-permute-start | bytes 786440 | tf_op jit(solution)/shard_map/ppermute | solution.py:124
  15.2 8.0 %collective-permute-start.7 = (bf16[1024,512]{1,0:T(8,128)(2,1)}, bf16[1024,512]{1,0:T(8,128)(2,1)S(1)}, u32[]{:S(2)}, u32[]{:S(2)}) collective-permute-start(bf16[1024,512]{1,0:T(8,128)(2,1)} %param.9), channel_id=1, source_target_pairs={{0,8},{8,0},{1,9},{9,1},{2,10},{10,2},{3,11},{11,3},{4,12},{12,4},... | collective-permute-start | bytes 3145736 | tf_op jit(solution)/shard_map/ppermute | solution.py:128
  23.2 1.9 collective-permute-start.4
  25.1 4.6 %collective-permute-start.1 = (bf16[128,1024]{1,0:T(8,128)(2,1)S(1)}, bf16[128,1024]{1,0:T(8,128)(2,1)S(1)}, u32[]{:S(2)}, u32[]{:S(2)}) collective-permute-start(bf16[128,1024]{1,0:T(8,128)(2,1)S(1)} %collective-permute-done.refs_1_), channel_id=1, source_target_pairs={{0,112},{16,0},{32,16},{48,32},{64,48},{80,64},{96,80},{112,96},{1... | collective-permute-start | bytes 786440 | tf_op jit(solution)/shard_map/ppermute | solution.py:124
  29.7 3.8 %collective-permute-done.4.refs_6_ = bf16[128,1024]{1,0:T(8,128)(2,1)S(1)} collective-permute-done((bf16[128,1024]{1,0:T(8,128)(2,1)S(1)}, bf16[128,1024]{1,0:T(8,128)(2,1)S(1)}, u32[]{:S(2)}, u32[]{:S(2)}) %collective-permute-start.4) | collective-permute-done | bytes 262176 | tf_op jit(solution)/shard_map/ppermute | solution.py:124
  33.5 1.9 collective-permute-start.5
  35.4 4.6 %collective-permute-start.2 = (bf16[128,1024]{1,0:T(8,128)(2,1)S(1)}, bf16[128,1024]{1,0:T(8,128)(2,1)S(1)}, u32[]{:S(2)}, u32[]{:S(2)}) collective-permute-start(bf16[128,1024]{1,0:T(8,128)(2,1)S(1)} %collective-permute-done.1.refs_2_), channel_id=1, source_target_pairs={{0,112},{16,0},{32,16},{48,32},{64,48},{80,64},{96,80},{112,96},{1... | collective-permute-start | bytes 786440 | tf_op jit(solution)/shard_map/ppermute | solution.py:124
  40.6 2.4 %collective-permute-done.5.refs_5_ = bf16[128,1024]{1,0:T(8,128)(2,1)S(1)} collective-permute-done((bf16[128,1024]{1,0:T(8,128)(2,1)S(1)}, bf16[128,1024]{1,0:T(8,128)(2,1)S(1)}, u32[]{:S(2)}, u32[]{:S(2)}) %collective-permute-start.5) | collective-permute-done | bytes 262176 | tf_op jit(solution)/shard_map/ppermute | solution.py:124
  43.7 1.9 collective-permute-start.6
  45.7 4.6 %collective-permute-start.8 = (bf16[64,1024]{1,0:T(8,128)(2,1)S(1)}, bf16[64,1024]{1,0:T(8,128)(2,1)}, u32[]{:S(2)}, u32[]{:S(2)}) collective-permute-start(bf16[64,1024]{1,0:T(8,128)(2,1)S(1)} %slice.78), channel_id=1, source_target_pairs={{0,112},{16,0},{32,16},{48,32},{64,48},{80,64},{96,80},{112,96},{1... | collective-permute-start | bytes 393224 | tf_op jit(solution)/shard_map/ppermute | solution.py:124
  50.3 4.4 %all-gather.2.cloned.1.call-done = bf16[2048,512]{1,0:T(8,128)(2,1)} async-done(((bf16[256,512]{1,0:T(8,128)(2,1)}), bf16[2048,512]{1,0:T(8,128)(2,1)}) %all-gather.2.cloned.1.call-update) | async-done | bytes 2097168 | tf_op jit(solution)/shard_map/all_gather | solution.py:145
  54.7 2.3 %fusion.5 = f32[2048,256]{1,0:T(8,128)S(1)} fusion(bf16[2048,512]{1,0:T(8,128)(2,1)} %all-gather.2.cloned.1.call-done, bf16[512,256]{1,0:T(8,128)(2,1)S(1)} %copy-done), kind=kOutput, calls=%fused_computation.24 | convolution fusion | flops 536870912 | bytes 4456448 | tf_op jit(solution)/shard_map/dot_general | solution.py:148
  57.1 60.1 %all-reduce.3.refs_8_ = bf16[2048,256]{1,0:T(8,128)(2,1)} all-reduce(f32[2048,256]{1,0:T(8,128)S(1)} %fusion.5), channel_id=1, replica_groups=mesh['dp'=4,'y'=8,'core'=2,'z'=8] {'y','core'}, use_global_device_ids=true, to_apply=%region_0.0 | all-reduce | flops 524288 | bytes 3145728 | tf_op jit(solution)/shard_map/psum | solution.py:150
  117.2 12.3 %attend.2 = bf16[512,1024]{1,0:T(8,128)(2,1)} custom-call(s32[3]{0:T(128)} %pad_add_fusion.ids, s32[8]{0:T(128)} %lengths.3, s32[32]{0:T(128)} %order.3, bf16[128,1024]{1,0:T(8,128)(2,1)} %refs_0_.3, bf16[128,1024]{1,0:T(8,128)(2,1)} %copy-done.9, bf16[128,1024]{1,0:T(8,128)(2,1)} %copy-done.11, bf16[128,1024]{1,0:T(8,128)(2,1)} %copy-done.7, ...), custom_call_target="tpu_custom_call" | custom-call | flops 2400000000 | bytes 4000000 | tf_op jit(solution)/shard_map/attend/pallas_call | solution.py:101
  129.5 2.9 %convolution_convert_fusion.3 = bf16[512,512]{0,1:T(8,128)(2,1)} fusion(bf16[512,1024]{1,0:T(8,128)(2,1)} %attend.2, bf16[1024,512]{1,0:T(8,128)(2,1)S(1)} %copy-done.1), kind=kOutput, calls=%fused_computation.3 | convolution fusion | flops 537133056 | bytes 2621440 | tf_op jit(solution)/shard_map/dot_general | solution.py:158
  132.4 1.6 convolution_convert_fusion.2
  134.0 11.8 %attend.3 = bf16[512,1024]{1,0:T(8,128)(2,1)} custom-call(s32[3]{0:T(128)} %pad_add_fusion.ids, s32[8]{0:T(128)} %lengths.3, s32[32]{0:T(128)} %order.3, bf16[128,1024]{1,0:T(8,128)(2,1)} %refs_0_.3, bf16[128,1024]{1,0:T(8,128)(2,1)} %copy-done.9, bf16[128,1024]{1,0:T(8,128)(2,1)} %copy-done.11, bf16[128,1024]{1,0:T(8,128)(2,1)} %copy-done.7, ...), custom_call_target="tpu_custom_call" | custom-call | flops 2400000000 | bytes 4000000 | tf_op jit(solution)/shard_map/attend/pallas_call | solution.py:101
  145.8 2.8 %convolution_convert_fusion.1 = bf16[512,512]{1,0:T(8,128)(2,1)} fusion(bf16[512,1024]{1,0:T(8,128)(2,1)} %attend.3, bf16[1024,512]{1,0:T(8,128)(2,1)S(1)} %copy-done.1), kind=kOutput, calls=%fused_computation.1 | convolution fusion | flops 537133056 | bytes 2621440 | tf_op jit(solution)/shard_map/dot_general | solution.py:168
  152.6 3.6 %collective-permute-start.13 = (bf16[64,512]{1,0:T(8,128)(2,1)S(1)}, bf16[64,512]{1,0:T(8,128)(2,1)S(1)}, u32[]{:S(2)}, u32[]{:S(2)}) collective-permute-start(bf16[64,512]{1,0:T(8,128)(2,1)S(1)} %convolution_convert_fusion.4), channel_id=1, source_target_pairs={{0,7},{1,0},{2,1},{3,2},{4,3},{5,4},{6,5},{7,6},{8,15},{9,8},{10,9... | collective-permute-start | bytes 196616 | tf_op jit(solution)/shard_map/ppermute | solution.py:124
  156.2 1.9 collective-permute-start.9
  159.0 4.6 %collective-permute-start.14 = (bf16[64,1024]{1,0:T(8,128)(2,1)S(1)}, bf16[64,1024]{1,0:T(8,128)(2,1)S(1)}, u32[]{:S(2)}, u32[]{:S(2)}) collective-permute-start(bf16[64,1024]{1,0:T(8,128)(2,1)S(1)} %add_convert_fusion.3), channel_id=1, source_target_pairs={{0,7},{1,0},{2,1},{3,2},{4,3},{5,4},{6,5},{7,6},{8,15},{9,8},{10,9... | collective-permute-start | bytes 393224 | tf_op jit(solution)/shard_map/ppermute | solution.py:124
  163.6 1.9 collective-permute-start.10
  165.6 4.9 %collective-permute-start.15 = (bf16[64,1024]{1,0:T(8,128)(2,1)S(1)}, bf16[64,1024]{1,0:T(8,128)(2,1)S(1)}, u32[]{:S(2)}, u32[]{:S(2)}) collective-permute-start(bf16[64,1024]{1,0:T(8,128)(2,1)S(1)} %add_convert_fusion.2), channel_id=1, source_target_pairs={{0,7},{1,0},{2,1},{3,2},{4,3},{5,4},{6,5},{7,6},{8,15},{9,8},{10,9... | collective-permute-start | bytes 393224 | tf_op jit(solution)/shard_map/ppermute | solution.py:124
  170.6 1.9 collective-permute-start.11
  172.5 1.5 collective-permute-done.15
  174.1 4.6 %collective-permute-start.16 = (bf16[64,1024]{1,0:T(8,128)(2,1)S(1)}, bf16[64,1024]{1,0:T(8,128)(2,1)S(1)}, u32[]{:S(2)}, u32[]{:S(2)}) collective-permute-start(bf16[64,1024]{1,0:T(8,128)(2,1)S(1)} %add_convert_fusion.1), channel_id=1, source_target_pairs={{0,7},{1,0},{2,1},{3,2},{4,3},{5,4},{6,5},{7,6},{8,15},{9,8},{10,9... | collective-permute-start | bytes 393224 | tf_op jit(solution)/shard_map/ppermute | solution.py:124
  178.6 1.4 collective-permute-done.11
  180.1 1.9 collective-permute-start.12
  182.7 7.8 %collective-permute-done.12 = bf16[64,1024]{1,0:T(8,128)(2,1)S(1)} collective-permute-done((bf16[64,1024]{1,0:T(8,128)(2,1)S(1)}, bf16[64,1024]{1,0:T(8,128)(2,1)S(1)}, u32[]{:S(2)}, u32[]{:S(2)}) %collective-permute-start.12) | collective-permute-done | bytes 131104 | tf_op jit(solution)/shard_map/ppermute | solution.py:124
  190.6 4.5 %reduce-scatter.4.cloned.1.call-done = bf16[64,1024]{1,0:T(8,128)(2,1)} async-done(((bf16[512,1024]{1,0:T(8,128)(2,1)}), bf16[64,1024]{1,0:T(8,128)(2,1)}) %reduce-scatter.4.cloned.1.call-update) | async-done | bytes 131088 | tf_op jit(solution)/shard_map/reduce_scatter | solution.py:160
  196.0 6.6 %collective-permute-start.17 = (bf16[128,512]{1,0:T(8,128)(2,1)S(1)}, bf16[128,512]{1,0:T(8,128)(2,1)S(1)}, u32[]{:S(2)}, u32[]{:S(2)}) collective-permute-start(bf16[128,512]{1,0:T(8,128)(2,1)S(1)} %get-tuple-element.24), channel_id=1, source_target_pairs={{0,8},{8,0},{1,9},{9,1},{2,10},{10,2},{3,11},{11,3},{4,12},{12,4},... | collective-permute-start | bytes 393224 | tf_op jit(solution)/shard_map/ppermute | solution.py:128
  (61 shorter events, 10.5 us)
Async XLA Ops:
  6.5 48.2 %copy-start = (bf16[512,256]{1,0:T(8,128)(2,1)S(1)}, bf16[512,256]{1,0:T(8,128)(2,1)}, u32[]{:S(2)}) copy-start(bf16[512,256]{1,0:T(8,128)(2,1)} %param.8) | copy-start | bytes 786436
  6.5 48.2 %all-gather.2.cloned.1.call-start = ((), (), s32[]{:S(2)}) async-start(), calls=%async_computation.1 | async-start | bytes 2359296 | tf_op jit(solution)/shard_map/all_gather | solution.py:145
  7.3 187.8 %reduce-scatter.4.cloned.1.call-start = ((), (), s32[]{:S(2)}) async-start(), calls=%async_computation.2 | async-start | bytes 1179648 | tf_op jit(solution)/shard_map/reduce_scatter | solution.py:160
  7.3 15.8 %collective-permute-start.3 = (bf16[128,1024]{1,0:T(8,128)(2,1)}, bf16[128,1024]{1,0:T(8,128)(2,1)S(1)}, u32[]{:S(2)}, u32[]{:S(2)}) collective-permute-start(bf16[128,1024]{1,0:T(8,128)(2,1)} %refs_0_.3), channel_id=1, source_target_pairs={{0,16},{16,32},{32,48},{48,64},{64,80},{80,96},{96,112},{112,0},{1... | collective-permute-start | bytes 786440 | tf_op jit(solution)/shard_map/ppermute | solution.py:124
  11.3 13.7 %collective-permute-start = (bf16[128,1024]{1,0:T(8,128)(2,1)}, bf16[128,1024]{1,0:T(8,128)(2,1)S(1)}, u32[]{:S(2)}, u32[]{:S(2)}) collective-permute-start(bf16[128,1024]{1,0:T(8,128)(2,1)} %refs_0_.3), channel_id=1, source_target_pairs={{0,112},{16,0},{32,16},{48,32},{64,48},{80,64},{96,80},{112,96},{1... | collective-permute-start | bytes 786440 | tf_op jit(solution)/shard_map/ppermute | solution.py:124
  15.2 41.9 %collective-permute-start.7 = (bf16[1024,512]{1,0:T(8,128)(2,1)}, bf16[1024,512]{1,0:T(8,128)(2,1)S(1)}, u32[]{:S(2)}, u32[]{:S(2)}) collective-permute-start(bf16[1024,512]{1,0:T(8,128)(2,1)} %param.9), channel_id=1, source_target_pairs={{0,8},{8,0},{1,9},{9,1},{2,10},{10,2},{3,11},{11,3},{4,12},{12,4},... | collective-permute-start | bytes 3145736 | tf_op jit(solution)/shard_map/ppermute | solution.py:128
  23.1 12.2 %copy-start.8 = (bf16[128,1024]{1,0:T(8,128)(2,1)}, bf16[128,1024]{1,0:T(8,128)(2,1)S(1)}, u32[]{:S(2)}) copy-start(bf16[128,1024]{1,0:T(8,128)(2,1)S(1)} %collective-permute-done.3.refs_7_) | copy-start | bytes 786436
  23.2 10.3 %collective-permute-start.4 = (bf16[128,1024]{1,0:T(8,128)(2,1)S(1)}, bf16[128,1024]{1,0:T(8,128)(2,1)S(1)}, u32[]{:S(2)}, u32[]{:S(2)}) collective-permute-start(bf16[128,1024]{1,0:T(8,128)(2,1)S(1)} %collective-permute-done.3.refs_7_), channel_id=1, source_target_pairs={{0,16},{16,32},{32,48},{48,64},{64,80},{80,96},{96,112},{112,0},{1... | collective-permute-start | bytes 786440 | tf_op jit(solution)/shard_map/ppermute | solution.py:124
  25.1 10.3 %copy-start.9 = (bf16[128,1024]{1,0:T(8,128)(2,1)}, bf16[128,1024]{1,0:T(8,128)(2,1)S(1)}, u32[]{:S(2)}) copy-start(bf16[128,1024]{1,0:T(8,128)(2,1)S(1)} %collective-permute-done.refs_1_) | copy-start | bytes 786436
  25.1 10.3 %collective-permute-start.1 = (bf16[128,1024]{1,0:T(8,128)(2,1)S(1)}, bf16[128,1024]{1,0:T(8,128)(2,1)S(1)}, u32[]{:S(2)}, u32[]{:S(2)}) collective-permute-start(bf16[128,1024]{1,0:T(8,128)(2,1)S(1)} %collective-permute-done.refs_1_), channel_id=1, source_target_pairs={{0,112},{16,0},{32,16},{48,32},{64,48},{80,64},{96,80},{112,96},{1... | collective-permute-start | bytes 786440 | tf_op jit(solution)/shard_map/ppermute | solution.py:124
  33.5 16.8 %copy-start.10 = (bf16[128,1024]{1,0:T(8,128)(2,1)}, bf16[128,1024]{1,0:T(8,128)(2,1)S(1)}, u32[]{:S(2)}) copy-start(bf16[128,1024]{1,0:T(8,128)(2,1)S(1)} %collective-permute-done.4.refs_6_) | copy-start | bytes 786436
  33.5 9.5 %collective-permute-start.5 = (bf16[128,1024]{1,0:T(8,128)(2,1)S(1)}, bf16[128,1024]{1,0:T(8,128)(2,1)S(1)}, u32[]{:S(2)}, u32[]{:S(2)}) collective-permute-start(bf16[128,1024]{1,0:T(8,128)(2,1)S(1)} %collective-permute-done.4.refs_6_), channel_id=1, source_target_pairs={{0,16},{16,32},{32,48},{48,64},{64,80},{80,96},{96,112},{112,0},{1... | collective-permute-start | bytes 786440 | tf_op jit(solution)/shard_map/ppermute | solution.py:124
  35.4 14.9 %copy-start.11 = (bf16[128,1024]{1,0:T(8,128)(2,1)}, bf16[128,1024]{1,0:T(8,128)(2,1)S(1)}, u32[]{:S(2)}) copy-start(bf16[128,1024]{1,0:T(8,128)(2,1)S(1)} %collective-permute-done.1.refs_2_) | copy-start | bytes 786436
  35.4 10.2 %collective-permute-start.2 = (bf16[128,1024]{1,0:T(8,128)(2,1)S(1)}, bf16[128,1024]{1,0:T(8,128)(2,1)S(1)}, u32[]{:S(2)}, u32[]{:S(2)}) collective-permute-start(bf16[128,1024]{1,0:T(8,128)(2,1)S(1)} %collective-permute-done.1.refs_2_), channel_id=1, source_target_pairs={{0,112},{16,0},{32,16},{48,32},{64,48},{80,64},{96,80},{112,96},{1... | collective-permute-start | bytes 786440 | tf_op jit(solution)/shard_map/ppermute | solution.py:124
  43.0 7.3 %copy-start.6 = (bf16[128,1024]{1,0:T(8,128)(2,1)}, bf16[128,1024]{1,0:T(8,128)(2,1)S(1)}, u32[]{:S(2)}) copy-start(bf16[128,1024]{1,0:T(8,128)(2,1)S(1)} %collective-permute-done.5.refs_5_) | copy-start | bytes 786436
  43.7 73.4 %collective-permute-start.6 = (bf16[64,1024]{1,0:T(8,128)(2,1)}, bf16[64,1024]{1,0:T(8,128)(2,1)}, u32[]{:S(2)}, u32[]{:S(2)}) collective-permute-start(bf16[64,1024]{1,0:T(8,128)(2,1)} %slice.77), channel_id=1, source_target_pairs={{0,16},{16,32},{32,48},{48,64},{64,80},{80,96},{96,112},{112,0},{1... | collective-permute-start | bytes 393224 | tf_op jit(solution)/shard_map/ppermute | solution.py:124
  45.6 4.6 %copy-start.7 = (bf16[128,1024]{1,0:T(8,128)(2,1)}, bf16[128,1024]{1,0:T(8,128)(2,1)S(1)}, u32[]{:S(2)}) copy-start(bf16[128,1024]{1,0:T(8,128)(2,1)S(1)} %collective-permute-done.2.refs_3_) | copy-start | bytes 786436
  45.7 88.3 %collective-permute-start.8 = (bf16[64,1024]{1,0:T(8,128)(2,1)S(1)}, bf16[64,1024]{1,0:T(8,128)(2,1)}, u32[]{:S(2)}, u32[]{:S(2)}) collective-permute-start(bf16[64,1024]{1,0:T(8,128)(2,1)S(1)} %slice.78), channel_id=1, source_target_pairs={{0,112},{16,0},{32,16},{48,32},{64,48},{80,64},{96,80},{112,96},{1... | collective-permute-start | bytes 393224 | tf_op jit(solution)/shard_map/ppermute | solution.py:124
  117.1 12.4 %copy-start.1 = (bf16[1024,512]{1,0:T(8,128)(2,1)S(1)}, bf16[1024,512]{1,0:T(8,128)(2,1)}, u32[]{:S(2)}) copy-start(bf16[1024,512]{1,0:T(8,128)(2,1)} %param.9) | copy-start | bytes 3145732
  145.7 4.0 %copy-start.2 = (bf16[512,512]{0,1:T(8,128)(2,1)S(1)}, bf16[512,512]{0,1:T(8,128)(2,1)}, u32[]{:S(2)}) copy-start(bf16[512,512]{0,1:T(8,128)(2,1)} %convolution_convert_fusion.3) | copy-start | bytes 1572868
  145.8 4.0 %copy-start.3 = (bf16[512,512]{0,1:T(8,128)(2,1)S(1)}, bf16[512,512]{0,1:T(8,128)(2,1)}, u32[]{:S(2)}) copy-start(bf16[512,512]{0,1:T(8,128)(2,1)} %convolution_convert_fusion.2) | copy-start | bytes 1572868
  151.2 6.9 %copy-start.5 = (bf16[512,1024]{1,0:T(8,128)(2,1)S(1)}, bf16[512,1024]{1,0:T(8,128)(2,1)}, u32[]{:S(2)}) copy-start(bf16[512,1024]{1,0:T(8,128)(2,1)} %attend.3) | copy-start | bytes 3145732
  151.2 7.6 %copy-start.4 = (bf16[512,512]{1,0:T(8,128)(2,1)S(1)}, bf16[512,512]{1,0:T(8,128)(2,1)}, u32[]{:S(2)}) copy-start(bf16[512,512]{1,0:T(8,128)(2,1)} %convolution_convert_fusion.1) | copy-start | bytes 1572868
  152.6 6.4 %collective-permute-start.13 = (bf16[64,512]{1,0:T(8,128)(2,1)S(1)}, bf16[64,512]{1,0:T(8,128)(2,1)S(1)}, u32[]{:S(2)}, u32[]{:S(2)}) collective-permute-start(bf16[64,512]{1,0:T(8,128)(2,1)S(1)} %convolution_convert_fusion.4), channel_id=1, source_target_pairs={{0,7},{1,0},{2,1},{3,2},{4,3},{5,4},{6,5},{7,6},{8,15},{9,8},{10,9... | collective-permute-start | bytes 196616 | tf_op jit(solution)/shard_map/ppermute | solution.py:124
  156.2 7.4 %collective-permute-start.9 = (bf16[64,512]{1,0:T(8,128)(2,1)S(1)}, bf16[64,512]{1,0:T(8,128)(2,1)S(1)}, u32[]{:S(2)}, u32[]{:S(2)}) collective-permute-start(bf16[64,512]{1,0:T(8,128)(2,1)S(1)} %convolution_convert_fusion.5), channel_id=1, source_target_pairs={{0,1},{1,2},{2,3},{3,4},{4,5},{5,6},{6,7},{7,0},{8,9},{9,10},{10,1... | collective-permute-start | bytes 196616 | tf_op jit(solution)/shard_map/ppermute | solution.py:124
  159.0 6.6 %collective-permute-start.14 = (bf16[64,1024]{1,0:T(8,128)(2,1)S(1)}, bf16[64,1024]{1,0:T(8,128)(2,1)S(1)}, u32[]{:S(2)}, u32[]{:S(2)}) collective-permute-start(bf16[64,1024]{1,0:T(8,128)(2,1)S(1)} %add_convert_fusion.3), channel_id=1, source_target_pairs={{0,7},{1,0},{2,1},{3,2},{4,3},{5,4},{6,5},{7,6},{8,15},{9,8},{10,9... | collective-permute-start | bytes 393224 | tf_op jit(solution)/shard_map/ppermute | solution.py:124
  163.6 6.9 %collective-permute-start.10 = (bf16[64,1024]{1,0:T(8,128)(2,1)S(1)}, bf16[64,1024]{1,0:T(8,128)(2,1)S(1)}, u32[]{:S(2)}, u32[]{:S(2)}) collective-permute-start(bf16[64,1024]{1,0:T(8,128)(2,1)S(1)} %add_convert_fusion.6), channel_id=1, source_target_pairs={{0,1},{1,2},{2,3},{3,4},{4,5},{5,6},{6,7},{7,0},{8,9},{9,10},{10,1... | collective-permute-start | bytes 393224 | tf_op jit(solution)/shard_map/ppermute | solution.py:124
  165.6 8.5 %collective-permute-start.15 = (bf16[64,1024]{1,0:T(8,128)(2,1)S(1)}, bf16[64,1024]{1,0:T(8,128)(2,1)S(1)}, u32[]{:S(2)}, u32[]{:S(2)}) collective-permute-start(bf16[64,1024]{1,0:T(8,128)(2,1)S(1)} %add_convert_fusion.2), channel_id=1, source_target_pairs={{0,7},{1,0},{2,1},{3,2},{4,3},{5,4},{6,5},{7,6},{8,15},{9,8},{10,9... | collective-permute-start | bytes 393224 | tf_op jit(solution)/shard_map/ppermute | solution.py:124
  170.6 9.5 %collective-permute-start.11 = (bf16[64,1024]{1,0:T(8,128)(2,1)S(1)}, bf16[64,1024]{1,0:T(8,128)(2,1)S(1)}, u32[]{:S(2)}, u32[]{:S(2)}) collective-permute-start(bf16[64,1024]{1,0:T(8,128)(2,1)S(1)} %add_convert_fusion.5), channel_id=1, source_target_pairs={{0,1},{1,2},{2,3},{3,4},{4,5},{5,6},{6,7},{7,0},{8,9},{9,10},{10,1... | collective-permute-start | bytes 393224 | tf_op jit(solution)/shard_map/ppermute | solution.py:124
  174.1 8.7 %collective-permute-start.16 = (bf16[64,1024]{1,0:T(8,128)(2,1)S(1)}, bf16[64,1024]{1,0:T(8,128)(2,1)S(1)}, u32[]{:S(2)}, u32[]{:S(2)}) collective-permute-start(bf16[64,1024]{1,0:T(8,128)(2,1)S(1)} %add_convert_fusion.1), channel_id=1, source_target_pairs={{0,7},{1,0},{2,1},{3,2},{4,3},{5,4},{6,5},{7,6},{8,15},{9,8},{10,9... | collective-permute-start | bytes 393224 | tf_op jit(solution)/shard_map/ppermute | solution.py:124
  180.1 10.5 %collective-permute-start.12 = (bf16[64,1024]{1,0:T(8,128)(2,1)S(1)}, bf16[64,1024]{1,0:T(8,128)(2,1)S(1)}, u32[]{:S(2)}, u32[]{:S(2)}) collective-permute-start(bf16[64,1024]{1,0:T(8,128)(2,1)S(1)} %add_convert_fusion.4), channel_id=1, source_target_pairs={{0,1},{1,2},{2,3},{3,4},{4,5},{5,6},{6,7},{7,0},{8,9},{9,10},{10,1... | collective-permute-start | bytes 393224 | tf_op jit(solution)/shard_map/ppermute | solution.py:124
  196.0 7.5 %collective-permute-start.17 = (bf16[128,512]{1,0:T(8,128)(2,1)S(1)}, bf16[128,512]{1,0:T(8,128)(2,1)S(1)}, u32[]{:S(2)}, u32[]{:S(2)}) collective-permute-start(bf16[128,512]{1,0:T(8,128)(2,1)S(1)} %get-tuple-element.24), channel_id=1, source_target_pairs={{0,8},{8,0},{1,9},{9,1},{2,10},{10,2},{3,11},{11,3},{4,12},{12,4},... | collective-permute-start | bytes 393224 | tf_op jit(solution)/shard_map/ppermute | solution.py:128
  (1 other events, 2.9 us)
Sparse Core Ops, SparseCore 0:
  9.4 45.2 all-gather.1
  151.4 43.6 reduce-scatter.3

commit v10 on v8

--- a/solution.py
+++ b/solution.py
@@ -17,7 +17,7 @@
 
 
 def attend_kernel(ids, lengths, order, *refs):
-    *pieces, kv_ref, out_ref, acc_ref, q_ref, sems = refs
+    *pieces, kv, out_ref, acc_ref, q_ref, kv_ref, sems = refs
     z, core = ids[0], ids[1]
     step = pl.program_id(0)
     owner = (z + step // 2) % RING
@@ -27,7 +27,7 @@
 
     @pl.when(step == 0)
     def _():
-        copies, place = [], 0
+        copies, place = [pltpu.make_async_copy(kv, kv_ref, sems.at[len(pieces)])], 0
         for i, piece in enumerate(pieces):
             here = q_ref.at[pl.ds(place, piece.shape[0])]
             copies.append(pltpu.make_async_copy(piece, here, sems.at[i]))
@@ -103,13 +103,13 @@
         grid_spec=pltpu.PrefetchScalarGridSpec(
             num_scalar_prefetch=3,
             grid=(total // BLOCK,),
-            in_specs=[pl.BlockSpec(memory_space=pl.ANY)] * len(pieces)
-            + [pl.BlockSpec(kv.shape, lambda i, *_: (0, 0))],
+            in_specs=[pl.BlockSpec(memory_space=pl.ANY)] * (len(pieces) + 1),
             out_specs=pl.BlockSpec((BLOCK, width), lambda i, *_: (i, 0)),
             scratch_shapes=[
                 pltpu.VMEM((HEAD, BLOCK * (width // HEAD)), jnp.float32),
                 pltpu.VMEM((total, width), jnp.bfloat16),
-                pltpu.SemaphoreType.DMA((len(pieces),)),
+                pltpu.VMEM(kv.shape, kv.dtype),
+                pltpu.SemaphoreType.DMA((len(pieces) + 1,)),
             ],
         ),
         cost_estimate=pl.CostEstimate(
@@ -144,8 +144,11 @@
     all_tokens = lax.all_gather(tokens, "z", axis=0, tiled=True)
     all_queries = ring_gather(queries, "y")
     other_weight = swap(out_weight)
+    weight = jnp.concatenate([out_weight, other_weight], axis=1)
     partial_kv = jnp.dot(all_tokens, key_value_weight, preferred_element_type=jnp.float32)
-    partial_kv, other_weight = lax.optimization_barrier((partial_kv, other_weight))
+    partial_kv, weight, other_weight = lax.optimization_barrier(
+        (partial_kv, weight, other_weight)
+    )
     kv = lax.psum(partial_kv, ("y", "core")).astype(jnp.bfloat16)
 
     f32, bf16 = jnp.float32, jnp.bfloat16
@@ -153,10 +156,7 @@
 
     attn = attend(ids, doc_lengths, block_order, all_queries, kv)
     far = slice(4 * rows, 5 * rows)
-    first = [
-        jnp.dot(attn[far], w, preferred_element_type=f32).astype(bf16)
-        for w in (out_weight, other_weight)
-    ]
+    first = jnp.dot(attn[far], weight, preferred_element_type=f32).astype(bf16)
     out = [
         jnp.dot(attn, w, preferred_element_type=f32).astype(bf16)
         for w in (out_weight, other_weight)
@@ -167,8 +167,8 @@
         return jnp.concatenate([part[here] for part in out], axis=1).astype(f32)
 
     zero = jnp.zeros((rows, width), bf16)
-    up = jnp.concatenate([shift(first[0], "z", 1), zero], axis=1)
-    down = jnp.concatenate([zero, shift(first[1], "z", -1)], axis=1)
+    up = jnp.concatenate([shift(first[:, :width], "z", 1), zero], axis=1)
+    down = jnp.concatenate([zero, shift(first[:, width:], "z", -1)], axis=1)
     for step in (3, 2, 1):
         up = shift((product(step) + up.astype(f32)).astype(bf16), "z", 1)
         down = shift((product(RING - step) + down.astype(f32)).astype(bf16), "z", -1)

time: 210 us -> 209 us (level)
  waiting for transfers between devices: 30.7 us -> 27.1 us
  other arithmetic: 1.23 us -> 4.01 us
    all_gather x1, waiting for transfers between devices: 7.48 us -> 0.02 us  [local(): all_tokens = lax.all_gather(tokens, 'z', axis=0, tiled=True)]
    ppermute x16, waiting for transfers between devices: 21.5 us -> 25.4 us  [shift(): return lax.ppermute(x, axis, [(i, (i + by) % RING) for i in range(RING)])]
    concatenate x0 -> x1, other arithmetic: none -> 2.86 us  [local(): weight = jnp.concatenate([out_weight, other_weight], axis=1)]
  transfers between devices with their start and end apart: 19 -> 19, of which waited for: 10 -> 10; matrix products, arithmetic and copies ran while one was open for 2% -> 3% of each run, Pallas kernels for 0% -> 0%
where the time goes in v10:
time: 209 us; the launch traced here: 208 us
  starting transfers between devices  74.2 us (36%)
  blocking collectives  59.7 us (29%)
  waiting for transfers between devices  27.1 us (13%)
  Pallas kernels  19.6 us (9%)
  between operations  13.8 us (7%)
  matrix products  7.59 us (4%)
  other arithmetic  4.01 us (2%)
    psum x1, blocking collectives, local(): kv = lax.psum(partial_kv, ('y', 'core')).astype(jnp.bfloat16)  59.7 us
    ppermute x16, starting transfers between devices, shift(): return lax.ppermute(x, axis, [(i, (i + by) % RING) for i in range(RING)])  53.6 us
    ppermute x16, waiting for transfers between devices, shift(): return lax.ppermute(x, axis, [(i, (i + by) % RING) for i in range(RING)])  25.4 us
    ppermute x2, starting transfers between devices, swap(): return lax.ppermute(x, 'core', [(0, 1), (1, 0)])  20.6 us
    pallas_call x1, Pallas kernels, attend(): pl.pallas_call(attend_kernel, out_shape=jax.ShapeDtypeStruct((total, widt...  19.6 us
    dot_general x2, matrix products, local(): jnp.dot(attn, w, preferred_element_type=f32).astype(bf16)  4.34 us
  transfers between devices with their start and end apart: 19, of which 10 were waited for; matrix products, arithmetic and copies ran while one was open for 3% of the time, Pallas kernels for 0%

profile of v10, /device:TPU:1, one launch (start us, length us, event | category | flops | bytes accessed | tf_op | source)
XLA Modules:
  0.0 208.0 jit_solution(17459406097780894403)
XLA Ops:
  7.3 8.7 %collective-permute-start.8 = (bf16[1024,512]{1,0:T(8,128)(2,1)}, bf16[1024,512]{1,0:T(8,128)(2,1)S(1)}, u32[]{:S(2)}, u32[]{:S(2)}) collective-permute-start(bf16[1024,512]{1,0:T(8,128)(2,1)} %param.9), channel_id=1, source_target_pairs={{0,8},{8,0},{1,9},{9,1},{2,10},{10,2},{3,11},{11,3},{4,12},{12,4},... | collective-permute-start | bytes 3145736 | tf_op jit(solution)/shard_map/ppermute | solution.py:127
  16.0 1.9 collective-permute-start
  17.9 3.4 %collective-permute-start.3 = (bf16[128,1024]{1,0:T(8,128)(2,1)}, bf16[128,1024]{1,0:T(8,128)(2,1)S(1)}, u32[]{:S(2)}, u32[]{:S(2)}) collective-permute-start(bf16[128,1024]{1,0:T(8,128)(2,1)} %refs_0_.1), channel_id=1, source_target_pairs={{0,16},{16,32},{32,48},{48,64},{64,80},{80,96},{96,112},{112,0},{1... | collective-permute-start | bytes 786440 | tf_op jit(solution)/shard_map/ppermute | solution.py:123
  21.3 4.7 %collective-permute-done.refs_1_ = bf16[128,1024]{1,0:T(8,128)(2,1)S(1)} collective-permute-done((bf16[128,1024]{1,0:T(8,128)(2,1)}, bf16[128,1024]{1,0:T(8,128)(2,1)S(1)}, u32[]{:S(2)}, u32[]{:S(2)}) %collective-permute-start) | collective-permute-done | bytes 262176 | tf_op jit(solution)/shard_map/ppermute | solution.py:123
  26.0 3.4 %collective-permute-start.1 = (bf16[128,1024]{1,0:T(8,128)(2,1)S(1)}, bf16[128,1024]{1,0:T(8,128)(2,1)S(1)}, u32[]{:S(2)}, u32[]{:S(2)}) collective-permute-start(bf16[128,1024]{1,0:T(8,128)(2,1)S(1)} %collective-permute-done.refs_1_), channel_id=1, source_target_pairs={{0,112},{16,0},{32,16},{48,32},{64,48},{80,64},{96,80},{112,96},{1... | collective-permute-start | bytes 786440 | tf_op jit(solution)/shard_map/ppermute | solution.py:123
  29.4 1.9 collective-permute-start.4
  31.3 3.6 %collective-permute-done.1.refs_2_ = bf16[128,1024]{1,0:T(8,128)(2,1)S(1)} collective-permute-done((bf16[128,1024]{1,0:T(8,128)(2,1)S(1)}, bf16[128,1024]{1,0:T(8,128)(2,1)S(1)}, u32[]{:S(2)}, u32[]{:S(2)}) %collective-permute-start.1) | collective-permute-done | bytes 262176 | tf_op jit(solution)/shard_map/ppermute | solution.py:123
  35.0 4.9 %collective-permute-start.2 = (bf16[128,1024]{1,0:T(8,128)(2,1)S(1)}, bf16[128,1024]{1,0:T(8,128)(2,1)S(1)}, u32[]{:S(2)}, u32[]{:S(2)}) collective-permute-start(bf16[128,1024]{1,0:T(8,128)(2,1)S(1)} %collective-permute-done.1.refs_2_), channel_id=1, source_target_pairs={{0,112},{16,0},{32,16},{48,32},{64,48},{80,64},{96,80},{112,96},{1... | collective-permute-start | bytes 786440 | tf_op jit(solution)/shard_map/ppermute | solution.py:123
  39.9 1.9 collective-permute-start.5
  42.4 1.7 collective-permute-done.2.refs_3_
  44.2 5.3 %collective-permute-start.7 = (bf16[64,1024]{1,0:T(8,128)(2,1)S(1)}, bf16[64,1024]{1,0:T(8,128)(2,1)}, u32[]{:S(2)}, u32[]{:S(2)}) collective-permute-start(bf16[64,1024]{1,0:T(8,128)(2,1)S(1)} %slice.85), channel_id=1, source_target_pairs={{0,112},{16,0},{32,16},{48,32},{64,48},{80,64},{96,80},{112,96},{1... | collective-permute-start | bytes 393224 | tf_op jit(solution)/shard_map/ppermute | solution.py:123
  50.2 1.9 collective-permute-start.6
  52.2 2.9 %pad_maximum_fusion = bf16[1024,1024]{1,0:T(8,128)(2,1)} fusion(bf16[1024,512]{1,0:T(8,128)(2,1)S(1)} %collective-permute-done.8, bf16[1024,512]{1,0:T(8,128)(2,1)} %param.9), kind=kLoop, calls=%fused_computation | loop fusion | flops 4194304 | bytes 4194304 | tf_op jit(solution)/shard_map/concatenate | solution.py:147
  55.1 2.3 %fusion.5 = f32[2048,256]{1,0:T(8,128)S(1)} fusion(bf16[2048,512]{1,0:T(8,128)(2,1)} %all-gather.2.cloned.1.call-done, bf16[512,256]{1,0:T(8,128)(2,1)S(1)} %copy-done), kind=kOutput, calls=%fused_computation.18 | convolution fusion | flops 536870912 | bytes 4456448 | tf_op jit(solution)/shard_map/dot_general | solution.py:148
  57.4 59.7 %all-reduce.3.refs_9_ = bf16[2048,256]{1,0:T(8,128)(2,1)} all-reduce(f32[2048,256]{1,0:T(8,128)S(1)} %fusion.5), channel_id=1, replica_groups=mesh['dp'=4,'y'=8,'core'=2,'z'=8] {'y','core'}, use_global_device_ids=true, to_apply=%region_0.0 | all-reduce | flops 524288 | bytes 3145728 | tf_op jit(solution)/shard_map/psum | solution.py:152
  117.1 19.6 %attend.1 = bf16[1024,1024]{1,0:T(8,128)(2,1)} custom-call(s32[3]{0:T(128)} %pad_add_fusion.ids, s32[8]{0:T(128)} %lengths.1, s32[32]{0:T(128)} %order.1, bf16[128,1024]{1,0:T(8,128)(2,1)} %refs_0_.1, bf16[128,1024]{1,0:T(8,128)(2,1)} %copy-done.6, bf16[128,1024]{1,0:T(8,128)(2,1)} %copy-done.8, bf16[128,1024]{1,0:T(8,128)(2,1)} %copy-done.3, ...), custom_call_target="tpu_custom_call" | custom-call | flops 4800000000 | bytes 6000000 | tf_op jit(solution)/shard_map/attend/pallas_call | solution.py:100
  136.7 3.0 %convolution_convert_fusion.1 = bf16[1024,512]{0,1:T(8,128)(2,1)S(1)} fusion(bf16[1024,1024]{1,0:T(8,128)(2,1)} %attend.1, bf16[1024,512]{1,0:T(8,128)(2,1)S(1)} %copy-done.2), kind=kOutput, calls=%fused_computation.2 | convolution fusion | flops 1074266112 | bytes 4194304 | tf_op jit(solution)/shard_map/dot_general | solution.py:161
  140.7 1.3 convolution_convert_fusion
  142.1 2.9 %collective-permute-start.9 = (bf16[128,512]{0,1:T(8,128)(2,1)S(1)}, bf16[128,512]{0,1:T(8,128)(2,1)S(1)}, u32[]{:S(2)}, u32[]{:S(2)}) collective-permute-start(bf16[128,512]{0,1:T(8,128)(2,1)S(1)} %get-tuple-element.27), channel_id=1, source_target_pairs={{0,1},{1,2},{2,3},{3,4},{4,5},{5,6},{6,7},{7,0},{8,9},{9,10},{10,1... | collective-permute-start | bytes 393224 | tf_op jit(solution)/shard_map/ppermute | solution.py:123
  145.0 5.2 %collective-permute-start.13 = (bf16[128,512]{0,1:T(8,128)(2,1)S(1)}, bf16[128,512]{0,1:T(8,128)(2,1)S(1)}, u32[]{:S(2)}, u32[]{:S(2)}) collective-permute-start(bf16[128,512]{0,1:T(8,128)(2,1)S(1)} %get-tuple-element.28), channel_id=1, source_target_pairs={{0,7},{1,0},{2,1},{3,2},{4,3},{5,4},{6,5},{7,6},{8,15},{9,8},{10,9... | collective-permute-start | bytes 393224 | tf_op jit(solution)/shard_map/ppermute | solution.py:123
  150.7 1.5 collective-permute-done.13
  152.2 5.0 %collective-permute-start.14 = (bf16[128,1024]{0,1:T(8,128)(2,1)S(1)}, bf16[128,1024]{0,1:T(8,128)(2,1)S(1)}, u32[]{:S(2)}, u32[]{:S(2)}) collective-permute-start(bf16[128,1024]{0,1:T(8,128)(2,1)S(1)} %add_convert_fusion.3), channel_id=1, source_target_pairs={{0,7},{1,0},{2,1},{3,2},{4,3},{5,4},{6,5},{7,6},{8,15},{9,8},{10,9... | collective-permute-start | bytes 786440 | tf_op jit(solution)/shard_map/ppermute | solution.py:123
  157.3 1.9 collective-permute-start.10
  159.2 1.6 collective-permute-done.14
  160.8 5.0 %collective-permute-start.15 = (bf16[128,1024]{0,1:T(8,128)(2,1)S(1)}, bf16[128,1024]{0,1:T(8,128)(2,1)S(1)}, u32[]{:S(2)}, u32[]{:S(2)}) collective-permute-start(bf16[128,1024]{0,1:T(8,128)(2,1)S(1)} %add_convert_fusion.2), channel_id=1, source_target_pairs={{0,7},{1,0},{2,1},{3,2},{4,3},{5,4},{6,5},{7,6},{8,15},{9,8},{10,9... | collective-permute-start | bytes 786440 | tf_op jit(solution)/shard_map/ppermute | solution.py:123
  165.9 1.9 collective-permute-start.11
  167.9 2.6 %collective-permute-done.15 = bf16[128,1024]{0,1:T(8,128)(2,1)S(1)} collective-permute-done((bf16[128,1024]{0,1:T(8,128)(2,1)S(1)}, bf16[128,1024]{0,1:T(8,128)(2,1)S(1)}, u32[]{:S(2)}, u32[]{:S(2)}) %collective-permute-start.15) | collective-permute-done | bytes 262176 | tf_op jit(solution)/shard_map/ppermute | solution.py:123
  170.6 5.0 %collective-permute-start.16 = (bf16[128,1024]{0,1:T(8,128)(2,1)S(1)}, bf16[128,1024]{0,1:T(8,128)(2,1)S(1)}, u32[]{:S(2)}, u32[]{:S(2)}) collective-permute-start(bf16[128,1024]{0,1:T(8,128)(2,1)S(1)} %add_convert_fusion.1), channel_id=1, source_target_pairs={{0,7},{1,0},{2,1},{3,2},{4,3},{5,4},{6,5},{7,6},{8,15},{9,8},{10,9... | collective-permute-start | bytes 786440 | tf_op jit(solution)/shard_map/ppermute | solution.py:123
  176.0 1.9 collective-permute-start.12
  177.9 3.5 %collective-permute-done.16 = bf16[128,1024]{0,1:T(8,128)(2,1)S(1)} collective-permute-done((bf16[128,1024]{0,1:T(8,128)(2,1)S(1)}, bf16[128,1024]{0,1:T(8,128)(2,1)S(1)}, u32[]{:S(2)}, u32[]{:S(2)}) %collective-permute-start.16) | collective-permute-done | bytes 262176 | tf_op jit(solution)/shard_map/ppermute | solution.py:123
  181.4 5.9 %collective-permute-done.12 = bf16[128,1024]{0,1:T(8,128)(2,1)S(1)} collective-permute-done((bf16[128,1024]{0,1:T(8,128)(2,1)S(1)}, bf16[128,1024]{0,1:T(8,128)(2,1)S(1)}, u32[]{:S(2)}, u32[]{:S(2)}) %collective-permute-start.12) | collective-permute-done | bytes 262176 | tf_op jit(solution)/shard_map/ppermute | solution.py:123
  187.4 11.9 %collective-permute-start.17 = (bf16[128,512]{0,1:T(8,128)(2,1)S(1)}, bf16[128,512]{0,1:T(8,128)(2,1)S(1)}, u32[]{:S(2)}, u32[]{:S(2)}) collective-permute-start(bf16[128,512]{0,1:T(8,128)(2,1)S(1)} %get-tuple-element.26), channel_id=1, source_target_pairs={{0,8},{8,0},{1,9},{9,1},{2,10},{10,2},{3,11},{11,3},{4,12},{12,4},... | collective-permute-start | bytes 393224 | tf_op jit(solution)/shard_map/ppermute | solution.py:127
  (49 shorter events, 6.2 us)
Async XLA Ops:
  6.5 48.5 %copy-start = (bf16[512,256]{1,0:T(8,128)(2,1)S(1)}, bf16[512,256]{1,0:T(8,128)(2,1)}, u32[]{:S(2)}) copy-start(bf16[512,256]{1,0:T(8,128)(2,1)} %param.8) | copy-start | bytes 786436
  6.5 48.5 %all-gather.2.cloned.1.call-start = ((), (), s32[]{:S(2)}) async-start(), calls=%async_computation | async-start | bytes 2359296 | tf_op jit(solution)/shard_map/all_gather | solution.py:144
  7.3 44.9 %collective-permute-start.8 = (bf16[1024,512]{1,0:T(8,128)(2,1)}, bf16[1024,512]{1,0:T(8,128)(2,1)S(1)}, u32[]{:S(2)}, u32[]{:S(2)}) collective-permute-start(bf16[1024,512]{1,0:T(8,128)(2,1)} %param.9), channel_id=1, source_target_pairs={{0,8},{8,0},{1,9},{9,1},{2,10},{10,2},{3,11},{11,3},{4,12},{12,4},... | collective-permute-start | bytes 3145736 | tf_op jit(solution)/shard_map/ppermute | solution.py:127
  16.0 10.0 %collective-permute-start = (bf16[128,1024]{1,0:T(8,128)(2,1)}, bf16[128,1024]{1,0:T(8,128)(2,1)S(1)}, u32[]{:S(2)}, u32[]{:S(2)}) collective-permute-start(bf16[128,1024]{1,0:T(8,128)(2,1)} %refs_0_.1), channel_id=1, source_target_pairs={{0,112},{16,0},{32,16},{48,32},{64,48},{80,64},{96,80},{112,96},{1... | collective-permute-start | bytes 786440 | tf_op jit(solution)/shard_map/ppermute | solution.py:123
  17.9 11.4 %collective-permute-start.3 = (bf16[128,1024]{1,0:T(8,128)(2,1)}, bf16[128,1024]{1,0:T(8,128)(2,1)S(1)}, u32[]{:S(2)}, u32[]{:S(2)}) collective-permute-start(bf16[128,1024]{1,0:T(8,128)(2,1)} %refs_0_.1), channel_id=1, source_target_pairs={{0,16},{16,32},{32,48},{48,64},{64,80},{80,96},{96,112},{112,0},{1... | collective-permute-start | bytes 786440 | tf_op jit(solution)/shard_map/ppermute | solution.py:123
  26.0 13.9 %copy-start.6 = (bf16[128,1024]{1,0:T(8,128)(2,1)}, bf16[128,1024]{1,0:T(8,128)(2,1)S(1)}, u32[]{:S(2)}) copy-start(bf16[128,1024]{1,0:T(8,128)(2,1)S(1)} %collective-permute-done.refs_1_) | copy-start | bytes 786436
  26.0 9.0 %collective-permute-start.1 = (bf16[128,1024]{1,0:T(8,128)(2,1)S(1)}, bf16[128,1024]{1,0:T(8,128)(2,1)S(1)}, u32[]{:S(2)}, u32[]{:S(2)}) collective-permute-start(bf16[128,1024]{1,0:T(8,128)(2,1)S(1)} %collective-permute-done.refs_1_), channel_id=1, source_target_pairs={{0,112},{16,0},{32,16},{48,32},{64,48},{80,64},{96,80},{112,96},{1... | collective-permute-start | bytes 786440 | tf_op jit(solution)/shard_map/ppermute | solution.py:123
  29.4 10.5 %copy-start.7 = (bf16[128,1024]{1,0:T(8,128)(2,1)}, bf16[128,1024]{1,0:T(8,128)(2,1)S(1)}, u32[]{:S(2)}) copy-start(bf16[128,1024]{1,0:T(8,128)(2,1)S(1)} %collective-permute-done.3.refs_8_) | copy-start | bytes 786436
  29.4 10.5 %collective-permute-start.4 = (bf16[128,1024]{1,0:T(8,128)(2,1)S(1)}, bf16[128,1024]{1,0:T(8,128)(2,1)S(1)}, u32[]{:S(2)}, u32[]{:S(2)}) collective-permute-start(bf16[128,1024]{1,0:T(8,128)(2,1)S(1)} %collective-permute-done.3.refs_8_), channel_id=1, source_target_pairs={{0,16},{16,32},{32,48},{48,64},{64,80},{80,96},{96,112},{112,0},{1... | collective-permute-start | bytes 786440 | tf_op jit(solution)/shard_map/ppermute | solution.py:123
  35.0 20.1 %copy-start.8 = (bf16[128,1024]{1,0:T(8,128)(2,1)}, bf16[128,1024]{1,0:T(8,128)(2,1)S(1)}, u32[]{:S(2)}) copy-start(bf16[128,1024]{1,0:T(8,128)(2,1)S(1)} %collective-permute-done.1.refs_2_) | copy-start | bytes 786436
  35.0 9.2 %collective-permute-start.2 = (bf16[128,1024]{1,0:T(8,128)(2,1)S(1)}, bf16[128,1024]{1,0:T(8,128)(2,1)S(1)}, u32[]{:S(2)}, u32[]{:S(2)}) collective-permute-start(bf16[128,1024]{1,0:T(8,128)(2,1)S(1)} %collective-permute-done.1.refs_2_), channel_id=1, source_target_pairs={{0,112},{16,0},{32,16},{48,32},{64,48},{80,64},{96,80},{112,96},{1... | collective-permute-start | bytes 786440 | tf_op jit(solution)/shard_map/ppermute | solution.py:123
  39.9 15.1 %copy-start.9 = (bf16[128,1024]{1,0:T(8,128)(2,1)}, bf16[128,1024]{1,0:T(8,128)(2,1)S(1)}, u32[]{:S(2)}) copy-start(bf16[128,1024]{1,0:T(8,128)(2,1)S(1)} %collective-permute-done.4.refs_7_) | copy-start | bytes 786436
  39.9 9.6 %collective-permute-start.5 = (bf16[128,1024]{1,0:T(8,128)(2,1)S(1)}, bf16[128,1024]{1,0:T(8,128)(2,1)S(1)}, u32[]{:S(2)}, u32[]{:S(2)}) collective-permute-start(bf16[128,1024]{1,0:T(8,128)(2,1)S(1)} %collective-permute-done.4.refs_7_), channel_id=1, source_target_pairs={{0,16},{16,32},{32,48},{48,64},{64,80},{80,96},{96,112},{112,0},{1... | collective-permute-start | bytes 786440 | tf_op jit(solution)/shard_map/ppermute | solution.py:123
  44.2 10.9 %copy-start.3 = (bf16[128,1024]{1,0:T(8,128)(2,1)}, bf16[128,1024]{1,0:T(8,128)(2,1)S(1)}, u32[]{:S(2)}) copy-start(bf16[128,1024]{1,0:T(8,128)(2,1)S(1)} %collective-permute-done.2.refs_3_) | copy-start | bytes 786436
  44.2 72.9 %collective-permute-start.7 = (bf16[64,1024]{1,0:T(8,128)(2,1)S(1)}, bf16[64,1024]{1,0:T(8,128)(2,1)}, u32[]{:S(2)}, u32[]{:S(2)}) collective-permute-start(bf16[64,1024]{1,0:T(8,128)(2,1)S(1)} %slice.85), channel_id=1, source_target_pairs={{0,112},{16,0},{32,16},{48,32},{64,48},{80,64},{96,80},{112,96},{1... | collective-permute-start | bytes 393224 | tf_op jit(solution)/shard_map/ppermute | solution.py:123
  49.5 5.5 %copy-start.4 = (bf16[128,1024]{1,0:T(8,128)(2,1)}, bf16[128,1024]{1,0:T(8,128)(2,1)S(1)}, u32[]{:S(2)}) copy-start(bf16[128,1024]{1,0:T(8,128)(2,1)S(1)} %collective-permute-done.5.refs_6_) | copy-start | bytes 786436
  50.2 66.9 %collective-permute-start.6 = (bf16[64,1024]{1,0:T(8,128)(2,1)}, bf16[64,1024]{1,0:T(8,128)(2,1)}, u32[]{:S(2)}, u32[]{:S(2)}) collective-permute-start(bf16[64,1024]{1,0:T(8,128)(2,1)} %slice.84), channel_id=1, source_target_pairs={{0,16},{16,32},{32,48},{48,64},{64,80},{80,96},{96,112},{112,0},{1... | collective-permute-start | bytes 393224 | tf_op jit(solution)/shard_map/ppermute | solution.py:123
  117.1 19.6 %copy-start.2 = (bf16[1024,512]{1,0:T(8,128)(2,1)S(1)}, bf16[1024,512]{1,0:T(8,128)(2,1)}, u32[]{:S(2)}) copy-start(bf16[1024,512]{1,0:T(8,128)(2,1)} %param.9) | copy-start | bytes 3145732
  136.7 3.1 %copy-start.1 = (bf16[1024,1024]{1,0:T(8,128)(2,1)S(1)}, bf16[1024,1024]{1,0:T(8,128)(2,1)}, u32[]{:S(2)}) copy-start(bf16[1024,1024]{1,0:T(8,128)(2,1)} %pad_maximum_fusion) | copy-start | bytes 6291460
  136.7 3.1 %copy-start.5 = (bf16[1024,1024]{1,0:T(8,128)(2,1)S(1)}, bf16[1024,1024]{1,0:T(8,128)(2,1)}, u32[]{:S(2)}) copy-start(bf16[1024,1024]{1,0:T(8,128)(2,1)} %attend.1) | copy-start | bytes 6291460
  142.1 15.1 %collective-permute-start.9 = (bf16[128,512]{0,1:T(8,128)(2,1)S(1)}, bf16[128,512]{0,1:T(8,128)(2,1)S(1)}, u32[]{:S(2)}, u32[]{:S(2)}) collective-permute-start(bf16[128,512]{0,1:T(8,128)(2,1)S(1)} %get-tuple-element.27), channel_id=1, source_target_pairs={{0,1},{1,2},{2,3},{3,4},{4,5},{5,6},{6,7},{7,0},{8,9},{9,10},{10,1... | collective-permute-start | bytes 393224 | tf_op jit(solution)/shard_map/ppermute | solution.py:123
  145.0 7.2 %collective-permute-start.13 = (bf16[128,512]{0,1:T(8,128)(2,1)S(1)}, bf16[128,512]{0,1:T(8,128)(2,1)S(1)}, u32[]{:S(2)}, u32[]{:S(2)}) collective-permute-start(bf16[128,512]{0,1:T(8,128)(2,1)S(1)} %get-tuple-element.28), channel_id=1, source_target_pairs={{0,7},{1,0},{2,1},{3,2},{4,3},{5,4},{6,5},{7,6},{8,15},{9,8},{10,9... | collective-permute-start | bytes 393224 | tf_op jit(solution)/shard_map/ppermute | solution.py:123
  152.2 8.5 %collective-permute-start.14 = (bf16[128,1024]{0,1:T(8,128)(2,1)S(1)}, bf16[128,1024]{0,1:T(8,128)(2,1)S(1)}, u32[]{:S(2)}, u32[]{:S(2)}) collective-permute-start(bf16[128,1024]{0,1:T(8,128)(2,1)S(1)} %add_convert_fusion.3), channel_id=1, source_target_pairs={{0,7},{1,0},{2,1},{3,2},{4,3},{5,4},{6,5},{7,6},{8,15},{9,8},{10,9... | collective-permute-start | bytes 786440 | tf_op jit(solution)/shard_map/ppermute | solution.py:123
  157.3 8.6 %collective-permute-start.10 = (bf16[128,1024]{0,1:T(8,128)(2,1)S(1)}, bf16[128,1024]{0,1:T(8,128)(2,1)S(1)}, u32[]{:S(2)}, u32[]{:S(2)}) collective-permute-start(bf16[128,1024]{0,1:T(8,128)(2,1)S(1)} %add_convert_fusion.6), channel_id=1, source_target_pairs={{0,1},{1,2},{2,3},{3,4},{4,5},{5,6},{6,7},{7,0},{8,9},{9,10},{10,1... | collective-permute-start | bytes 786440 | tf_op jit(solution)/shard_map/ppermute | solution.py:123
  160.8 9.7 %collective-permute-start.15 = (bf16[128,1024]{0,1:T(8,128)(2,1)S(1)}, bf16[128,1024]{0,1:T(8,128)(2,1)S(1)}, u32[]{:S(2)}, u32[]{:S(2)}) collective-permute-start(bf16[128,1024]{0,1:T(8,128)(2,1)S(1)} %add_convert_fusion.2), channel_id=1, source_target_pairs={{0,7},{1,0},{2,1},{3,2},{4,3},{5,4},{6,5},{7,6},{8,15},{9,8},{10,9... | collective-permute-start | bytes 786440 | tf_op jit(solution)/shard_map/ppermute | solution.py:123
  165.9 9.9 %collective-permute-start.11 = (bf16[128,1024]{0,1:T(8,128)(2,1)S(1)}, bf16[128,1024]{0,1:T(8,128)(2,1)S(1)}, u32[]{:S(2)}, u32[]{:S(2)}) collective-permute-start(bf16[128,1024]{0,1:T(8,128)(2,1)S(1)} %add_convert_fusion.5), channel_id=1, source_target_pairs={{0,1},{1,2},{2,3},{3,4},{4,5},{5,6},{6,7},{7,0},{8,9},{9,10},{10,1... | collective-permute-start | bytes 786440 | tf_op jit(solution)/shard_map/ppermute | solution.py:123
  170.6 10.8 %collective-permute-start.16 = (bf16[128,1024]{0,1:T(8,128)(2,1)S(1)}, bf16[128,1024]{0,1:T(8,128)(2,1)S(1)}, u32[]{:S(2)}, u32[]{:S(2)}) collective-permute-start(bf16[128,1024]{0,1:T(8,128)(2,1)S(1)} %add_convert_fusion.1), channel_id=1, source_target_pairs={{0,7},{1,0},{2,1},{3,2},{4,3},{5,4},{6,5},{7,6},{8,15},{9,8},{10,9... | collective-permute-start | bytes 786440 | tf_op jit(solution)/shard_map/ppermute | solution.py:123
  176.0 11.3 %collective-permute-start.12 = (bf16[128,1024]{0,1:T(8,128)(2,1)S(1)}, bf16[128,1024]{0,1:T(8,128)(2,1)S(1)}, u32[]{:S(2)}, u32[]{:S(2)}) collective-permute-start(bf16[128,1024]{0,1:T(8,128)(2,1)S(1)} %add_convert_fusion.4), channel_id=1, source_target_pairs={{0,1},{1,2},{2,3},{3,4},{4,5},{5,6},{6,7},{7,0},{8,9},{9,10},{10,1... | collective-permute-start | bytes 786440 | tf_op jit(solution)/shard_map/ppermute | solution.py:123
  187.4 12.8 %collective-permute-start.17 = (bf16[128,512]{0,1:T(8,128)(2,1)S(1)}, bf16[128,512]{0,1:T(8,128)(2,1)S(1)}, u32[]{:S(2)}, u32[]{:S(2)}) collective-permute-start(bf16[128,512]{0,1:T(8,128)(2,1)S(1)} %get-tuple-element.26), channel_id=1, source_target_pairs={{0,8},{8,0},{1,9},{9,1},{2,10},{10,2},{3,11},{11,3},{4,12},{12,4},... | collective-permute-start | bytes 393224 | tf_op jit(solution)/shard_map/ppermute | solution.py:127
Sparse Core Ops, SparseCore 0:
  9.4 45.1 all-gather.1

commit v11 on v8

--- a/solution.py
+++ b/solution.py
@@ -174,11 +174,8 @@
         down = shift((product(RING - step) + down.astype(f32)).astype(bf16), "z", -1)
     total = (product(0) + up.astype(f32) + down.astype(f32)).astype(bf16)
     mine, theirs = total[:, :width], swap(total[:, width:])
-    return jnp.where(
-        core == 0,
-        jnp.concatenate([mine, theirs], axis=0),
-        jnp.concatenate([theirs, mine], axis=0),
-    )
+    around = jnp.concatenate([mine, theirs, mine], axis=0)
+    return lax.dynamic_slice_in_dim(around, core * mine.shape[0], 2 * mine.shape[0], 0)
 
 
 def solution(mesh):

time: 210 us -> 210 us (level)
  no operation moved by 1% of the time
where the time goes in v11:
time: 210 us; the launch traced here: 209 us
  starting transfers between devices  72.2 us (34%)
  blocking collectives  59.9 us (29%)
  waiting for transfers between devices  30.7 us (15%)
  Pallas kernels  20.5 us (10%)
  between operations  13.8 us (7%)
  matrix products  8.64 us (4%)
    psum x1, blocking collectives, local(): kv = lax.psum(partial_kv, ('y', 'core')).astype(jnp.bfloat16)  59.9 us
    ppermute x16, starting transfers between devices, shift(): return lax.ppermute(x, axis, [(i, (i + by) % RING) for i in range(RING)])  53.2 us
    ppermute x16, waiting for transfers between devices, shift(): return lax.ppermute(x, axis, [(i, (i + by) % RING) for i in range(RING)])  21.5 us
    pallas_call x1, Pallas kernels, attend(): pl.pallas_call(attend_kernel, out_shape=jax.ShapeDtypeStruct((total, widt...  20.5 us
    ppermute x2, starting transfers between devices, swap(): return lax.ppermute(x, 'core', [(0, 1), (1, 0)])  18.9 us
    all_gather x1, waiting for transfers between devices, local(): all_tokens = lax.all_gather(tokens, 'z', axis=0, tiled=True)  7.48 us
    dot_general x2, matrix products, local(): jnp.dot(attn, w, preferred_element_type=f32).astype(bf16)  4.33 us
  transfers between devices with their start and end apart: 19, of which 10 were waited for; matrix products, arithmetic and copies ran while one was open for 2% of the time, Pallas kernels for 0%

profile of v11, /device:TPU:1, one launch (start us, length us, event | category | flops | bytes accessed | tf_op | source)
XLA Modules:
  0.0 209.1 jit_solution(10271642977256744967)
XLA Ops:
  7.3 5.9 %collective-permute-start = (bf16[128,1024]{1,0:T(8,128)(2,1)}, bf16[128,1024]{1,0:T(8,128)(2,1)S(1)}, u32[]{:S(2)}, u32[]{:S(2)}) collective-permute-start(bf16[128,1024]{1,0:T(8,128)(2,1)} %refs_0_.1), channel_id=1, source_target_pairs={{0,112},{16,0},{32,16},{48,32},{64,48},{80,64},{96,80},{112,96},{1... | collective-permute-start | bytes 786440 | tf_op jit(solution)/shard_map/ppermute | solution.py:123
  13.2 1.9 collective-permute-start.3
  15.1 6.8 %collective-permute-start.8 = (bf16[1024,512]{1,0:T(8,128)(2,1)}, bf16[1024,512]{1,0:T(8,128)(2,1)S(1)}, u32[]{:S(2)}, u32[]{:S(2)}) collective-permute-start(bf16[1024,512]{1,0:T(8,128)(2,1)} %param.9), channel_id=1, source_target_pairs={{0,8},{8,0},{1,9},{9,1},{2,10},{10,2},{3,11},{11,3},{4,12},{12,4},... | collective-permute-start | bytes 3145736 | tf_op jit(solution)/shard_map/ppermute | solution.py:127
  21.9 2.9 %collective-permute-start.1 = (bf16[128,1024]{1,0:T(8,128)(2,1)S(1)}, bf16[128,1024]{1,0:T(8,128)(2,1)S(1)}, u32[]{:S(2)}, u32[]{:S(2)}) collective-permute-start(bf16[128,1024]{1,0:T(8,128)(2,1)S(1)} %collective-permute-done.refs_1_), channel_id=1, source_target_pairs={{0,112},{16,0},{32,16},{48,32},{64,48},{80,64},{96,80},{112,96},{1... | collective-permute-start | bytes 786440 | tf_op jit(solution)/shard_map/ppermute | solution.py:123
  24.8 2.4 %collective-permute-start.4 = (bf16[128,1024]{1,0:T(8,128)(2,1)S(1)}, bf16[128,1024]{1,0:T(8,128)(2,1)S(1)}, u32[]{:S(2)}, u32[]{:S(2)}) collective-permute-start(bf16[128,1024]{1,0:T(8,128)(2,1)S(1)} %collective-permute-done.3.refs_8_), channel_id=1, source_target_pairs={{0,16},{16,32},{32,48},{48,64},{64,80},{80,96},{96,112},{112,0},{1... | collective-permute-start | bytes 786440 | tf_op jit(solution)/shard_map/ppermute | solution.py:123
  27.2 3.8 %collective-permute-done.1.refs_2_ = bf16[128,1024]{1,0:T(8,128)(2,1)S(1)} collective-permute-done((bf16[128,1024]{1,0:T(8,128)(2,1)S(1)}, bf16[128,1024]{1,0:T(8,128)(2,1)S(1)}, u32[]{:S(2)}, u32[]{:S(2)}) %collective-permute-start.1) | collective-permute-done | bytes 262176 | tf_op jit(solution)/shard_map/ppermute | solution.py:123
  31.0 4.0 %collective-permute-start.2 = (bf16[128,1024]{1,0:T(8,128)(2,1)S(1)}, bf16[128,1024]{1,0:T(8,128)(2,1)S(1)}, u32[]{:S(2)}, u32[]{:S(2)}) collective-permute-start(bf16[128,1024]{1,0:T(8,128)(2,1)S(1)} %collective-permute-done.1.refs_2_), channel_id=1, source_target_pairs={{0,112},{16,0},{32,16},{48,32},{64,48},{80,64},{96,80},{112,96},{1... | collective-permute-start | bytes 786440 | tf_op jit(solution)/shard_map/ppermute | solution.py:123
  35.1 1.9 collective-permute-start.5
  37.7 1.6 collective-permute-done.2.refs_3_
  39.3 5.3 %collective-permute-start.7 = (bf16[64,1024]{1,0:T(8,128)(2,1)S(1)}, bf16[64,1024]{1,0:T(8,128)(2,1)}, u32[]{:S(2)}, u32[]{:S(2)}) collective-permute-start(bf16[64,1024]{1,0:T(8,128)(2,1)S(1)} %slice.78), channel_id=1, source_target_pairs={{0,112},{16,0},{32,16},{48,32},{64,48},{80,64},{96,80},{112,96},{1... | collective-permute-start | bytes 393224 | tf_op jit(solution)/shard_map/ppermute | solution.py:123
  45.4 1.9 collective-permute-start.6
  47.3 7.5 %all-gather.2.cloned.1.call-done = bf16[2048,512]{1,0:T(8,128)(2,1)} async-done(((bf16[256,512]{1,0:T(8,128)(2,1)}), bf16[2048,512]{1,0:T(8,128)(2,1)}) %all-gather.2.cloned.1.call-update) | async-done | bytes 2097168 | tf_op jit(solution)/shard_map/all_gather | solution.py:144
  54.8 2.3 %fusion.7 = f32[2048,256]{1,0:T(8,128)S(1)} fusion(bf16[2048,512]{1,0:T(8,128)(2,1)} %all-gather.2.cloned.1.call-done, bf16[512,256]{1,0:T(8,128)(2,1)S(1)} %copy-done), kind=kOutput, calls=%fused_computation.22 | convolution fusion | flops 536870912 | bytes 4456448 | tf_op jit(solution)/shard_map/dot_general | solution.py:147
  57.1 59.9 %all-reduce.3.refs_9_ = bf16[2048,256]{1,0:T(8,128)(2,1)} all-reduce(f32[2048,256]{1,0:T(8,128)S(1)} %fusion.7), channel_id=1, replica_groups=mesh['dp'=4,'y'=8,'core'=2,'z'=8] {'y','core'}, use_global_device_ids=true, to_apply=%region_0.0 | all-reduce | flops 524288 | bytes 3145728 | tf_op jit(solution)/shard_map/psum | solution.py:149
  117.0 20.5 %attend.1 = bf16[1024,1024]{1,0:T(8,128)(2,1)} custom-call(s32[3]{0:T(128)} %pad_add_fusion.ids, s32[8]{0:T(128)} %lengths.1, s32[32]{0:T(128)} %order.1, bf16[128,1024]{1,0:T(8,128)(2,1)} %refs_0_.1, bf16[128,1024]{1,0:T(8,128)(2,1)} %copy-done.5, bf16[128,1024]{1,0:T(8,128)(2,1)} %copy-done.7, bf16[128,1024]{1,0:T(8,128)(2,1)} %copy-done.3, ...), custom_call_target="tpu_custom_call" | custom-call | flops 4800000000 | bytes 6000000 | tf_op jit(solution)/shard_map/attend/pallas_call | solution.py:100
  137.5 1.5 convolution_convert_fusion.2
  139.0 3.0 %convolution_convert_fusion = bf16[1024,512]{0,1:T(8,128)(2,1)S(1)} fusion(bf16[1024,1024]{1,0:T(8,128)(2,1)} %attend.1, bf16[1024,512]{1,0:T(8,128)(2,1)S(1)} %collective-permute-done.8), kind=kOutput, calls=%fused_computation | convolution fusion | flops 1074266112 | bytes 4194304 | tf_op jit(solution)/shard_map/dot_general | solution.py:161
  142.6 1.3 convolution_convert_fusion.1
  143.9 2.9 %collective-permute-start.9 = (bf16[128,512]{0,1:T(8,128)(2,1)S(1)}, bf16[128,512]{0,1:T(8,128)(2,1)S(1)}, u32[]{:S(2)}, u32[]{:S(2)}) collective-permute-start(bf16[128,512]{0,1:T(8,128)(2,1)S(1)} %convolution_convert_fusion.3), channel_id=1, source_target_pairs={{0,1},{1,2},{2,3},{3,4},{4,5},{5,6},{6,7},{7,0},{8,9},{9,10},{10,1... | collective-permute-start | bytes 393224 | tf_op jit(solution)/shard_map/ppermute | solution.py:123
  146.8 3.6 %collective-permute-start.13 = (bf16[128,512]{0,1:T(8,128)(2,1)S(1)}, bf16[128,512]{0,1:T(8,128)(2,1)S(1)}, u32[]{:S(2)}, u32[]{:S(2)}) collective-permute-start(bf16[128,512]{0,1:T(8,128)(2,1)S(1)} %convolution_convert_fusion.2), channel_id=1, source_target_pairs={{0,7},{1,0},{2,1},{3,2},{4,3},{5,4},{6,5},{7,6},{8,15},{9,8},{10,9... | collective-permute-start | bytes 393224 | tf_op jit(solution)/shard_map/ppermute | solution.py:123
  150.8 1.7 collective-permute-done.13
  152.6 4.8 %collective-permute-start.14 = (bf16[128,1024]{0,1:T(8,128)(2,1)S(1)}, bf16[128,1024]{0,1:T(8,128)(2,1)S(1)}, u32[]{:S(2)}, u32[]{:S(2)}) collective-permute-start(bf16[128,1024]{0,1:T(8,128)(2,1)S(1)} %add_convert_fusion.3), channel_id=1, source_target_pairs={{0,7},{1,0},{2,1},{3,2},{4,3},{5,4},{6,5},{7,6},{8,15},{9,8},{10,9... | collective-permute-start | bytes 786440 | tf_op jit(solution)/shard_map/ppermute | solution.py:123
  157.4 1.9 collective-permute-start.10
  159.3 1.9 collective-permute-done.14
  161.3 5.0 %collective-permute-start.15 = (bf16[128,1024]{0,1:T(8,128)(2,1)S(1)}, bf16[128,1024]{0,1:T(8,128)(2,1)S(1)}, u32[]{:S(2)}, u32[]{:S(2)}) collective-permute-start(bf16[128,1024]{0,1:T(8,128)(2,1)S(1)} %add_convert_fusion.2), channel_id=1, source_target_pairs={{0,7},{1,0},{2,1},{3,2},{4,3},{5,4},{6,5},{7,6},{8,15},{9,8},{10,9... | collective-permute-start | bytes 786440 | tf_op jit(solution)/shard_map/ppermute | solution.py:123
  166.4 1.9 collective-permute-start.11
  168.3 3.1 %collective-permute-done.15 = bf16[128,1024]{0,1:T(8,128)(2,1)S(1)} collective-permute-done((bf16[128,1024]{0,1:T(8,128)(2,1)S(1)}, bf16[128,1024]{0,1:T(8,128)(2,1)S(1)}, u32[]{:S(2)}, u32[]{:S(2)}) %collective-permute-start.15) | collective-permute-done | bytes 262176 | tf_op jit(solution)/shard_map/ppermute | solution.py:123
  171.5 4.9 %collective-permute-start.16 = (bf16[128,1024]{0,1:T(8,128)(2,1)S(1)}, bf16[128,1024]{0,1:T(8,128)(2,1)S(1)}, u32[]{:S(2)}, u32[]{:S(2)}) collective-permute-start(bf16[128,1024]{0,1:T(8,128)(2,1)S(1)} %add_convert_fusion.1), channel_id=1, source_target_pairs={{0,7},{1,0},{2,1},{3,2},{4,3},{5,4},{6,5},{7,6},{8,15},{9,8},{10,9... | collective-permute-start | bytes 786440 | tf_op jit(solution)/shard_map/ppermute | solution.py:123
  176.7 1.9 collective-permute-start.12
  178.7 3.8 %collective-permute-done.16 = bf16[128,1024]{0,1:T(8,128)(2,1)S(1)} collective-permute-done((bf16[128,1024]{0,1:T(8,128)(2,1)S(1)}, bf16[128,1024]{0,1:T(8,128)(2,1)S(1)}, u32[]{:S(2)}, u32[]{:S(2)}) %collective-permute-start.16) | collective-permute-done | bytes 262176 | tf_op jit(solution)/shard_map/ppermute | solution.py:123
  182.5 5.4 %collective-permute-done.12 = bf16[128,1024]{0,1:T(8,128)(2,1)S(1)} collective-permute-done((bf16[128,1024]{0,1:T(8,128)(2,1)S(1)}, bf16[128,1024]{0,1:T(8,128)(2,1)S(1)}, u32[]{:S(2)}, u32[]{:S(2)}) %collective-permute-start.12) | collective-permute-done | bytes 262176 | tf_op jit(solution)/shard_map/ppermute | solution.py:123
  188.0 12.2 %collective-permute-start.17 = (bf16[128,512]{0,1:T(8,128)(2,1)S(1)}, bf16[128,512]{0,1:T(8,128)(2,1)S(1)}, u32[]{:S(2)}, u32[]{:S(2)}) collective-permute-start(bf16[128,512]{0,1:T(8,128)(2,1)S(1)} %get-tuple-element.23), channel_id=1, source_target_pairs={{0,8},{8,0},{1,9},{9,1},{2,10},{10,2},{3,11},{11,3},{4,12},{12,4},... | collective-permute-start | bytes 393224 | tf_op jit(solution)/shard_map/ppermute | solution.py:127
  (46 shorter events, 5.9 us)
Async XLA Ops:
  6.5 48.3 %copy-start = (bf16[512,256]{1,0:T(8,128)(2,1)S(1)}, bf16[512,256]{1,0:T(8,128)(2,1)}, u32[]{:S(2)}) copy-start(bf16[512,256]{1,0:T(8,128)(2,1)} %param.8) | copy-start | bytes 786436
  6.5 48.3 %all-gather.2.cloned.1.call-start = ((), (), s32[]{:S(2)}) async-start(), calls=%async_computation | async-start | bytes 2359296 | tf_op jit(solution)/shard_map/all_gather | solution.py:144
  7.3 14.6 %collective-permute-start = (bf16[128,1024]{1,0:T(8,128)(2,1)}, bf16[128,1024]{1,0:T(8,128)(2,1)S(1)}, u32[]{:S(2)}, u32[]{:S(2)}) collective-permute-start(bf16[128,1024]{1,0:T(8,128)(2,1)} %refs_0_.1), channel_id=1, source_target_pairs={{0,112},{16,0},{32,16},{48,32},{64,48},{80,64},{96,80},{112,96},{1... | collective-permute-start | bytes 786440 | tf_op jit(solution)/shard_map/ppermute | solution.py:123
  13.2 11.6 %collective-permute-start.3 = (bf16[128,1024]{1,0:T(8,128)(2,1)}, bf16[128,1024]{1,0:T(8,128)(2,1)S(1)}, u32[]{:S(2)}, u32[]{:S(2)}) collective-permute-start(bf16[128,1024]{1,0:T(8,128)(2,1)} %refs_0_.1), channel_id=1, source_target_pairs={{0,16},{16,32},{32,48},{48,64},{64,80},{80,96},{96,112},{112,0},{1... | collective-permute-start | bytes 786440 | tf_op jit(solution)/shard_map/ppermute | solution.py:123
  15.1 42.0 %collective-permute-start.8 = (bf16[1024,512]{1,0:T(8,128)(2,1)}, bf16[1024,512]{1,0:T(8,128)(2,1)S(1)}, u32[]{:S(2)}, u32[]{:S(2)}) collective-permute-start(bf16[1024,512]{1,0:T(8,128)(2,1)} %param.9), channel_id=1, source_target_pairs={{0,8},{8,0},{1,9},{9,1},{2,10},{10,2},{3,11},{11,3},{4,12},{12,4},... | collective-permute-start | bytes 3145736 | tf_op jit(solution)/shard_map/ppermute | solution.py:127
  21.9 13.2 %copy-start.5 = (bf16[128,1024]{1,0:T(8,128)(2,1)}, bf16[128,1024]{1,0:T(8,128)(2,1)S(1)}, u32[]{:S(2)}) copy-start(bf16[128,1024]{1,0:T(8,128)(2,1)S(1)} %collective-permute-done.refs_1_) | copy-start | bytes 786436
  21.9 9.1 %collective-permute-start.1 = (bf16[128,1024]{1,0:T(8,128)(2,1)S(1)}, bf16[128,1024]{1,0:T(8,128)(2,1)S(1)}, u32[]{:S(2)}, u32[]{:S(2)}) collective-permute-start(bf16[128,1024]{1,0:T(8,128)(2,1)S(1)} %collective-permute-done.refs_1_), channel_id=1, source_target_pairs={{0,112},{16,0},{32,16},{48,32},{64,48},{80,64},{96,80},{112,96},{1... | collective-permute-start | bytes 786440 | tf_op jit(solution)/shard_map/ppermute | solution.py:123
  24.8 10.3 %copy-start.6 = (bf16[128,1024]{1,0:T(8,128)(2,1)}, bf16[128,1024]{1,0:T(8,128)(2,1)S(1)}, u32[]{:S(2)}) copy-start(bf16[128,1024]{1,0:T(8,128)(2,1)S(1)} %collective-permute-done.3.refs_8_) | copy-start | bytes 786436
  24.8 10.3 %collective-permute-start.4 = (bf16[128,1024]{1,0:T(8,128)(2,1)S(1)}, bf16[128,1024]{1,0:T(8,128)(2,1)S(1)}, u32[]{:S(2)}, u32[]{:S(2)}) collective-permute-start(bf16[128,1024]{1,0:T(8,128)(2,1)S(1)} %collective-permute-done.3.refs_8_), channel_id=1, source_target_pairs={{0,16},{16,32},{32,48},{48,64},{64,80},{80,96},{96,112},{112,0},{1... | collective-permute-start | bytes 786440 | tf_op jit(solution)/shard_map/ppermute | solution.py:123
  31.0 16.3 %copy-start.7 = (bf16[128,1024]{1,0:T(8,128)(2,1)}, bf16[128,1024]{1,0:T(8,128)(2,1)S(1)}, u32[]{:S(2)}) copy-start(bf16[128,1024]{1,0:T(8,128)(2,1)S(1)} %collective-permute-done.1.refs_2_) | copy-start | bytes 786436
  31.0 8.3 %collective-permute-start.2 = (bf16[128,1024]{1,0:T(8,128)(2,1)S(1)}, bf16[128,1024]{1,0:T(8,128)(2,1)S(1)}, u32[]{:S(2)}, u32[]{:S(2)}) collective-permute-start(bf16[128,1024]{1,0:T(8,128)(2,1)S(1)} %collective-permute-done.1.refs_2_), channel_id=1, source_target_pairs={{0,112},{16,0},{32,16},{48,32},{64,48},{80,64},{96,80},{112,96},{1... | collective-permute-start | bytes 786440 | tf_op jit(solution)/shard_map/ppermute | solution.py:123
  35.1 12.2 %copy-start.8 = (bf16[128,1024]{1,0:T(8,128)(2,1)}, bf16[128,1024]{1,0:T(8,128)(2,1)S(1)}, u32[]{:S(2)}) copy-start(bf16[128,1024]{1,0:T(8,128)(2,1)S(1)} %collective-permute-done.4.refs_7_) | copy-start | bytes 786436
  35.1 9.5 %collective-permute-start.5 = (bf16[128,1024]{1,0:T(8,128)(2,1)S(1)}, bf16[128,1024]{1,0:T(8,128)(2,1)S(1)}, u32[]{:S(2)}, u32[]{:S(2)}) collective-permute-start(bf16[128,1024]{1,0:T(8,128)(2,1)S(1)} %collective-permute-done.4.refs_7_), channel_id=1, source_target_pairs={{0,16},{16,32},{32,48},{48,64},{64,80},{80,96},{96,112},{112,0},{1... | collective-permute-start | bytes 786440 | tf_op jit(solution)/shard_map/ppermute | solution.py:123
  39.3 8.0 %copy-start.3 = (bf16[128,1024]{1,0:T(8,128)(2,1)}, bf16[128,1024]{1,0:T(8,128)(2,1)S(1)}, u32[]{:S(2)}) copy-start(bf16[128,1024]{1,0:T(8,128)(2,1)S(1)} %collective-permute-done.2.refs_3_) | copy-start | bytes 786436
  39.3 77.7 %collective-permute-start.7 = (bf16[64,1024]{1,0:T(8,128)(2,1)S(1)}, bf16[64,1024]{1,0:T(8,128)(2,1)}, u32[]{:S(2)}, u32[]{:S(2)}) collective-permute-start(bf16[64,1024]{1,0:T(8,128)(2,1)S(1)} %slice.78), channel_id=1, source_target_pairs={{0,112},{16,0},{32,16},{48,32},{64,48},{80,64},{96,80},{112,96},{1... | collective-permute-start | bytes 393224 | tf_op jit(solution)/shard_map/ppermute | solution.py:123
  44.6 2.7 %copy-start.4 = (bf16[128,1024]{1,0:T(8,128)(2,1)}, bf16[128,1024]{1,0:T(8,128)(2,1)S(1)}, u32[]{:S(2)}) copy-start(bf16[128,1024]{1,0:T(8,128)(2,1)S(1)} %collective-permute-done.5.refs_6_) | copy-start | bytes 786436
  45.4 71.6 %collective-permute-start.6 = (bf16[64,1024]{1,0:T(8,128)(2,1)}, bf16[64,1024]{1,0:T(8,128)(2,1)}, u32[]{:S(2)}, u32[]{:S(2)}) collective-permute-start(bf16[64,1024]{1,0:T(8,128)(2,1)} %slice.77), channel_id=1, source_target_pairs={{0,16},{16,32},{32,48},{48,64},{64,80},{80,96},{96,112},{112,0},{1... | collective-permute-start | bytes 393224 | tf_op jit(solution)/shard_map/ppermute | solution.py:123
  138.9 3.1 %copy-start.1 = (bf16[1024,512]{1,0:T(8,128)(2,1)S(1)}, bf16[1024,512]{1,0:T(8,128)(2,1)}, u32[]{:S(2)}) copy-start(bf16[1024,512]{1,0:T(8,128)(2,1)} %param.9) | copy-start | bytes 3145732
  139.0 3.1 %copy-start.2 = (bf16[1024,1024]{1,0:T(8,128)(2,1)S(1)}, bf16[1024,1024]{1,0:T(8,128)(2,1)}, u32[]{:S(2)}) copy-start(bf16[1024,1024]{1,0:T(8,128)(2,1)} %attend.1) | copy-start | bytes 6291460
  143.9 13.5 %collective-permute-start.9 = (bf16[128,512]{0,1:T(8,128)(2,1)S(1)}, bf16[128,512]{0,1:T(8,128)(2,1)S(1)}, u32[]{:S(2)}, u32[]{:S(2)}) collective-permute-start(bf16[128,512]{0,1:T(8,128)(2,1)S(1)} %convolution_convert_fusion.3), channel_id=1, source_target_pairs={{0,1},{1,2},{2,3},{3,4},{4,5},{5,6},{6,7},{7,0},{8,9},{9,10},{10,1... | collective-permute-start | bytes 393224 | tf_op jit(solution)/shard_map/ppermute | solution.py:123
  146.8 5.7 %collective-permute-start.13 = (bf16[128,512]{0,1:T(8,128)(2,1)S(1)}, bf16[128,512]{0,1:T(8,128)(2,1)S(1)}, u32[]{:S(2)}, u32[]{:S(2)}) collective-permute-start(bf16[128,512]{0,1:T(8,128)(2,1)S(1)} %convolution_convert_fusion.2), channel_id=1, source_target_pairs={{0,7},{1,0},{2,1},{3,2},{4,3},{5,4},{6,5},{7,6},{8,15},{9,8},{10,9... | collective-permute-start | bytes 393224 | tf_op jit(solution)/shard_map/ppermute | solution.py:123
  152.6 8.7 %collective-permute-start.14 = (bf16[128,1024]{0,1:T(8,128)(2,1)S(1)}, bf16[128,1024]{0,1:T(8,128)(2,1)S(1)}, u32[]{:S(2)}, u32[]{:S(2)}) collective-permute-start(bf16[128,1024]{0,1:T(8,128)(2,1)S(1)} %add_convert_fusion.3), channel_id=1, source_target_pairs={{0,7},{1,0},{2,1},{3,2},{4,3},{5,4},{6,5},{7,6},{8,15},{9,8},{10,9... | collective-permute-start | bytes 786440 | tf_op jit(solution)/shard_map/ppermute | solution.py:123
  157.4 8.9 %collective-permute-start.10 = (bf16[128,1024]{0,1:T(8,128)(2,1)S(1)}, bf16[128,1024]{0,1:T(8,128)(2,1)S(1)}, u32[]{:S(2)}, u32[]{:S(2)}) collective-permute-start(bf16[128,1024]{0,1:T(8,128)(2,1)S(1)} %add_convert_fusion.6), channel_id=1, source_target_pairs={{0,1},{1,2},{2,3},{3,4},{4,5},{5,6},{6,7},{7,0},{8,9},{9,10},{10,1... | collective-permute-start | bytes 786440 | tf_op jit(solution)/shard_map/ppermute | solution.py:123
  161.3 10.2 %collective-permute-start.15 = (bf16[128,1024]{0,1:T(8,128)(2,1)S(1)}, bf16[128,1024]{0,1:T(8,128)(2,1)S(1)}, u32[]{:S(2)}, u32[]{:S(2)}) collective-permute-start(bf16[128,1024]{0,1:T(8,128)(2,1)S(1)} %add_convert_fusion.2), channel_id=1, source_target_pairs={{0,7},{1,0},{2,1},{3,2},{4,3},{5,4},{6,5},{7,6},{8,15},{9,8},{10,9... | collective-permute-start | bytes 786440 | tf_op jit(solution)/shard_map/ppermute | solution.py:123
  166.4 10.3 %collective-permute-start.11 = (bf16[128,1024]{0,1:T(8,128)(2,1)S(1)}, bf16[128,1024]{0,1:T(8,128)(2,1)S(1)}, u32[]{:S(2)}, u32[]{:S(2)}) collective-permute-start(bf16[128,1024]{0,1:T(8,128)(2,1)S(1)} %add_convert_fusion.5), channel_id=1, source_target_pairs={{0,1},{1,2},{2,3},{3,4},{4,5},{5,6},{6,7},{7,0},{8,9},{9,10},{10,1... | collective-permute-start | bytes 786440 | tf_op jit(solution)/shard_map/ppermute | solution.py:123
  171.5 11.0 %collective-permute-start.16 = (bf16[128,1024]{0,1:T(8,128)(2,1)S(1)}, bf16[128,1024]{0,1:T(8,128)(2,1)S(1)}, u32[]{:S(2)}, u32[]{:S(2)}) collective-permute-start(bf16[128,1024]{0,1:T(8,128)(2,1)S(1)} %add_convert_fusion.1), channel_id=1, source_target_pairs={{0,7},{1,0},{2,1},{3,2},{4,3},{5,4},{6,5},{7,6},{8,15},{9,8},{10,9... | collective-permute-start | bytes 786440 | tf_op jit(solution)/shard_map/ppermute | solution.py:123
  176.7 11.2 %collective-permute-start.12 = (bf16[128,1024]{0,1:T(8,128)(2,1)S(1)}, bf16[128,1024]{0,1:T(8,128)(2,1)S(1)}, u32[]{:S(2)}, u32[]{:S(2)}) collective-permute-start(bf16[128,1024]{0,1:T(8,128)(2,1)S(1)} %add_convert_fusion.4), channel_id=1, source_target_pairs={{0,1},{1,2},{2,3},{3,4},{4,5},{5,6},{6,7},{7,0},{8,9},{9,10},{10,1... | collective-permute-start | bytes 786440 | tf_op jit(solution)/shard_map/ppermute | solution.py:123
  188.0 13.1 %collective-permute-start.17 = (bf16[128,512]{0,1:T(8,128)(2,1)S(1)}, bf16[128,512]{0,1:T(8,128)(2,1)S(1)}, u32[]{:S(2)}, u32[]{:S(2)}) collective-permute-start(bf16[128,512]{0,1:T(8,128)(2,1)S(1)} %get-tuple-element.23), channel_id=1, source_target_pairs={{0,8},{8,0},{1,9},{9,1},{2,10},{10,2},{3,11},{11,3},{4,12},{12,4},... | collective-permute-start | bytes 393224 | tf_op jit(solution)/shard_map/ppermute | solution.py:127
Sparse Core Ops, SparseCore 0:
  9.4 45.3 all-gather.1
